TPU v7x, 32 devices: a whole 2x2x4 slice. The times are simulated.
32 devices in a mesh: replica: 4 (over y, x), fsdp: 8 (over z, core).
Axes of the slice: x: 2, y: 2, z: 4, core: 2. Of those that a mesh axis runs over, the one named last changes fastest.
Arguments:
- latents: bfloat16 [32, 256, 1152], P(('replica', 'fsdp')), may hold values from -6 to 6
- condition: bfloat16 [32, 1152], P(('replica', 'fsdp')), may hold values from -6 to 6
- bucket: int32 [32], P(('replica', 'fsdp')), may hold values from 0 to 2, as said below
- keep_slots: int32 [32, 128], P(('replica', 'fsdp')), may hold values from 0 to 255, as said below
- modulation_weight: bfloat16 [1152, 6912], P('fsdp'), may hold values from -0.1875 to 0.1875
- modulation_bias: bfloat16 [6912], P('fsdp'), may hold values from -1.5 to 1.5
- projection_weight: bfloat16 [1152, 3456], P('fsdp'), may hold values from -0.1875 to 0.1875
- query_value_bias: bfloat16 [2304], P('fsdp'), may hold values from -1.5 to 1.5
- output_weight: bfloat16 [1152, 1152], P('fsdp'), may hold values from -0.75 to 0.75
- output_bias: bfloat16 [1152], P('fsdp'), may hold values from -1.5 to 1.5
- expand_weight: bfloat16 [1152, 4608], P('fsdp'), may hold values from -0.1875 to 0.1875
- expand_bias: bfloat16 [4608], P('fsdp'), may hold values from -2.5 to 2.5
- reduce_weight: bfloat16 [4608, 1152], P('fsdp'), may hold values from -0.125 to 0.125
- reduce_bias: bfloat16 [1152], P('fsdp'), may hold values from -1.5 to 1.5
- cotangent: bfloat16 [32, 256, 1152], P(('replica', 'fsdp')), may hold values from -6 to 6
Outputs:
- block_out: bfloat16 [32, 256, 1152], P(('replica', 'fsdp'))
- grad_latents: bfloat16 [32, 256, 1152], P(('replica', 'fsdp'))
- grad_condition: float32 [32, 1152], P(('replica', 'fsdp'))
- grad_modulation_weight: float32 [1152, 6912], P('fsdp')
- grad_modulation_bias: float32 [6912], P('fsdp')
- grad_projection_weight: float32 [1152, 3456], P('fsdp')
- grad_query_value_bias: float32 [2304], P('fsdp')
- grad_output_weight: float32 [1152, 1152], P('fsdp')
- grad_output_bias: float32 [1152], P('fsdp')
- grad_expand_weight: float32 [1152, 4608], P('fsdp')
- grad_expand_bias: float32 [4608], P('fsdp')
- grad_reduce_weight: float32 [4608, 1152], P('fsdp')
- grad_reduce_bias: float32 [1152], P('fsdp')
Inputs may be any that keep to these rules, and one draw needn't show every extreme that they name: `bucket`: 0 marks a 16 x 16 grid of tokens, 1 and 2 grids of (12) x (20) and (20) x (12); an image's real tokens fill its first slots, the rest are padding. `keep_slots`: each row holds distinct slots of that image's real tokens in random order; the first live_count entries are the kept tokens, the others of the image are routed past the block.
All inputs are finite; a program needn't handle non-finite values.
Results may differ from a plain program's by a relative error of at most 0.02.
Values may be sent and summed in bfloat16 or wider, within the bound.
A program may use at most 256 MiB of HBM per device.

v0:
```python
import jax
import jax.numpy as jnp
from jax import lax
from jax.sharding import PartitionSpec as P

HEADS = 16
HEAD_DIM = 72


def layer_norm(rows_in):
    row_mean = jnp.mean(rows_in, axis=-1, keepdims=True)
    centred = rows_in - row_mean
    row_var = jnp.mean(centred * centred, axis=-1, keepdims=True)
    return centred * lax.rsqrt(row_var + 1e-06)


def modulate(rows_in, shift_part, scale_part):
    return layer_norm(rows_in) * (1.0 + scale_part) + shift_part


def gelu_tanh(values_in):
    return jax.nn.gelu(values_in, approximate=True)


def place_rows(target_rows, target_index, new_rows):
    return target_rows.at[target_index].set(new_rows, mode="drop")


def column_sums(rows_in):
    return jnp.sum(rows_in.astype(jnp.float32), axis=0)


def local(
    latents,
    condition,
    bucket,
    keep_slots,
    modulation_weight,
    modulation_bias,
    projection_weight,
    query_value_bias,
    output_weight,
    output_bias,
    expand_weight,
    expand_bias,
    reduce_weight,
    reduce_bias,
    cotangent,
):
    f32 = jnp.float32
    bf16 = jnp.bfloat16
    images, slot_count, model_width = latents.shape
    kept_rows = keep_slots.shape[1]
    row_count = images * kept_rows
    score_scale = HEAD_DIM ** (-0.5)
    shape_heads = (images, kept_rows, HEADS, HEAD_DIM)
    (
        full_mod_w,
        full_mod_b,
        full_proj_w,
        full_qv_b,
        full_out_w,
        full_out_b,
        full_exp_w,
        full_exp_b,
        full_red_w,
        full_red_b,
    ) = (
        lax.all_gather(modulation_weight, "fsdp", axis=0, tiled=True),
        lax.all_gather(modulation_bias, "fsdp", axis=0, tiled=True),
        lax.all_gather(projection_weight, "fsdp", axis=0, tiled=True),
        lax.all_gather(query_value_bias, "fsdp", axis=0, tiled=True),
        lax.all_gather(output_weight, "fsdp", axis=0, tiled=True),
        lax.all_gather(output_bias, "fsdp", axis=0, tiled=True),
        lax.all_gather(expand_weight, "fsdp", axis=0, tiled=True),
        lax.all_gather(expand_bias, "fsdp", axis=0, tiled=True),
        lax.all_gather(reduce_weight, "fsdp", axis=0, tiled=True),
        lax.all_gather(reduce_bias, "fsdp", axis=0, tiled=True),
    )
    live_count = jnp.where(bucket == 0, slot_count, slot_count - 16) // 2
    live_rows = jnp.arange(kept_rows, dtype=jnp.int32)[None, :] < live_count[:, None]
    live_float = live_rows.astype(f32)[:, :, None]
    gather_index = keep_slots[:, :, None]
    kept = jnp.take_along_axis(latents, gather_index, axis=1).astype(f32)
    cond_float = condition.astype(f32)
    cond_act = jax.nn.silu(cond_float).astype(bf16)
    modulation = jnp.dot(cond_act, full_mod_w, preferred_element_type=f32) + full_mod_b.astype(f32)
    pieces = [modulation[:, None, i * model_width : (i + 1) * model_width] for i in range(6)]
    shift_attn, scale_attn, gate_attn, shift_mlp, scale_mlp, gate_mlp = pieces
    normed_one = modulate(kept, shift_attn, scale_attn).astype(bf16).reshape(row_count, model_width)
    projected = jnp.dot(normed_one, full_proj_w, preferred_element_type=f32)
    bias_qv = full_qv_b.astype(f32)
    query_rows = (
        (projected[:, :model_width] + bias_qv[:model_width]).astype(bf16).reshape(shape_heads)
    )
    key_rows = projected[:, model_width : 2 * model_width].astype(bf16).reshape(shape_heads)
    value_rows = (
        (projected[:, 2 * model_width :] + bias_qv[model_width:]).astype(bf16).reshape(shape_heads)
    )

    def masked_scores(queries, keys_in):
        raw = (
            jnp.einsum("bqhd,bkhd->bhqk", queries, keys_in, preferred_element_type=f32)
            * score_scale
        )
        return jnp.where(live_rows[:, None, None, :], raw, -1e30)

    scores = masked_scores(query_rows, key_rows)
    row_max = jnp.max(scores, axis=-1, keepdims=True)
    row_total = jnp.sum(jnp.exp(scores - row_max), axis=-1, keepdims=True)
    log_total = row_max + jnp.log(row_total)
    probs = jnp.exp(scores - log_total)
    attended = (
        jnp.einsum("bhqk,bkhd->bqhd", probs.astype(bf16), value_rows, preferred_element_type=f32)
        .astype(bf16)
        .reshape(row_count, model_width)
    )
    branch_attn = (
        jnp.dot(attended, full_out_w, preferred_element_type=f32) + full_out_b.astype(f32)
    ).reshape(images, kept_rows, model_width)
    mixed = kept + gate_attn * branch_attn
    normed_two = modulate(mixed, shift_mlp, scale_mlp).astype(bf16).reshape(row_count, model_width)
    hidden = jnp.dot(normed_two, full_exp_w, preferred_element_type=f32) + full_exp_b.astype(f32)
    activation = gelu_tanh(hidden).astype(bf16)
    branch_mlp = (
        jnp.dot(activation, full_red_w, preferred_element_type=f32) + full_red_b.astype(f32)
    ).reshape(images, kept_rows, model_width)
    result = mixed + gate_mlp * branch_mlp
    target = jnp.where(live_rows, keep_slots, slot_count)
    block_out = jax.vmap(place_rows)(latents, target, result.astype(bf16))
    back_mod_w, back_proj_w, back_out_w, back_exp_w, back_red_w = (
        lax.all_gather(modulation_weight, "fsdp", axis=0, tiled=True),
        lax.all_gather(projection_weight, "fsdp", axis=0, tiled=True),
        lax.all_gather(output_weight, "fsdp", axis=0, tiled=True),
        lax.all_gather(expand_weight, "fsdp", axis=0, tiled=True),
        lax.all_gather(reduce_weight, "fsdp", axis=0, tiled=True),
    )
    grad_rows = jnp.take_along_axis(cotangent, gather_index, axis=1).astype(f32) * live_float
    grad_gate_mlp = jnp.sum(grad_rows * branch_mlp, axis=1)
    grad_mlp = (gate_mlp * grad_rows).astype(bf16).reshape(row_count, model_width)
    local_red_w = jnp.einsum("rm,rd->md", activation, grad_mlp, preferred_element_type=f32)
    local_red_b = column_sums(grad_mlp)
    grad_act = jnp.einsum("rd,md->rm", grad_mlp, back_red_w, preferred_element_type=f32)
    gelu_pull = jax.vjp(gelu_tanh, hidden)[1]
    grad_hidden = gelu_pull(grad_act)[0].astype(bf16)
    local_exp_w = jnp.einsum("rd,rm->dm", normed_two, grad_hidden, preferred_element_type=f32)
    local_exp_b = column_sums(grad_hidden)
    mlp_red_w, mlp_red_b, mlp_exp_w, mlp_exp_b = (
        lax.psum_scatter(
            local_red_w.astype(jnp.bfloat16), "fsdp", scatter_dimension=0, tiled=True
        ).astype(jnp.float32),
        lax.psum_scatter(
            local_red_b.astype(jnp.bfloat16), "fsdp", scatter_dimension=0, tiled=True
        ).astype(jnp.float32),
        lax.psum_scatter(
            local_exp_w.astype(jnp.bfloat16), "fsdp", scatter_dimension=0, tiled=True
        ).astype(jnp.float32),
        lax.psum_scatter(
            local_exp_b.astype(jnp.bfloat16), "fsdp", scatter_dimension=0, tiled=True
        ).astype(jnp.float32),
    )
    grad_normed_two = jnp.einsum(
        "rm,dm->rd", grad_hidden, back_exp_w, preferred_element_type=f32
    ).reshape(images, kept_rows, model_width)
    pull_two = jax.vjp(modulate, mixed, shift_mlp, scale_mlp)[1]
    grad_mixed_ln, grad_shift_mlp, grad_scale_mlp = pull_two(grad_normed_two)
    grad_mixed = grad_rows + grad_mixed_ln
    grad_gate_attn = jnp.sum(grad_mixed * branch_attn, axis=1)
    grad_attn = (gate_attn * grad_mixed).astype(bf16).reshape(row_count, model_width)
    local_out_w = jnp.einsum("rd,re->de", attended, grad_attn, preferred_element_type=f32)
    local_out_b = column_sums(grad_attn)
    grad_attended = (
        jnp.einsum("re,de->rd", grad_attn, back_out_w, preferred_element_type=f32)
        .astype(bf16)
        .reshape(shape_heads)
    )
    scores_again = masked_scores(query_rows, key_rows)
    probs_again = jnp.exp(scores_again - log_total)
    grad_values = jnp.einsum(
        "bhqk,bqhd->bkhd", probs_again.astype(bf16), grad_attended, preferred_element_type=f32
    ).astype(bf16)
    grad_probs = jnp.einsum(
        "bqhd,bkhd->bhqk", grad_attended, value_rows, preferred_element_type=f32
    )
    row_inner = jnp.sum(grad_probs * probs_again, axis=-1, keepdims=True)
    grad_scores = (probs_again * (grad_probs - row_inner)).astype(bf16)
    grad_query = (
        jnp.einsum("bhqk,bkhd->bqhd", grad_scores, key_rows, preferred_element_type=f32)
        * score_scale
    ).astype(bf16)
    grad_keys = (
        jnp.einsum("bhqk,bqhd->bkhd", grad_scores, query_rows, preferred_element_type=f32)
        * score_scale
    ).astype(bf16)
    grad_projected = jnp.concatenate(
        [
            grad_query.reshape(row_count, model_width),
            grad_keys.reshape(row_count, model_width),
            grad_values.reshape(row_count, model_width),
        ],
        axis=1,
    )
    local_proj_w = jnp.einsum("rd,re->de", normed_one, grad_projected, preferred_element_type=f32)
    local_qv_b = jnp.concatenate(
        [
            column_sums(grad_projected[:, :model_width]),
            column_sums(grad_projected[:, 2 * model_width :]),
        ]
    )
    grad_normed_one = jnp.einsum(
        "re,de->rd", grad_projected, back_proj_w, preferred_element_type=f32
    ).reshape(images, kept_rows, model_width)
    pull_one = jax.vjp(modulate, kept, shift_attn, scale_attn)[1]
    grad_kept_ln, grad_shift_attn, grad_scale_attn = pull_one(grad_normed_one)
    grad_kept = grad_mixed + grad_kept_ln
    grad_latents = jax.vmap(place_rows)(cotangent, target, grad_kept.astype(bf16))
    grad_modulation = jnp.concatenate(
        [
            grad_shift_attn[:, 0],
            grad_scale_attn[:, 0],
            grad_gate_attn,
            grad_shift_mlp[:, 0],
            grad_scale_mlp[:, 0],
            grad_gate_mlp,
        ],
        axis=1,
    ).astype(bf16)
    grad_cond_act = jnp.einsum("be,de->bd", grad_modulation, back_mod_w, preferred_element_type=f32)
    silu_pull = jax.vjp(jax.nn.silu, cond_float)[1]
    grad_condition = silu_pull(grad_cond_act)[0]
    local_mod_w = jnp.einsum("bd,be->de", cond_act, grad_modulation, preferred_element_type=f32)
    local_mod_b = column_sums(grad_modulation)
    rest_mod_w, rest_mod_b, rest_proj_w, rest_qv_b, rest_out_w, rest_out_b = (
        lax.psum_scatter(
            local_mod_w.astype(jnp.bfloat16), "fsdp", scatter_dimension=0, tiled=True
        ).astype(jnp.float32),
        lax.psum_scatter(
            local_mod_b.astype(jnp.bfloat16), "fsdp", scatter_dimension=0, tiled=True
        ).astype(jnp.float32),
        lax.psum_scatter(
            local_proj_w.astype(jnp.bfloat16), "fsdp", scatter_dimension=0, tiled=True
        ).astype(jnp.float32),
        lax.psum_scatter(
            local_qv_b.astype(jnp.bfloat16), "fsdp", scatter_dimension=0, tiled=True
        ).astype(jnp.float32),
        lax.psum_scatter(
            local_out_w.astype(jnp.bfloat16), "fsdp", scatter_dimension=0, tiled=True
        ).astype(jnp.float32),
        lax.psum_scatter(
            local_out_b.astype(jnp.bfloat16), "fsdp", scatter_dimension=0, tiled=True
        ).astype(jnp.float32),
    )
    shares = (
        lax.psum_scatter(
            rest_mod_w.astype(jnp.bfloat16), "replica", scatter_dimension=1, tiled=True
        ).astype(jnp.float32),
        lax.psum_scatter(
            rest_proj_w.astype(jnp.bfloat16), "replica", scatter_dimension=1, tiled=True
        ).astype(jnp.float32),
        lax.psum_scatter(
            rest_out_w.astype(jnp.bfloat16), "replica", scatter_dimension=1, tiled=True
        ).astype(jnp.float32),
        lax.psum_scatter(
            mlp_exp_w.astype(jnp.bfloat16), "replica", scatter_dimension=1, tiled=True
        ).astype(jnp.float32),
        lax.psum_scatter(
            mlp_red_w.astype(jnp.bfloat16), "replica", scatter_dimension=1, tiled=True
        ).astype(jnp.float32),
    )
    sum_mod_w, sum_proj_w, sum_out_w, sum_exp_w, sum_red_w = (
        lax.all_gather(shares[0].astype(jnp.bfloat16), "replica", axis=1, tiled=True).astype(
            jnp.float32
        ),
        lax.all_gather(shares[1].astype(jnp.bfloat16), "replica", axis=1, tiled=True).astype(
            jnp.float32
        ),
        lax.all_gather(shares[2].astype(jnp.bfloat16), "replica", axis=1, tiled=True).astype(
            jnp.float32
        ),
        lax.all_gather(shares[3].astype(jnp.bfloat16), "replica", axis=1, tiled=True).astype(
            jnp.float32
        ),
        lax.all_gather(shares[4].astype(jnp.bfloat16), "replica", axis=1, tiled=True).astype(
            jnp.float32
        ),
    )
    sum_mod_b, sum_qv_b, sum_out_b, sum_exp_b, sum_red_b = lax.psum(
        (rest_mod_b, rest_qv_b, rest_out_b, mlp_exp_b, mlp_red_b), "replica"
    )
    return (
        block_out,
        grad_latents,
        grad_condition,
        sum_mod_w,
        sum_mod_b,
        sum_proj_w,
        sum_qv_b,
        sum_out_w,
        sum_out_b,
        sum_exp_w,
        sum_exp_b,
        sum_red_w,
        sum_red_b,
    )


def solution(mesh):
    placed = (
        P(("replica", "fsdp"), None, None),
        P(("replica", "fsdp"), None),
        P(("replica", "fsdp")),
        P(("replica", "fsdp"), None),
        P("fsdp", None),
        P("fsdp"),
        P("fsdp", None),
        P("fsdp"),
        P("fsdp", None),
        P("fsdp"),
        P("fsdp", None),
        P("fsdp"),
        P("fsdp", None),
        P("fsdp"),
        P(("replica", "fsdp"), None, None),
    )
    return jax.shard_map(
        local,
        mesh=mesh,
        in_specs=placed,
        out_specs=(
            P(("replica", "fsdp"), None, None),
            P(("replica", "fsdp"), None, None),
            P(("replica", "fsdp"), None),
            P("fsdp", None),
            P("fsdp"),
            P("fsdp", None),
            P("fsdp"),
            P("fsdp", None),
            P("fsdp"),
            P("fsdp", None),
            P("fsdp"),
            P("fsdp", None),
            P("fsdp"),
        ),
        check_vma=False,
    )
```

profile of v0, /device:TPU:25, one launch (start us, length us, event | category | flops | bytes accessed | tf_op | source)
XLA Modules:
  0.0 1304.1 jit_solution(7844802750100305167)
XLA Ops:
  7.2 1.1 copy.104
  8.3 1.1 copy.105
  17.3 28.3 %all-reduce.12 = (bf16[2304]{0:T(1024)(128)(2,1)S(1)}, bf16[6912]{0:T(1024)(128)(2,1)S(1)}, bf16[4608]{0:T(1024)(128)(2,1)S(1)}, bf16[1152]{0:T(1024)(128)(2,1)S(1)}, bf16[1152]{0:T(1024)(128)(2,1)S(1)}) all-reduce(bf16[2304]{0:T(1024)(128)(2,1)S(1)} %dynamic-update-slice.1, ...), channel_id=1, replica_groups=mesh['replica'=4,'fsdp'=8] {'fsdp'}, use_global_device_ids=true, to_apply=%add.1 | all-reduce | flops 16128 | bytes 64512
  45.6 0.9 gather_fusion
  46.5 0.9 gather_fusion.1
  48.5 104.8 %all-gather.12.cloned.1.call-done = bf16[1152,6912]{1,0:T(8,128)(2,1)} async-done(((bf16[144,6912]{1,0:T(8,128)(2,1)}), bf16[1152,6912]{1,0:T(8,128)(2,1)}) %all-gather.12.cloned.1.call-update) | async-done | bytes 15925264 | tf_op jit(solution)/shard_map/all_gather | solution.py:69
  153.3 7.7 convolution_reduce_fusion
  161.2 70.8 %all-gather.14.cloned.1.call-done = bf16[1152,3456]{1,0:T(8,128)(2,1)} async-done(((bf16[144,3456]{1,0:T(8,128)(2,1)}), bf16[1152,3456]{1,0:T(8,128)(2,1)}) %all-gather.14.cloned.1.call-update) | async-done | bytes 7962640 | tf_op jit(solution)/shard_map/all_gather | solution.py:71
  232.0 4.7 fusion.65
  237.1 0.9 copy.62
  238.2 1.4 fusion.75
  239.8 1.0 convolution_convert_fusion.6
  240.9 26.3 %all-gather.16.cloned.1.call-done = bf16[1152,1152]{1,0:T(8,128)(2,1)} async-done(((bf16[144,1152]{1,0:T(8,128)(2,1)}), bf16[1152,1152]{1,0:T(8,128)(2,1)}) %all-gather.16.cloned.1.call-update) | async-done | bytes 2654224 | tf_op jit(solution)/shard_map/all_gather | solution.py:73
  267.2 3.3 fusion.72
  270.7 96.5 %all-gather.18.cloned.1.call-done = bf16[1152,4608]{1,0:T(8,128)(2,1)} async-done(((bf16[144,4608]{1,0:T(8,128)(2,1)}), bf16[1152,4608]{1,0:T(8,128)(2,1)}) %all-gather.18.cloned.1.call-update) | async-done | bytes 10616848 | tf_op jit(solution)/shard_map/all_gather | solution.py:75
  367.2 7.2 convolution_add_fusion
  374.4 93.2 %all-gather.20.cloned.1.call-done = bf16[4608,1152]{1,0:T(8,128)(2,1)} async-done(((bf16[576,1152]{1,0:T(8,128)(2,1)}), bf16[4608,1152]{1,0:T(8,128)(2,1)}) %all-gather.20.cloned.1.call-update) | async-done | bytes 10616848 | tf_op jit(solution)/shard_map/all_gather | solution.py:77
  467.6 8.6 fusion.77
  476.2 1.0 copy-done.6
  477.2 6.0 convolution_convert_fusion.1
  483.3 9.4 convolution_convert_fusion
  492.8 8.0 fusion.25
  503.7 1.6 convolution_convert_fusion.4
  505.4 1.8 copy.65
  507.2 1.1 reduce_sum.251
  508.3 1.5 multiply_reduce_fusion
  512.0 6.9 fusion.76
  519.6 8.0 fusion.24
  529.3 5.9 multiply_convert_fusion
  536.1 3.3 convolution_convert_fusion.3
  539.5 6.8 convolution_convert_fusion.2
  546.4 45.7 %reduce-scatter.27.cloned.1.call-done = bf16[144,4608]{1,0:T(8,128)(2,1)} async-done(((bf16[1152,4608]{1,0:T(8,128)(2,1)}), bf16[144,4608]{1,0:T(8,128)(2,1)}) %reduce-scatter.27.cloned.1.call-update) | async-done | bytes 1327120 | tf_op jit(solution)/shard_map/reduce_scatter | solution.py:155
  592.0 3.8 copy.84
  595.9 107.6 %reduce-scatter.29.cloned.1.call-done = bf16[576,1152]{1,0:T(8,128)(2,1)} async-done(((bf16[4608,1152]{1,0:T(8,128)(2,1)}), bf16[576,1152]{1,0:T(8,128)(2,1)}) %reduce-scatter.29.cloned.1.call-update) | async-done | bytes 1327120 | tf_op jit(solution)/shard_map/reduce_scatter | solution.py:149
  703.5 2.6 copy.86
  706.2 158.8 %reduce-scatter.21.cloned.1.call-done = bf16[144,6912]{1,0:T(8,128)(2,1)} async-done(((bf16[1152,6912]{1,0:T(8,128)(2,1)}), bf16[144,6912]{1,0:T(8,128)(2,1)}) %reduce-scatter.21.cloned.1.call-update) | async-done | bytes 1990672 | tf_op jit(solution)/shard_map/reduce_scatter | solution.py:234
  865.0 4.5 copy.78
  869.6 36.2 %reduce-scatter.25.cloned.1.call-done = bf16[144,1152]{1,0:T(8,128)(2,1)} async-done(((bf16[1152,1152]{1,0:T(8,128)(2,1)}), bf16[144,1152]{1,0:T(8,128)(2,1)}) %reduce-scatter.25.cloned.1.call-update) | async-done | bytes 331792 | tf_op jit(solution)/shard_map/reduce_scatter | solution.py:246
  905.7 2.0 copy.82
  907.8 83.4 %reduce-scatter.23.cloned.1.call-done = bf16[144,3456]{1,0:T(8,128)(2,1)} async-done(((bf16[1152,3456]{1,0:T(8,128)(2,1)}), bf16[144,3456]{1,0:T(8,128)(2,1)}) %reduce-scatter.23.cloned.1.call-update) | async-done | bytes 995344 | tf_op jit(solution)/shard_map/reduce_scatter | solution.py:240
  991.2 2.6 copy.80
  993.9 39.6 %reduce-scatter.37.cloned.1.call-done = bf16[1152,144]{1,0:T(8,128)(2,1)} async-done(((bf16[4608,144]{1,0:T(8,128)(2,1)}), bf16[1152,144]{1,0:T(8,128)(2,1)}) %reduce-scatter.37.cloned.1.call-update) | async-done | bytes 331792
  1033.5 2.0 copy.85
  1035.6 31.1 %reduce-scatter.39.cloned.1.call-done = bf16[288,576]{1,0:T(8,128)(2,1)} async-done(((bf16[1152,576]{1,0:T(8,128)(2,1)}), bf16[288,576]{1,0:T(8,128)(2,1)}) %reduce-scatter.39.cloned.1.call-update) | async-done | bytes 331792
  1066.7 51.2 %reduce-scatter.31.cloned.1.call-done = bf16[1728,144]{1,0:T(8,128)(2,1)} async-done(((bf16[6912,144]{1,0:T(8,128)(2,1)}), bf16[1728,144]{1,0:T(8,128)(2,1)}) %reduce-scatter.31.cloned.1.call-update) | async-done | bytes 497680
  1117.9 2.2 copy.79
  1122.8 2.0 scatter_custom_fusion
  1124.9 2.5 scatter_custom_fusion.1
  1127.6 26.3 %all-reduce.11 = (bf16[6912]{0:T(1024)(128)(2,1)S(1)}, bf16[2304]{0:T(1024)(128)(2,1)S(1)}, bf16[1152]{0:T(1024)(128)(2,1)S(1)}, bf16[4608]{0:T(1024)(128)(2,1)S(1)}, bf16[1152]{0:T(1024)(128)(2,1)S(1)}) all-reduce(bf16[6912]{0:T(1024)(128)(2,1)S(1)} %dynamic-update-slice.10, ...), channel_id=4, replica_groups=mesh['replica'=4,'fsdp'=8] {'fsdp'}, use_global_device_ids=true, to_apply=%region_21.23.clone | all-reduce | flops 16128 | bytes 64512
  1154.2 12.5 all-reduce.10
  1166.7 10.5 fusion.50
  1177.2 1.0 copy.83
  1178.2 8.1 all-gather.2
  1186.5 1.3 reshape.552
  1187.7 1.2 copy.81
  1188.9 14.0 %all-gather.1 = bf16[4,864,144]{1,2,0:T(8,128)(2,1)S(1)} all-gather(bf16[1,864,144]{1,2,0:T(8,128)(2,1)S(1)} %bitcast.260), channel_id=1, replica_groups=mesh['replica'=4,'fsdp'=8] {'replica'}, dimensions={0}, use_global_device_ids=true | all-gather | bytes 1244160 | tf_op jit(solution)/shard_map/all_gather | solution.py:274
  1203.4 2.4 reshape.551
  1205.7 11.6 all-gather.22.cloned.1.call-done
  1217.4 3.1 convert_element_type.254
  1220.5 28.8 %all-gather.24.cloned.1.call-done = bf16[576,1152]{0,1:T(8,128)(2,1)} async-done(((bf16[576,288]{0,1:T(8,128)(2,1)}), bf16[576,1152]{0,1:T(8,128)(2,1)}) %all-gather.24.cloned.1.call-update) | async-done | bytes 1327120 | tf_op jit(solution)/shard_map/all_gather | solution.py:283
  1249.3 2.9 copy.73
  1252.2 34.4 %all-gather.26.cloned.1.call-done = bf16[4,1728,144]{1,2,0:T(8,128)(2,1)} async-done(((bf16[1,1728,144]{1,2,0:T(8,128)(2,1)}), bf16[4,1728,144]{1,2,0:T(8,128)(2,1)}) %all-gather.26.cloned.1.call-update) | async-done | bytes 1990672 | tf_op jit(solution)/shard_map/all_gather | solution.py:271
  1286.6 4.6 copy.69
  1291.2 5.9 reshape.550
  (173 shorter events, 16.8 us)
Async XLA Ops:
  7.2 146.2 %all-gather.12.cloned.1.call-start = ((), (), s32[]{:S(2)}) async-start(), calls=%async_computation.10 | async-start | bytes 17915904 | tf_op jit(solution)/shard_map/all_gather | solution.py:69
  9.4 3.4 copy-start.19
  9.4 6.6 copy-start.29
  9.4 6.9 copy-start.30
  9.4 7.1 copy-start.24
  9.4 7.4 copy-start.20
  9.4 7.6 copy-start.21
  9.5 36.1 %copy-start.31 = (s32[1,128]{1,0:T(1,128)S(1)}, s32[1,128]{1,0:T(1,128)}, u32[]{:S(2)}) copy-start(s32[1,128]{1,0:T(1,128)} %param.20) | copy-start | bytes 1540
  9.5 222.5 %all-gather.14.cloned.1.call-start = ((), (), s32[]{:S(2)}) async-start(), calls=%async_computation.11 | async-start | bytes 8957952 | tf_op jit(solution)/shard_map/all_gather | solution.py:71
  10.2 257.0 %all-gather.16.cloned.1.call-start = ((), (), s32[]{:S(2)}) async-start(), calls=%async_computation.12 | async-start | bytes 2985984 | tf_op jit(solution)/shard_map/all_gather | solution.py:73
  11.0 356.2 %all-gather.18.cloned.1.call-start = ((), (), s32[]{:S(2)}) async-start(), calls=%async_computation.13 | async-start | bytes 11943936 | tf_op jit(solution)/shard_map/all_gather | solution.py:75
  11.5 456.0 %all-gather.20.cloned.1.call-start = ((), (), s32[]{:S(2)}) async-start(), calls=%async_computation.14 | async-start | bytes 11943936 | tf_op jit(solution)/shard_map/all_gather | solution.py:77
  12.1 579.9 %reduce-scatter.27.cloned.1.call-start = ((), (), s32[]{:S(2)}) async-start(), calls=%async_computation.18 | async-start | bytes 11943936 | tf_op jit(solution)/shard_map/reduce_scatter | solution.py:155
  45.6 2.9 copy-start.18
  47.9 0.5 copy-start.25
  237.1 3.8 copy-start.9
  238.2 29.0 %copy-start.11 = (bf16[128,1152]{0,1:T(8,128)(2,1)}, bf16[128,1152]{0,1:T(8,128)(2,1)S(1)}, u32[]{:S(2)}) copy-start(bf16[128,1152]{0,1:T(8,128)(2,1)S(1)} %copy.63) | copy-start | bytes 884740
  270.7 103.7 %copy-start.27 = (f32[128]{0:T(128)}, f32[128]{0:T(128)S(1)}, u32[]{:S(2)}) copy-start(f32[128]{0:T(128)S(1)} %multiply_reduce_fusion.1) | copy-start | bytes 1540
  476.2 1.0 copy-start.6
  483.2 220.2 %reduce-scatter.29.cloned.1.call-start = ((), (), s32[]{:S(2)}) async-start(), calls=%async_computation.20 | async-start | bytes 11943936 | tf_op jit(solution)/shard_map/reduce_scatter | solution.py:149
  492.7 372.3 %reduce-scatter.21.cloned.1.call-start = ((), (), s32[]{:S(2)}) async-start(), calls=%async_computation.15 | async-start | bytes 17915904 | tf_op jit(solution)/shard_map/reduce_scatter | solution.py:234
  492.8 8.0 copy-start.28
  500.8 0.8 copy-start.3
  500.8 2.9 copy-start.2
  501.9 0.8 copy-start.4
  501.9 3.5 copy-start.22
  503.0 0.7 copy-start.8
  508.3 1.8 copy-start.13
  509.8 1.0 copy-start.12
  509.8 1.5 copy-start.10
  510.8 8.0 copy-start.16
  511.3 7.5 copy-start.17
  511.9 6.9 copy-start.15
  511.9 7.6 copy-start.5
  512.0 7.6 copy-start.23
  519.5 8.0 copy-start.26
  519.6 8.0 copy-start.14
  535.2 1.0 copy-start.7
  535.2 370.5 %reduce-scatter.25.cloned.1.call-start = ((), (), s32[]{:S(2)}) async-start(), calls=%async_computation.17 | async-start | bytes 2985984 | tf_op jit(solution)/shard_map/reduce_scatter | solution.py:246
  539.4 451.8 %reduce-scatter.23.cloned.1.call-start = ((), (), s32[]{:S(2)}) async-start(), calls=%async_computation.16 | async-start | bytes 8957952 | tf_op jit(solution)/shard_map/reduce_scatter | solution.py:240
  546.3 487.2 %reduce-scatter.37.cloned.1.call-start = ((), (), s32[]{:S(2)}) async-start(), calls=%async_computation.26 | async-start | bytes 2949120
  595.8 470.8 %reduce-scatter.39.cloned.1.call-start = ((), (), s32[]{:S(2)}) async-start(), calls=%async_computation.27 | async-start | bytes 1843200
  706.1 411.8 %reduce-scatter.31.cloned.1.call-start = ((), (), s32[]{:S(2)}) async-start(), calls=%async_computation.23 | async-start | bytes 4423680
  869.5 307.6 %reduce-scatter.35.cloned.1.call-start = ((), (), s32[]{:S(2)}) async-start(), calls=%async_computation.25 | async-start | bytes 737280
  907.8 280.0 %reduce-scatter.33.cloned.1.call-start = ((), (), s32[]{:S(2)}) async-start(), calls=%async_computation.24 | async-start | bytes 2211840
  993.8 128.9 %copy-start.32 = (s32[1,128]{1,0:T(1,128)S(1)}, s32[1,128]{1,0:T(1,128)}, u32[]{:S(2)}) copy-start(s32[1,128]{1,0:T(1,128)} %param.20) | copy-start | bytes 1540
  993.8 223.6 %all-gather.22.cloned.1.call-start = ((), (), s32[]{:S(2)}) async-start(), calls=%async_computation.19 | async-start | bytes 1658880 | tf_op jit(solution)/shard_map/all_gather | solution.py:280
  1035.5 213.8 %all-gather.24.cloned.1.call-start = ((), (), s32[]{:S(2)}) async-start(), calls=%async_computation.21 | async-start | bytes 1843200 | tf_op jit(solution)/shard_map/all_gather | solution.py:283
  1066.7 219.9 %all-gather.26.cloned.1.call-start = ((), (), s32[]{:S(2)}) async-start(), calls=%async_computation.22 | async-start | bytes 2580480 | tf_op jit(solution)/shard_map/all_gather | solution.py:271
  1124.8 52.3 %copy-start.1 = (bf16[256,1152]{1,0:T(8,128)(2,1)}, bf16[256,1152]{1,0:T(8,128)(2,1)S(1)}, u32[]{:S(2)}) copy-start(bf16[256,1152]{1,0:T(8,128)(2,1)S(1)} %scatter_custom_fusion) | copy-start | bytes 1769476
  1127.4 49.8 %copy-start = (bf16[256,1152]{1,0:T(8,128)(2,1)}, bf16[256,1152]{1,0:T(8,128)(2,1)S(1)}, u32[]{:S(2)}) copy-start(bf16[256,1152]{1,0:T(8,128)(2,1)S(1)} %scatter_custom_fusion.1) | copy-start | bytes 1769476
Sparse Core Ops, SparseCore 0:
  9.7 143.6 all-gather.11
  155.0 76.9 all-gather.13
  233.6 33.5 all-gather.15
  268.7 98.4 all-gather.17
  368.7 98.8 all-gather.19
  483.4 108.6 reduce-scatter.26
  594.4 108.9 reduce-scatter.28
  705.8 159.1 reduce-scatter.20
  868.0 37.7 reduce-scatter.24
  908.0 83.1 reduce-scatter.22
  994.8 38.5 reduce-scatter.36
  1036.3 30.3 reduce-scatter.38
  1070.6 47.2 reduce-scatter.30
  1121.4 24.9 reduce-scatter.34
  1149.9 33.0 reduce-scatter.32
  1185.2 32.0 all-gather.21
  1219.1 30.1 all-gather.23
  1251.5 35.0 all-gather.25
where the time goes:
time: 1310 us; the launch traced here: 1300 us
  waiting for transfers between devices  1020 us (78%)
  matrix products  97.6 us (7%)
  blocking collectives  89.2 us (7%)
  local copies, waits for them, and re-layouts  55.8 us (4%)
  between operations  21 us (2%)
  other arithmetic  17.3 us (1%)
    reduce_scatter x1, waiting for transfers between devices, local(): lax.psum_scatter(local_mod_w.astype(jnp.bfloat16), 'fsdp', scatter_dimens...  159 us
    unnamed x23, waiting for transfers between devices  125 us
    reduce_scatter x1, waiting for transfers between devices, local(): lax.psum_scatter(local_red_w.astype(jnp.bfloat16), 'fsdp', scatter_dimens...  108 us
    all_gather x1, waiting for transfers between devices, local(): lax.all_gather(modulation_weight, 'fsdp', axis=0, tiled=True)  105 us
    all_gather x1, waiting for transfers between devices, local(): lax.all_gather(expand_weight, 'fsdp', axis=0, tiled=True)  96.5 us
    all_gather x1, waiting for transfers between devices, local(): lax.all_gather(reduce_weight, 'fsdp', axis=0, tiled=True)  93.2 us
    reduce_scatter x1, waiting for transfers between devices, local(): lax.psum_scatter(local_proj_w.astype(jnp.bfloat16), 'fsdp', scatter_dimen...  83.4 us
    all_gather x1, waiting for transfers between devices, local(): lax.all_gather(projection_weight, 'fsdp', axis=0, tiled=True)  70.8 us
  transfers between devices with their start and end apart: 18, of which 16 were waited for; matrix products, arithmetic and copies ran while one was open for 11% of the time, Pallas kernels for 0%

commit v1 on v0

--- a/solution.py
+++ b/solution.py
@@ -304,6 +304,238 @@
     )
 
 
+def local_tp(
+    latents,
+    condition,
+    bucket,
+    keep_slots,
+    modulation_weight,
+    modulation_bias,
+    projection_weight,
+    query_value_bias,
+    output_weight,
+    output_bias,
+    expand_weight,
+    expand_bias,
+    reduce_weight,
+    reduce_bias,
+    cotangent,
+):
+    f32 = jnp.float32
+    bf16 = jnp.bfloat16
+    n = lax.axis_size("fsdp")
+    copies = lax.axis_size("replica")
+    me = lax.axis_index("fsdp")
+    images, slot_count, width = latents.shape
+    kept_rows = keep_slots.shape[1]
+    rows = images * kept_rows
+    group_images = images * n
+    group_rows = rows * n
+    heads = HEADS // n
+    part = width // n
+    scale = HEAD_DIM ** (-0.5)
+
+    def gather(value, axis=0):
+        return lax.all_gather(value, "fsdp", axis=axis, tiled=True)
+
+    def scatter(value):
+        return lax.psum_scatter(value, "fsdp", scatter_dimension=0, tiled=True)
+
+    def exchange(value, split, concat):
+        return lax.all_to_all(value, "fsdp", split, concat, tiled=True)
+
+    cond_float = condition.astype(f32)
+    cond_act = jax.nn.silu(cond_float).astype(bf16)
+    cond_cols = exchange(cond_act, 1, 0)
+    modulation = scatter(jnp.dot(cond_cols, modulation_weight, preferred_element_type=f32))
+    cuts = [modulation_bias.shape[0], query_value_bias.shape[0], output_bias.shape[0]]
+    biases = gather(
+        jnp.concatenate([modulation_bias, query_value_bias, output_bias, reduce_bias])[None]
+    )
+    mod_b = biases[:, : cuts[0]].reshape(-1).astype(f32)
+    qv_b = biases[:, cuts[0] : cuts[0] + cuts[1]].reshape(2, n, part).astype(f32)
+    out_b = biases[:, cuts[0] + cuts[1] : cuts[0] + cuts[1] + cuts[2]].reshape(-1).astype(f32)
+    red_b = biases[:, cuts[0] + cuts[1] + cuts[2] :].reshape(-1).astype(f32)
+    my_qv_b = lax.dynamic_index_in_dim(qv_b, me, 1, keepdims=False)
+    modulation = modulation + mod_b
+    pieces = [modulation[:, None, i * width : (i + 1) * width] for i in range(6)]
+    shift_attn, scale_attn, gate_attn, shift_mlp, scale_mlp, gate_mlp = pieces
+
+    proj = exchange(
+        projection_weight.reshape(part, 3, n, part).transpose(2, 0, 1, 3), 0, 1
+    ).reshape(width, 3 * part)
+    exp_w = exchange(expand_weight, 1, 0)
+
+    live_count = jnp.where(bucket == 0, slot_count, slot_count - 16) // 2
+    live_rows = jnp.arange(kept_rows, dtype=jnp.int32)[None, :] < live_count[:, None]
+    live_float = live_rows.astype(f32)[:, :, None]
+    live_all = gather(live_rows.astype(f32)) > 0.5
+    gather_index = keep_slots[:, :, None]
+    kept = jnp.take_along_axis(latents, gather_index, axis=1).astype(f32)
+    grad_rows = jnp.take_along_axis(cotangent, gather_index, axis=1).astype(f32) * live_float
+    grad_mlp = (gate_mlp * grad_rows).astype(bf16).reshape(rows, width)
+    all_grad_mlp = gather(grad_mlp)
+
+    normed_one = gather(modulate(kept, shift_attn, scale_attn).astype(bf16).reshape(rows, width))
+    projected = jnp.dot(normed_one, proj, preferred_element_type=f32)
+    head_shape = (group_images, kept_rows, heads, HEAD_DIM)
+    query = (projected[:, :part] + my_qv_b[0]).astype(bf16).reshape(head_shape)
+    keys = projected[:, part : 2 * part].astype(bf16).reshape(head_shape)
+    values = (projected[:, 2 * part :] + my_qv_b[1]).astype(bf16).reshape(head_shape)
+    scores = jnp.einsum("bqhd,bkhd->bhqk", query, keys, preferred_element_type=f32) * scale
+    scores = jnp.where(live_all[:, None, None, :], scores, -1e30)
+    probs = jax.nn.softmax(scores, axis=-1)
+    probs_low = probs.astype(bf16)
+    attended = (
+        jnp.einsum("bhqk,bkhd->bqhd", probs_low, values, preferred_element_type=f32)
+        .astype(bf16)
+        .reshape(group_rows, part)
+    )
+    branch_attn = scatter(
+        jnp.dot(attended, output_weight, preferred_element_type=f32).astype(bf16)
+    ).astype(f32)
+    branch_attn = (branch_attn + out_b).reshape(images, kept_rows, width)
+    mixed = kept + gate_attn * branch_attn
+    normed_two = gather(modulate(mixed, shift_mlp, scale_mlp).astype(bf16).reshape(rows, width))
+    hidden = jnp.dot(normed_two, exp_w, preferred_element_type=f32) + expand_bias.astype(f32)
+    activation, gelu_pull = jax.vjp(gelu_tanh, hidden)
+    activation = activation.astype(bf16)
+    branch_mlp = scatter(
+        jnp.dot(activation, reduce_weight, preferred_element_type=f32).astype(bf16)
+    ).astype(f32)
+    branch_mlp = (branch_mlp + red_b).reshape(images, kept_rows, width)
+    result = mixed + gate_mlp * branch_mlp
+    target = jnp.where(live_rows, keep_slots, slot_count)
+    block_out = jax.vmap(place_rows)(latents, target, result.astype(bf16))
+    grad_gate_mlp = jnp.sum(grad_rows * branch_mlp, axis=1)
+
+    grad_act = jnp.einsum("rd,md->rm", all_grad_mlp, reduce_weight, preferred_element_type=f32)
+    grad_hidden = gelu_pull(grad_act)[0].astype(bf16)
+    local_red = jnp.einsum("rm,rd->md", activation, all_grad_mlp, preferred_element_type=f32)
+    local_exp = jnp.einsum("rd,rm->dm", normed_two, grad_hidden, preferred_element_type=f32)
+    grad_normed_two = scatter(
+        jnp.einsum("rm,dm->rd", grad_hidden, exp_w, preferred_element_type=f32).astype(bf16)
+    ).astype(f32)
+    pull_two = jax.vjp(modulate, mixed, shift_mlp, scale_mlp)[1]
+    grad_mixed_ln, grad_shift_mlp, grad_scale_mlp = pull_two(
+        grad_normed_two.reshape(images, kept_rows, width)
+    )
+    grad_mixed = grad_rows + grad_mixed_ln
+    grad_gate_attn = jnp.sum(grad_mixed * branch_attn, axis=1)
+    grad_attn = gather((gate_attn * grad_mixed).astype(bf16).reshape(rows, width))
+    local_out = jnp.einsum("rd,re->de", attended, grad_attn, preferred_element_type=f32)
+    grad_attended = (
+        jnp.einsum("re,de->rd", grad_attn, output_weight, preferred_element_type=f32)
+        .astype(bf16)
+        .reshape(head_shape)
+    )
+    grad_values = jnp.einsum(
+        "bhqk,bqhd->bkhd", probs_low, grad_attended, preferred_element_type=f32
+    ).astype(bf16)
+    grad_probs = jnp.einsum("bqhd,bkhd->bhqk", grad_attended, values, preferred_element_type=f32)
+    row_inner = jnp.sum(grad_probs * probs, axis=-1, keepdims=True)
+    grad_scores = (probs * (grad_probs - row_inner)).astype(bf16)
+    grad_query = (
+        jnp.einsum("bhqk,bkhd->bqhd", grad_scores, keys, preferred_element_type=f32) * scale
+    ).astype(bf16)
+    grad_keys = (
+        jnp.einsum("bhqk,bqhd->bkhd", grad_scores, query, preferred_element_type=f32) * scale
+    ).astype(bf16)
+    grad_projected = jnp.concatenate(
+        [g.reshape(group_rows, part) for g in (grad_query, grad_keys, grad_values)], axis=1
+    )
+    local_proj = jnp.einsum("rd,re->de", normed_one, grad_projected, preferred_element_type=f32)
+    grad_normed_one = scatter(
+        jnp.einsum("re,de->rd", grad_projected, proj, preferred_element_type=f32).astype(bf16)
+    ).astype(f32)
+    pull_one = jax.vjp(modulate, kept, shift_attn, scale_attn)[1]
+    grad_kept_ln, grad_shift_attn, grad_scale_attn = pull_one(
+        grad_normed_one.reshape(images, kept_rows, width)
+    )
+    grad_kept = grad_mixed + grad_kept_ln
+    grad_latents = jax.vmap(place_rows)(cotangent, target, grad_kept.astype(bf16))
+    grad_modulation = jnp.concatenate(
+        [
+            grad_shift_attn[:, 0],
+            grad_scale_attn[:, 0],
+            grad_gate_attn,
+            grad_shift_mlp[:, 0],
+            grad_scale_mlp[:, 0],
+            grad_gate_mlp,
+        ],
+        axis=1,
+    ).astype(bf16)
+
+    every = ("replica", "fsdp")
+    all_grad_mod = lax.all_gather(grad_modulation, every, axis=0, tiled=True)
+    all_cond = lax.all_gather(cond_cols, "replica", axis=0, tiled=True)
+    sum_mod_w = jnp.einsum("bd,be->de", all_cond, all_grad_mod, preferred_element_type=f32)
+    mod_part = modulation_bias.shape[0]
+    sum_mod_b = column_sums(lax.dynamic_slice_in_dim(all_grad_mod, me * mod_part, mod_part, 1))
+    group_grad_mod = lax.dynamic_slice_in_dim(
+        all_grad_mod, lax.axis_index("replica") * group_images, group_images, 0
+    )
+    grad_cond_cols = jnp.einsum(
+        "be,de->bd", group_grad_mod, modulation_weight, preferred_element_type=f32
+    )
+    grad_cond_act = exchange(grad_cond_cols, 0, 1)
+    grad_condition = jax.vjp(jax.nn.silu, cond_float)[1](grad_cond_act)[0]
+
+    local_exp = exchange(local_exp.astype(bf16), 0, 1)
+    local_proj = (
+        exchange(local_proj.astype(bf16).reshape(n, part, 3 * part), 0, 0)
+        .reshape(n, part, 3, part)
+        .transpose(1, 2, 0, 3)
+        .reshape(part, 3 * width)
+    )
+    hidden_part = reduce_weight.shape[0]
+    flat = jnp.concatenate(
+        [
+            local_proj,
+            local_out.astype(bf16),
+            local_exp,
+            local_red.astype(bf16).reshape(part, hidden_part // part * width),
+        ],
+        axis=1,
+    )
+    flat = lax.psum_scatter(flat, "replica", scatter_dimension=1, tiled=True)
+    flat = lax.all_gather(flat, "replica", axis=1, tiled=True).astype(f32)
+    ends = [3 * width, 4 * width, 4 * width + expand_weight.shape[1]]
+    sum_proj_w = flat[:, : ends[0]]
+    sum_out_w = flat[:, ends[0] : ends[1]]
+    sum_exp_w = flat[:, ends[1] : ends[2]]
+    sum_red_w = flat[:, ends[2] :].reshape(hidden_part, width)
+
+    qv_sums = column_sums(grad_projected)
+    whole_red = lax.dynamic_slice_in_dim(column_sums(all_grad_mlp), me * part, part, 0)
+    whole_out = lax.dynamic_slice_in_dim(column_sums(grad_attn), me * part, part, 0)
+    exp_sums = column_sums(grad_hidden)
+    sums = lax.psum(
+        jnp.concatenate([qv_sums[:part], qv_sums[2 * part :], whole_out, exp_sums, whole_red]),
+        "replica",
+    )
+    qv_all = gather(sums[: 2 * part].reshape(1, 2, part), 0).transpose(1, 0, 2).reshape(-1)
+    sum_qv_b = lax.dynamic_slice_in_dim(qv_all, me * 2 * part, 2 * part, 0)
+    sum_out_b = sums[2 * part : 3 * part]
+    sum_exp_b = sums[3 * part : 3 * part + hidden_part]
+    sum_red_b = sums[3 * part + hidden_part :]
+    return (
+        block_out,
+        grad_latents,
+        grad_condition,
+        sum_mod_w,
+        sum_mod_b,
+        sum_proj_w,
+        sum_qv_b,
+        sum_out_w,
+        sum_out_b,
+        sum_exp_w,
+        sum_exp_b,
+        sum_red_w,
+        sum_red_b,
+    )
+
+
 def solution(mesh):
     placed = (
         P(("replica", "fsdp"), None, None),
@@ -322,8 +554,9 @@
         P("fsdp"),
         P(("replica", "fsdp"), None, None),
     )
+    body = local_tp if HEADS % mesh.shape["fsdp"] == 0 else local
     return jax.shard_map(
-        local,
+        body,
         mesh=mesh,
         in_specs=placed,
         out_specs=(

time: 1310 us -> 739 us (0.56)
  waiting for transfers between devices: 1020 us -> 333 us
  blocking collectives: 89.2 us -> 145 us
  starting transfers between devices: 0.73 us -> 41.8 us
  local copies, waits for them, and re-layouts: 55.8 us -> 91.2 us
  matrix products: 97.6 us -> 62.5 us
  other arithmetic: 17.3 us -> 38.3 us
    all_gather x8 -> x5, waiting for transfers between devices: 466 us -> 50.5 us  [the longest x4 50.5 us: gather(): return lax.all_gather(value, 'fsdp', axis=axis, tiled=True)]
    reduce_scatter x5 -> x4, waiting for transfers between devices: 432 us -> 105 us  [scatter(): return lax.psum_scatter(value, 'fsdp', scatter_dimension=0, tiled=True)]
    all_gather x2 -> x4, blocking collectives: 22.1 us -> 112 us  [the longest x2 68.3 us: gather(): return lax.all_gather(value, 'fsdp', axis=axis, tiled=True)]
    all_to_all x0 -> x6, waiting for transfers between devices: none -> 56.6 us  [exchange(): return lax.all_to_all(value, 'fsdp', split, concat, tiled=True)]
    all_to_all x0 -> x6, starting transfers between devices: none -> 41 us  [exchange(): return lax.all_to_all(value, 'fsdp', split, concat, tiled=True)]
    dot_general x20, matrix products: 97.6 us -> 60 us  [the longest x1 6.34 us: local_tp(): jnp.einsum('rd,md->rm', all_grad_mlp, reduce_weight, preferred_element_ty...]
    unnamed x2 -> x1, blocking collectives: 54.6 us -> 25.2 us
    all_to_all x0 -> x9, local copies, waits for them, and re-layouts: none -> 20.3 us  [exchange(): return lax.all_to_all(value, 'fsdp', split, concat, tiled=True)]
  transfers between devices with their start and end apart: 18 -> 17, of which waited for: 16 -> 11; matrix products, arithmetic and copies ran while one was open for 11% -> 14% of each run, Pallas kernels for 0% -> 0%
where the time goes in v1:
time: 739 us; the launch traced here: 728 us
  waiting for transfers between devices  333 us (45%)
  blocking collectives  145 us (20%)
  local copies, waits for them, and re-layouts  91.2 us (12%)
  matrix products  62.5 us (8%)
  starting transfers between devices  41.8 us (6%)
  other arithmetic  38.3 us (5%)
  between operations  16.5 us (2%)
    unnamed x13, waiting for transfers between devices  121 us
    reduce_scatter x4, waiting for transfers between devices, scatter(): return lax.psum_scatter(value, 'fsdp', scatter_dimension=0, tiled=True)  105 us
    all_gather x2, blocking collectives, gather(): return lax.all_gather(value, 'fsdp', axis=axis, tiled=True)  68.3 us
    all_to_all x6, waiting for transfers between devices, exchange(): return lax.all_to_all(value, 'fsdp', split, concat, tiled=True)  56.6 us
    all_gather x4, waiting for transfers between devices, gather(): return lax.all_gather(value, 'fsdp', axis=axis, tiled=True)  50.5 us
    all_to_all x6, starting transfers between devices, exchange(): return lax.all_to_all(value, 'fsdp', split, concat, tiled=True)  41 us
    all_gather x1, blocking collectives, local_tp(): all_grad_mod = lax.all_gather(grad_modulation, every, axis=0, tiled=True)  37.4 us
    unnamed x1, blocking collectives  25.2 us
  transfers between devices with their start and end apart: 17, of which 11 were waited for; matrix products, arithmetic and copies ran while one was open for 14% of the time, Pallas kernels for 0%

profile of v1, /device:TPU:25, one launch (start us, length us, event | category | flops | bytes accessed | tf_op | source)
XLA Modules:
  0.0 728.1 jit_solution(17704941746629069182)
XLA Ops:
  11.1 5.4 all-to-all-start
  18.2 25.2 %all-reduce = bf16[11520]{0:T(1024)(128)(2,1)S(1)} all-reduce(bf16[11520]{0:T(1024)(128)(2,1)S(1)} %dynamic-update-slice), channel_id=2, replica_groups=mesh['replica'=4,'fsdp'=8] {'fsdp'}, use_global_device_ids=true, to_apply=%add | all-reduce | flops 11520 | bytes 46080
  48.4 53.7 %all-reduce.4.cloned.1.call-done = f32[8,6912]{1,0:T(8,128)} async-done(((f32[8,6912]{1,0:T(8,128)}), f32[8,6912]{1,0:T(8,128)}) %all-reduce.4.cloned.1.call-update) | async-done | bytes 221200
  105.4 4.6 reshape.496
  110.0 4.1 copy.136
  114.0 6.2 all-to-all-start.1
  120.4 56.1 %all-gather.6 = f32[8,1,128]{2,1,0:T(1,128)S(1)} all-gather(f32[1,1,128]{2,1,0:T(1,128)S(1)} %fusion.107), channel_id=1, replica_groups=mesh['replica'=4,'fsdp'=8] {'fsdp'}, dimensions={0}, use_global_device_ids=true | all-gather | bytes 4608 | tf_op jit(solution)/shard_map/all_gather | solution.py:339
  176.5 3.3 copy.137
  179.9 3.9 reshape.497
  183.8 3.2 fusion.18
  188.9 2.5 fusion.126
  193.9 2.3 convolution_convert_fusion.2
  197.1 35.3 %reduce-scatter.8.cloned.1.call-done = bf16[128,1152]{1,0:T(8,128)(2,1)} async-done(((bf16[1024,1152]{1,0:T(8,128)(2,1)}), bf16[128,1152]{1,0:T(8,128)(2,1)}) %reduce-scatter.8.cloned.1.call-update) | async-done | bytes 294928 | tf_op jit(solution)/shard_map/reduce_scatter | solution.py:342
  234.9 2.0 add_convert_fusion.1
  237.5 3.7 all_to_all.66
  241.3 2.7 copy.144
  243.9 6.1 all-to-all-start.2
  250.1 47.6 %all-to-all-done.2 = bf16[144,8,576]{2,0,1:T(8,128)(2,1)} async-done(((bf16[144,8,576]{2,0,1:T(8,128)(2,1)}), bf16[144,8,576]{2,0,1:T(8,128)(2,1)}, u32[]{:S(2)}, u32[]{:S(2)}) %all-to-all-start.2) | async-done | bytes 1327136 | tf_op jit(solution)/shard_map/all_to_all | solution.py:345
  297.7 5.2 fusion.15
  302.9 16.3 %all-gather.20.cloned.1.call-done = bf16[1,1024,1152]{2,1,0:T(8,128)(2,1)} async-done(((bf16[1,128,1152]{2,1,0:T(8,128)(2,1)}), bf16[1,1024,1152]{2,1,0:T(8,128)(2,1)}) %all-gather.20.cloned.1.call-update) | async-done | bytes 2359312 | tf_op jit(solution)/shard_map/all_gather | solution.py:339
  319.2 6.3 convert_reduce_fusion.2
  326.5 5.0 convolution_convert_fusion
  331.6 35.8 %reduce-scatter.12.cloned.1.call-done = bf16[128,1152]{1,0:T(8,128)(2,1)} async-done(((bf16[1024,1152]{1,0:T(8,128)(2,1)}), bf16[128,1152]{1,0:T(8,128)(2,1)}) %reduce-scatter.12.cloned.1.call-update) | async-done | bytes 294928 | tf_op jit(solution)/shard_map/reduce_scatter | solution.py:342
  370.2 2.1 multiply_convert_fusion.2
  372.4 4.8 convolution_convert_fusion.4
  377.2 2.6 copy.162
  379.8 6.3 all-to-all-start.5
  386.1 34.2 %all-gather.22.cloned.1.call-done = bf16[1,1024,1152]{2,1,0:T(8,128)(2,1)} async-done(((bf16[1,128,1152]{2,1,0:T(8,128)(2,1)}), bf16[1,1024,1152]{2,1,0:T(8,128)(2,1)}) %all-gather.22.cloned.1.call-update) | async-done | bytes 2359312 | tf_op jit(solution)/shard_map/all_gather | solution.py:339
  420.3 2.7 fusion.32
  427.4 2.3 convolution_convert_fusion.6
  429.6 2.4 copy.159
  432.6 7.1 all-to-all-start.4
  439.7 5.7 convolution_convert_fusion.5
  445.3 3.3 reshape.516
  448.6 2.8 copy.163
  451.4 3.6 all_to_all.77
  455.0 3.0 convolution_convert_fusion.7
  458.0 8.5 %all-to-all-done.4 = bf16[8,144,432]{2,1,0:T(8,128)(2,1)} async-done(((bf16[8,144,432]{2,1,0:T(8,128)(2,1)}), bf16[8,144,432]{2,1,0:T(8,128)(2,1)}, u32[]{:S(2)}, u32[]{:S(2)}) %all-to-all-start.4) | async-done | bytes 995360 | tf_op jit(solution)/shard_map/all_to_all | solution.py:345
  466.5 2.7 copy.160
  469.2 4.3 copy.161
  473.4 4.0 reshape.515
  477.4 3.5 pad_maximum_fusion
  480.9 7.9 %copy.169 = bf16[144,13824]{0,1:T(8,128)(2,1)} copy(bf16[144,13824]{1,0:T(8,128)(2,1)} %pad_maximum_fusion) | data formatting | bytes 7962624
  489.1 6.0 convolution_convert_fusion.1
  495.2 4.4 convolution_convert_fusion.3
  499.8 66.6 %reduce-scatter.16.cloned.1.call-done = bf16[3456,144]{1,0:T(8,128)(2,1)} async-done(((bf16[13824,144]{1,0:T(8,128)(2,1)}), bf16[3456,144]{1,0:T(8,128)(2,1)}) %reduce-scatter.16.cloned.1.call-update) | async-done | bytes 995344
  566.4 2.5 copy.170
  569.1 5.9 all-gather.5
  575.1 2.2 convert_reduce_fusion
  578.0 26.5 %reduce-scatter.10.cloned.1.call-done = bf16[128,1152]{1,0:T(8,128)(2,1)} async-done(((bf16[1024,1152]{1,0:T(8,128)(2,1)}), bf16[128,1152]{1,0:T(8,128)(2,1)}) %reduce-scatter.10.cloned.1.call-update) | async-done | bytes 294928 | tf_op jit(solution)/shard_map/reduce_scatter | solution.py:342
  604.5 3.6 scatter_custom_fusion
  608.2 2.1 convert_reduce_fusion.1
  612.0 8.0 %psum.7 = f32[1152]{0:T(1024)S(1)} all-reduce(f32[1152]{0:T(1024)S(1)} %concatenate.46), channel_id=1, replica_groups=mesh['replica'=4,'fsdp'=8] {'replica'}, use_global_device_ids=true, to_apply=%region_30.32 | all-reduce | flops 1152 | bytes 9216 | tf_op jit(solution)/shard_map/psum | solution.py:513
  620.7 12.2 %all_gather.39 = f32[8,2,144]{2,1,0:T(2,128)S(1)} all-gather(f32[1,2,144]{2,1,0:T(2,128)S(1)} %reshape.517), channel_id=1, replica_groups=mesh['replica'=4,'fsdp'=8] {'fsdp'}, dimensions={0}, use_global_device_ids=true | all-gather | bytes 10368 | tf_op jit(solution)/shard_map/all_gather | solution.py:339
  635.6 7.4 %reduce-scatter.14.cloned.1.call-done = bf16[128,1152]{1,0:T(8,128)(2,1)} async-done(((bf16[1024,1152]{1,0:T(8,128)(2,1)}), bf16[128,1152]{1,0:T(8,128)(2,1)}) %reduce-scatter.14.cloned.1.call-update) | async-done | bytes 294928 | tf_op jit(solution)/shard_map/reduce_scatter | solution.py:342
  644.0 2.0 fusion.55
  646.7 1.9 fusion.49
  649.3 37.4 %all-gather.7 = bf16[32,1,6912]{2,1,0:T(2,128)(2,1)S(1)} all-gather(bf16[1,1,6912]{2,1,0:T(2,128)(2,1)S(1)} %bitcast.350), channel_id=1, replica_groups=mesh['replica'=4,'fsdp'=8] {'replica','fsdp'}, dimensions={0}, use_global_device_ids=true | all-gather | bytes 456192 | tf_op jit(solution)/shard_map/all_gather | solution.py:470
  689.1 9.9 %all-to-all-start.3 = ((f32[8,1,144]{2,1,0:T(1,128)}), f32[8,1,144]{2,1,0:T(1,128)S(1)}, u32[]{:S(2)}, u32[]{:S(2)}) async-start(f32[8,1,144]{2,1,0:T(1,128)} %copy.157), calls=%async_computation.7 | async-start | bytes 16384 | tf_op jit(solution)/shard_map/all_to_all | solution.py:345
  699.1 2.6 scatter_custom_fusion.1
  701.7 4.0 fusion.63
  708.3 4.7 fusion.122
  713.0 3.6 reshape.519
  718.5 2.6 slice.132
  (230 shorter events, 44.9 us)
Async XLA Ops:
  7.2 40.0 %copy-start = (bf16[144,6912]{1,0:T(8,128)(2,1)S(1)}, bf16[144,6912]{1,0:T(8,128)(2,1)}, u32[]{:S(2)}) copy-start(bf16[144,6912]{1,0:T(8,128)(2,1)} %param.21) | copy-start | bytes 5971972
  7.2 9.3 %copy-start.40 = (u32[32]{0:T(128)S(1)}, u32[32]{0:T(128)}, u32[]{:S(2)}) copy-start(u32[32]{0:T(128)} %constant.128) | copy-start | bytes 388
  7.2 2.5 copy-start.23
  7.2 9.3 %copy-start.49 = (s32[1,128]{1,0:T(1,128)S(1)}, s32[1,128]{1,0:T(1,128)}, u32[]{:S(2)}) copy-start(s32[1,128]{1,0:T(1,128)} %param.20) | copy-start | bytes 1540
  7.2 10.6 %copy-start.41 = (bf16[864]{0:T(1024)(128)(2,1)S(1)}, bf16[864]{0:T(1024)(128)(2,1)}, u32[]{:S(2)}) copy-start(bf16[864]{0:T(1024)(128)(2,1)} %param.22) | copy-start | bytes 5188
  7.2 10.6 %copy-start.43 = (bf16[288]{0:T(512)(128)(2,1)S(1)}, bf16[288]{0:T(512)(128)(2,1)}, u32[]{:S(2)}) copy-start(bf16[288]{0:T(512)(128)(2,1)} %param.24) | copy-start | bytes 1732
  7.3 10.6 %copy-start.46 = (bf16[144]{0:T(256)(128)(2,1)S(1)}, bf16[144]{0:T(256)(128)(2,1)}, u32[]{:S(2)}) copy-start(bf16[144]{0:T(256)(128)(2,1)} %param.26) | copy-start | bytes 868
  7.3 10.6 %copy-start.47 = (bf16[144]{0:T(256)(128)(2,1)S(1)}, bf16[144]{0:T(256)(128)(2,1)}, u32[]{:S(2)}) copy-start(bf16[144]{0:T(256)(128)(2,1)} %param.30) | copy-start | bytes 868
  8.5 37.7 %copy-start.3 = (bf16[1,256,1152]{2,1,0:T(8,128)(2,1)}, bf16[1,256,1152]{2,1,0:T(8,128)(2,1)S(1)}, u32[]{:S(2)}) copy-start(bf16[1,256,1152]{2,1,0:T(8,128)(2,1)S(1)} %copy.245) | copy-start | bytes 1769476
  11.1 36.1 %all-to-all-start = ((bf16[1,8,144]{2,0,1:T(2,128)(2,1)}), bf16[1,8,144]{2,0,1:T(2,128)(2,1)S(1)}, u32[]{:S(2)}, u32[]{:S(2)}) async-start(bf16[1,8,144]{2,0,1:T(2,128)(2,1)} %all_to_all.78), calls=%async_computation | async-start | bytes 16384 | tf_op jit(solution)/shard_map/all_to_all | solution.py:345
  16.5 85.6 %all-reduce.4.cloned.1.call-start = ((), (), s32[]{:S(2)}) async-start(), calls=%async_computation.21 | async-start | bytes 442368
  44.7 59.6 %copy-start.28 = (f32[128]{0:T(128)}, f32[128]{0:T(128)S(1)}, u32[]{:S(2)}) copy-start(f32[128]{0:T(128)S(1)} %broadcast_multiply_fusion.1) | copy-start | bytes 1540
  44.9 3.3 copy-start.44
  46.2 58.1 %copy-start.32 = (f32[128]{0:T(128)S(1)}, f32[128]{0:T(128)}, u32[]{:S(2)}) copy-start(f32[128]{0:T(128)} %fusion.110) | copy-start | bytes 1540
  47.2 323.0 %copy-start.5 = (bf16[128,1152]{1,0:T(8,128)(2,1)}, bf16[128,1152]{1,0:T(8,128)(2,1)S(1)}, u32[]{:S(2)}) copy-start(bf16[128,1152]{1,0:T(8,128)(2,1)S(1)} %gather_fusion.1) | copy-start | bytes 884740
  48.3 135.5 %all-gather.16.cloned.1.call-start = ((), (), s32[]{:S(2)}) async-start(), calls=%async_computation.16 | async-start | bytes 2654208 | tf_op jit(solution)/shard_map/all_gather | solution.py:339
  48.4 65.7 %copy-start.34 = (f32[128]{0:T(128)}, f32[128]{0:T(128)S(1)}, u32[]{:S(2)}) copy-start(f32[128]{0:T(128)S(1)} %compare_convert_fusion) | copy-start | bytes 1540
  114.0 62.5 %all-to-all-start.1 = ((bf16[8,144,3,144]{1,3,2,0:T(8,128)(2,1)}), bf16[8,144,3,144]{1,3,2,0:T(8,128)(2,1)}, u32[]{:S(2)}, u32[]{:S(2)}) async-start(bf16[8,144,3,144]{1,3,2,0:T(8,128)(2,1)} %copy.136), calls=%async_computation.1 | async-start | bytes 3538944 | tf_op jit(solution)/shard_map/all_to_all | solution.py:345
  120.2 112.2 %reduce-scatter.8.cloned.1.call-start = ((), (), s32[]{:S(2)}) async-start(), calls=%async_computation.11 | async-start | bytes 2654208 | tf_op jit(solution)/shard_map/reduce_scatter | solution.py:342
  187.3 5.8 copy-start.12
  191.4 4.8 copy-start.30
  191.4 2.5 copy-start.16
  196.2 38.7 %copy-start.19 = (f32[1152]{0:T(1024)S(1)}, f32[1152]{0:T(1024)}, u32[]{:S(2)}) copy-start(f32[1152]{0:T(1024)} %get-tuple-element.21) | copy-start | bytes 13828
  196.3 101.4 %all-gather.18.cloned.1.call-start = ((), (), s32[]{:S(2)}) async-start(), calls=%async_computation.17 | async-start | bytes 2654208 | tf_op jit(solution)/shard_map/all_gather | solution.py:339
  233.6 136.5 %copy-start.21 = (f32[128]{0:T(128)}, f32[128]{0:T(128)S(1)}, u32[]{:S(2)}) copy-start(f32[128]{0:T(128)S(1)} %broadcast_multiply_fusion) | copy-start | bytes 1540
  234.9 135.3 %copy-start.26 = (f32[128]{0:T(128)}, f32[128]{0:T(128)S(1)}, u32[]{:S(2)}) copy-start(f32[128]{0:T(128)S(1)} %fusion.111) | copy-start | bytes 1540
  236.9 82.2 %all-gather.20.cloned.1.call-start = ((), (), s32[]{:S(2)}) async-start(), calls=%async_computation.18 | async-start | bytes 2654208 | tf_op jit(solution)/shard_map/all_gather | solution.py:339
  241.3 8.8 %copy-start.39 = (bf16[576]{0:T(1024)(128)(2,1)S(1)}, bf16[576]{0:T(1024)(128)(2,1)}, u32[]{:S(2)}) copy-start(bf16[576]{0:T(1024)(128)(2,1)} %param.28) | copy-start | bytes 3460
  243.9 53.7 %all-to-all-start.2 = ((bf16[144,8,576]{2,0,1:T(8,128)(2,1)}), bf16[144,8,576]{2,0,1:T(8,128)(2,1)}, u32[]{:S(2)}, u32[]{:S(2)}) async-start(bf16[144,8,576]{2,0,1:T(8,128)(2,1)} %copy.144), calls=%async_computation.3 | async-start | bytes 2949120 | tf_op jit(solution)/shard_map/all_to_all | solution.py:345
  250.1 117.4 %reduce-scatter.12.cloned.1.call-start = ((), (), s32[]{:S(2)}) async-start(), calls=%async_computation.13 | async-start | bytes 2654208 | tf_op jit(solution)/shard_map/reduce_scatter | solution.py:342
  331.5 35.9 %copy-start.1 = (bf16[128,1152]{1,0:T(8,128)(2,1)S(1)}, bf16[128,1152]{1,0:T(8,128)(2,1)}, u32[]{:S(2)}) copy-start(bf16[128,1152]{1,0:T(8,128)(2,1)} %reduce-scatter.8.cloned.1.call-done) | copy-start | bytes 884740
  331.5 38.7 %copy-start.35 = (f32[128]{0:T(128)S(1)}, f32[128]{0:T(128)}, u32[]{:S(2)}) copy-start(f32[128]{0:T(128)} %copy-done.34) | copy-start | bytes 1540
  331.6 88.8 %all-gather.22.cloned.1.call-start = ((), (), s32[]{:S(2)}) async-start(), calls=%async_computation.19 | async-start | bytes 2654208 | tf_op jit(solution)/shard_map/all_gather | solution.py:339
  368.8 3.6 copy-start.37
  370.2 2.2 copy-start.38
  377.2 43.2 %copy-start.17 = (bf16[144,1152]{1,0:T(8,128)(2,1)S(1)}, bf16[144,1152]{1,0:T(8,128)(2,1)}, u32[]{:S(2)}) copy-start(bf16[144,1152]{1,0:T(8,128)(2,1)} %param.25) | copy-start | bytes 995332
  379.8 52.8 %all-to-all-start.5 = ((bf16[8,144,576]{2,1,0:T(8,128)(2,1)}), bf16[8,144,576]{2,1,0:T(8,128)(2,1)}, u32[]{:S(2)}, u32[]{:S(2)}) async-start(bf16[8,144,576]{2,1,0:T(8,128)(2,1)} %bitcast.333), calls=%async_computation.9 | async-start | bytes 2949120 | tf_op jit(solution)/shard_map/all_to_all | solution.py:345
  420.3 2.7 copy-start.15
  420.3 2.7 copy-start.31
  424.4 1.4 copy-start.13
  425.4 2.0 copy-start.48
  432.6 33.9 %all-to-all-start.4 = ((bf16[8,144,432]{2,1,0:T(8,128)(2,1)}), bf16[8,144,432]{2,1,0:T(8,128)(2,1)}, u32[]{:S(2)}, u32[]{:S(2)}) async-start(bf16[8,144,432]{2,1,0:T(8,128)(2,1)} %bitcast.334), calls=%async_computation.8 | async-start | bytes 2359296 | tf_op jit(solution)/shard_map/all_to_all | solution.py:345
  439.6 126.8 %reduce-scatter.16.cloned.1.call-start = ((), (), s32[]{:S(2)}) async-start(), calls=%async_computation.20 | async-start | bytes 8847360
  448.6 6.4 copy-start.8
  469.2 8.2 %copy-start.11 = (bf16[144,1152]{1,0:T(8,128)(2,1)S(1)}, bf16[144,1152]{1,0:T(8,128)(2,1)}, u32[]{:S(2)}) copy-start(bf16[144,1152]{1,0:T(8,128)(2,1)} %convolution_convert_fusion.7) | copy-start | bytes 995332
  488.8 115.7 %reduce-scatter.10.cloned.1.call-start = ((), (), s32[]{:S(2)}) async-start(), calls=%async_computation.12 | async-start | bytes 2654208 | tf_op jit(solution)/shard_map/reduce_scatter | solution.py:342
  495.2 147.8 %reduce-scatter.14.cloned.1.call-start = ((), (), s32[]{:S(2)}) async-start(), calls=%async_computation.14 | async-start | bytes 2654208 | tf_op jit(solution)/shard_map/reduce_scatter | solution.py:342
  499.7 69.3 %copy-start.20 = (f32[8,144]{1,0:T(8,128)S(1)}, f32[8,144]{1,0:T(8,128)}, u32[]{:S(2)}) copy-start(f32[8,144]{1,0:T(8,128)} %get-tuple-element.32) | copy-start | bytes 13828
  499.7 69.3 %copy-start.50 = (s32[1,128]{1,0:T(1,128)S(1)}, s32[1,128]{1,0:T(1,128)}, u32[]{:S(2)}) copy-start(s32[1,128]{1,0:T(1,128)} %param.20) | copy-start | bytes 1540
  499.7 208.6 %all-gather.14.cloned.1.call-start = ((), (), s32[]{:S(2)}) async-start(), calls=%async_computation.15 | async-start | bytes 4976640 | tf_op jit(solution)/shard_map/all_gather | solution.py:502
  568.9 8.5 %copy-start.4 = (bf16[128,1152]{1,0:T(8,128)(2,1)S(1)}, bf16[128,1152]{1,0:T(8,128)(2,1)}, u32[]{:S(2)}) copy-start(bf16[128,1152]{1,0:T(8,128)(2,1)} %reduce-scatter.12.cloned.1.call-done) | copy-start | bytes 884740
  569.1 39.1 %copy-start.51 = (s32[128]{0:T(128)}, s32[128]{0:T(128)S(1)}, u32[]{:S(2)}) copy-start(s32[128]{0:T(128)S(1)} %fusion.108) | copy-start | bytes 1540
  578.0 66.0 %copy-start.22 = (f32[128]{0:T(128)S(1)}, f32[128]{0:T(128)}, u32[]{:S(2)}) copy-start(f32[128]{0:T(128)} %copy-done.21) | copy-start | bytes 1540
  608.2 2.2 copy-start.10
  646.0 53.0 %copy-start.27 = (f32[128]{0:T(128)S(1)}, f32[128]{0:T(128)}, u32[]{:S(2)}) copy-start(f32[128]{0:T(128)} %copy-done.26) | copy-start | bytes 1540
  646.0 53.0 %copy-start.29 = (f32[128]{0:T(128)S(1)}, f32[128]{0:T(128)}, u32[]{:S(2)}) copy-start(f32[128]{0:T(128)} %copy-done.28) | copy-start | bytes 1540
  646.0 53.0 %copy-start.33 = (f32[128]{0:T(128)S(1)}, f32[128]{0:T(128)}, u32[]{:S(2)}) copy-start(f32[128]{0:T(128)} %fusion.110) | copy-start | bytes 1540
  646.0 53.0 %copy-start.36 = (f32[128]{0:T(128)S(1)}, f32[128]{0:T(128)}, u32[]{:S(2)}) copy-start(f32[128]{0:T(128)} %copy-done.34) | copy-start | bytes 1540
  646.7 40.0 %copy-start.42 = (f32[128]{0:T(128)}, f32[128]{0:T(128)S(1)}, u32[]{:S(2)}) copy-start(f32[128]{0:T(128)S(1)} %multiply_multiply_fusion.2) | copy-start | bytes 1540
  648.6 50.4 %copy-start.45 = (f32[128]{0:T(128)S(1)}, f32[128]{0:T(128)}, u32[]{:S(2)}) copy-start(f32[128]{0:T(128)} %get-tuple-element.17) | copy-start | bytes 1540
  689.1 18.4 %all-to-all-start.3 = ((f32[8,1,144]{2,1,0:T(1,128)}), f32[8,1,144]{2,1,0:T(1,128)S(1)}, u32[]{:S(2)}, u32[]{:S(2)}) async-start(f32[8,1,144]{2,1,0:T(1,128)} %copy.157), calls=%async_computation.7 | async-start | bytes 16384 | tf_op jit(solution)/shard_map/all_to_all | solution.py:345
  701.7 11.4 %copy-start.2 = (bf16[256,1152]{1,0:T(8,128)(2,1)}, bf16[256,1152]{1,0:T(8,128)(2,1)S(1)}, u32[]{:S(2)}) copy-start(bf16[256,1152]{1,0:T(8,128)(2,1)S(1)} %scatter_custom_fusion.1) | copy-start | bytes 1769476
  701.7 6.0 copy-start.24
  701.7 6.0 copy-start.25
  (6 other events, 5.5 us)
Sparse Core Ops, SparseCore 0:
  48.4 53.5 all-reduce.3
  105.5 50.7 all-gather.15
  196.4 35.9 reduce-scatter.7
  237.1 48.7 all-gather.17
  288.0 31.1 all-gather.19
  331.7 35.7 reduce-scatter.11
  372.5 47.8 all-gather.21
  489.0 77.4 reduce-scatter.15
  569.4 35.0 reduce-scatter.9
  607.4 35.5 reduce-scatter.13
  645.5 54.2 all-gather.13

commit v2 on v0

--- a/solution.py
+++ b/solution.py
@@ -1,6 +1,8 @@
 import jax
 import jax.numpy as jnp
 from jax import lax
+from jax.experimental import pallas as pl
+from jax.experimental.pallas import tpu as pltpu
 from jax.sharding import PartitionSpec as P
 
 HEADS = 16
@@ -304,6 +306,986 @@
     )
 
 
+MESH = pl.DeviceIdType.MESH
+SAME_CORE = ((1, 0), (0, 1), (1, 1))
+PAD = 80
+LANES_Q = 256
+
+
+def fused_kernel(
+    latents,
+    cotangent,
+    slots,
+    live_col,
+    live_row,
+    cond_pack,
+    mod_bias,
+    extra,
+    mod_w,
+    proj_pack,
+    exp_pack,
+    red_pack,
+    out_shard,
+    o_block,
+    o_latents,
+    o_slabs,
+    o_cond,
+    o_gcond,
+    o_exp,
+    o_red,
+    o_proj,
+    o_out,
+    cond_all,
+    extra_all,
+    live_all,
+    mod_send,
+    mod_all,
+    proj_all,
+    exp_all,
+    red_all,
+    out_w,
+    proj_wide,
+    spread,
+    x_one,
+    x_two,
+    g_mlp,
+    g_attn,
+    qkv,
+    probs,
+    attended,
+    act,
+    g_hid,
+    d_qkv,
+    part_a,
+    part_b,
+    sib_a,
+    sib_b,
+    rows_a,
+    rows_b,
+    kept,
+    norm_one,
+    rstd_one,
+    g_rows,
+    branch_a,
+    mixed,
+    norm_two,
+    rstd_two,
+    g_mixed,
+    slab,
+    slabs,
+    gcond,
+    d_exp,
+    d_red,
+    d_proj,
+    d_out,
+    z_exp,
+    z_red,
+    z_proj,
+    z_out,
+    local_sem,
+    small_s,
+    small_r,
+    w_s,
+    w_r,
+    ag_s,
+    ag_r,
+    sb_s,
+    sb_r,
+    rs_s,
+    rs_r,
+    dz_s,
+    dz_r,
+    dp_s,
+    dp_r,
+    ow_s,
+    ow_r,
+):
+    f32 = jnp.float32
+    bf16 = jnp.bfloat16
+    r = lax.axis_index("replica")
+    f = lax.axis_index("fsdp")
+    x, y, c, z = r % 2, r // 2, f % 2, f // 2
+    width = latents.shape[1]
+    rows = slots.shape[0]
+    part = out_shard.shape[0]
+    third = width // 3
+    me = 4 * c + r
+    other = (c + 1) % 2
+
+    def ident(r2, f2):
+        return {"replica": r2, "fsdp": f2}
+
+    def remote(src, dst, s_sem, r_sem, dev):
+        return pltpu.make_async_remote_copy(
+            src_ref=src,
+            dst_ref=dst,
+            send_sem=s_sem,
+            recv_sem=r_sem,
+            device_id=dev,
+            device_id_type=MESH,
+        )
+
+    def plane(dx, dy):
+        return ((y + dy) % 2) * 2 + (x + dx) % 2
+
+    sibling = ident(r, 2 * z + other)
+    line = []
+    for dz in range(4):
+        for dc in range(2):
+            if dz or dc:
+                line.append(((z + dz) % 4, (c + dc) % 2))
+    board = []
+    for dx in range(2):
+        for dy in range(2):
+            for dc in range(2):
+                if dx or dy or dc:
+                    board.append((plane(dx, dy), (c + dc) % 2))
+
+    barrier = pltpu.get_barrier_semaphore()
+    for z2, c2 in line:
+        pl.semaphore_signal(barrier, inc=1, device_id=ident(r, 2 * z2 + c2), device_id_type=MESH)
+    for r2, c2 in board:
+        pl.semaphore_signal(barrier, inc=1, device_id=ident(r2, 2 * z + c2), device_id_type=MESH)
+    pl.semaphore_wait(barrier, len(line) + len(board))
+
+    def line_send(kind, sems_s, sems_r, src_of, dst_of):
+        copies = []
+        for k, (z2, c2) in enumerate(line):
+            f2 = 2 * z2 + c2
+            cp = remote(
+                src_of(f2, c2),
+                dst_of(f),
+                sems_s.at[kind, k],
+                sems_r.at[kind, f],
+                ident(r, f2),
+            )
+            cp.start()
+            copies.append(cp)
+        return copies
+
+    def line_wait(kind, sems_s, sems_r, src_of, dst_of):
+        for k, (z2, c2) in enumerate(line):
+            f2 = 2 * z2 + c2
+            remote(
+                src_of(f, c), dst_of(f2), sems_s.at[kind, k], sems_r.at[kind, f2], ident(r, f2)
+            ).wait_recv()
+
+    def drain(copies):
+        for cp in copies:
+            cp.wait_send()
+
+    def cond_src(f2, c2):
+        return cond_pack.at[f2]
+
+    def cond_dst(f2):
+        return cond_all.at[f2]
+
+    def extra_src(f2, c2):
+        return extra.at[c2]
+
+    def extra_dst(f2):
+        return extra_all.at[f2]
+
+    def proj_src(f2, c2):
+        return proj_pack.at[c2]
+
+    def proj_dst(f2):
+        return proj_all.at[pl.ds(pl.multiple_of(f2 * part, 16), part)]
+
+    def exp_src(f2, c2):
+        return exp_pack.at[c2]
+
+    def exp_dst(f2):
+        return exp_all.at[pl.ds(pl.multiple_of(f2 * part, 16), part)]
+
+    def red_src(f2, c2):
+        return red_pack.at[c2]
+
+    def red_dst(f2):
+        return red_all.at[pl.ds(pl.multiple_of(f2 * PAD, 16), PAD)]
+
+    sent = line_send(0, small_s, small_r, cond_src, cond_dst)
+    sent += line_send(0, w_s, w_r, proj_src, proj_dst)
+    sent += line_send(1, small_s, small_r, extra_src, extra_dst)
+    live_sent = []
+    for k, (r2, c2) in enumerate(board):
+        cp = remote(
+            live_row,
+            live_all.at[me],
+            small_s.at[3, k],
+            small_r.at[3, me],
+            ident(r2, 2 * z + c2),
+        )
+        cp.start()
+        live_sent.append(cp)
+    local = [
+        pltpu.make_async_copy(cond_pack.at[f], cond_all.at[f], local_sem.at[0]),
+        pltpu.make_async_copy(extra.at[c], extra_all.at[f], local_sem.at[1]),
+        pltpu.make_async_copy(proj_pack.at[c], proj_dst(f), local_sem.at[2]),
+        pltpu.make_async_copy(exp_pack.at[c], exp_dst(f), local_sem.at[3]),
+        pltpu.make_async_copy(red_pack.at[c], red_dst(f), local_sem.at[4]),
+        pltpu.make_async_copy(live_row, live_all.at[me], local_sem.at[5]),
+    ]
+    for cp in local:
+        cp.start()
+
+    def one_hot():
+        ids = lax.broadcasted_iota(jnp.int32, (rows, latents.shape[0]), 1)
+        return jnp.where(ids == slots[...], 1.0, 0.0)
+
+    def dot(a, b):
+        return jnp.dot(a, b, preferred_element_type=f32)
+
+    def dot_t(a, b):
+        return lax.dot_general(a, b, (((1,), (1,)), ((), ())), preferred_element_type=f32)
+
+    def t_dot(a, b):
+        return lax.dot_general(a, b, (((0,), (0,)), ((), ())), preferred_element_type=f32)
+
+    kept[...] = dot(one_hot().astype(bf16), latents[...])
+    g_rows[...] = dot((one_hot() * live_col[...]).astype(bf16), cotangent[...])
+
+    def normalise(values, norm_ref, rstd_ref):
+        centred = values - jnp.mean(values, axis=-1, keepdims=True)
+        rstd = lax.rsqrt(jnp.mean(centred * centred, axis=-1, keepdims=True) + 1e-06)
+        norm_ref[...] = centred * rstd
+        rstd_ref[...] = rstd
+
+    normalise(kept[...], norm_one, rstd_one)
+    out_w[part:, :] = jnp.zeros((out_w.shape[0] - part, width), bf16)
+    split = lax.broadcasted_iota(jnp.int32, spread.shape, 0)
+    column = lax.broadcasted_iota(jnp.int32, spread.shape, 1)
+    skip = jnp.where(split >= part, LANES_Q - part, 0) + jnp.where(
+        split >= 2 * part, LANES_Q - part, 0
+    )
+    spread[...] = jnp.where(column == split + skip, 1.0, 0.0).astype(bf16)
+
+    for cp in local:
+        cp.wait()
+    line_wait(0, small_s, small_r, cond_src, cond_dst)
+    cond_cols = jnp.sum(cond_all[...].astype(f32), axis=1).astype(bf16)
+    mod_send[...] = jnp.zeros(mod_send.shape, f32)
+    for p in range(6):
+        piece = dot(cond_cols, mod_w[:, p * width : (p + 1) * width]) + mod_bias[p : p + 1, :]
+        mod_send[:, p, :] = piece
+
+    def mod_src(f2, c2):
+        return mod_send.at[f2]
+
+    def mod_dst(f2):
+        return mod_all.at[f2]
+
+    sent += line_send(2, small_s, small_r, mod_src, mod_dst)
+    mod_all[f] = mod_send[f]
+    cond_sent = []
+    for k, (dx, dy) in enumerate(SAME_CORE):
+        cp = remote(
+            cond_all,
+            o_cond.at[r],
+            small_s.at[4, k],
+            small_r.at[4, r],
+            ident(plane(dx, dy), f),
+        )
+        cp.start()
+        cond_sent.append(cp)
+    own_cond = pltpu.make_async_copy(cond_all, o_cond.at[r], local_sem.at[0])
+    own_cond.start()
+    line_wait(2, small_s, small_r, mod_src, mod_dst)
+    modulation = jnp.sum(mod_all[...], axis=0)
+    shift_attn, scale_attn, gate_attn, shift_mlp, scale_mlp, gate_mlp = [
+        modulation[p : p + 1, :] for p in range(6)
+    ]
+
+    def own(ref):
+        return ref.at[pl.ds(pl.multiple_of(me * rows, rows), rows)]
+
+    def slot(ref, u):
+        return ref.at[pl.ds(pl.multiple_of(u * rows, rows), rows)]
+
+    def gather_start(kind, buf):
+        copies = [
+            remote(own(buf), own(buf), ag_s.at[kind, 0], ag_r.at[kind, me], sibling),
+        ]
+        for k, (dx, dy) in enumerate(SAME_CORE):
+            copies.append(
+                remote(
+                    own(buf),
+                    own(buf),
+                    ag_s.at[kind, 1 + k],
+                    ag_r.at[kind, me],
+                    ident(plane(dx, dy), f),
+                )
+            )
+        for cp in copies:
+            cp.start()
+        return copies
+
+    def gather_end(kind, buf):
+        copies = []
+        for k, (dx, dy) in enumerate(SAME_CORE):
+            u = 4 * c + plane(dx, dy)
+            cp = remote(slot(buf, u), slot(buf, u), ag_s.at[kind, 4 + k], ag_r.at[kind, u], sibling)
+            cp.wait_recv()
+            cp.start()
+            copies.append(cp)
+        for r2 in range(4):
+            u = 4 * other + r2
+            remote(
+                slot(buf, u), slot(buf, u), ag_s.at[kind, 0], ag_r.at[kind, u], sibling
+            ).wait_recv()
+        return copies
+
+    def reduce_chunk(kind, k, cc, values, buf, sib, landing):
+        base = pl.multiple_of(cc * 4 * rows + (k % 2) * 2 * rows, 2 * rows)
+        here = pl.ds(base, 2 * rows)
+        there = pl.ds(pl.multiple_of((k % 2) * 2 * rows, 2 * rows), 2 * rows)
+        slot_k = k % 2
+
+        @pl.when(k < 2)
+        def _():
+            buf[here, :] = values.astype(bf16)
+            remote(
+                buf.at[here], sib.at[there], sb_s.at[kind, slot_k], sb_r.at[kind, slot_k], sibling
+            ).start()
+
+        @pl.when(k >= 2)
+        def _():
+            remote(
+                buf.at[here], sib.at[there], sb_s.at[kind, slot_k], sb_r.at[kind, slot_k], sibling
+            ).wait_recv()
+            buf[here, :] = (values + sib[there, :].astype(f32)).astype(bf16)
+            for x2 in range(2):
+                r2 = 2 * slot_k + x2
+
+                @pl.when(r2 != r)
+                def _():
+                    remote(
+                        slot(buf, 4 * c + r2),
+                        landing.at[r],
+                        rs_s.at[kind, r2],
+                        rs_r.at[kind, r],
+                        ident(r2, f),
+                    ).start()
+
+    def reduce_end(kind, buf, landing):
+        total = own(buf)[...].astype(f32)
+        for dx, dy in SAME_CORE:
+            r2 = plane(dx, dy)
+            remote(
+                own(buf), landing.at[r2], rs_s.at[kind, r2], rs_r.at[kind, r2], ident(r2, f)
+            ).wait_recv()
+            total += landing[r2].astype(f32)
+        return total
+
+    def reduce_drain(kind, buf, sib, landing):
+        for k in range(2):
+            there = pl.ds(k * 2 * rows, 2 * rows)
+            remote(
+                sib.at[there], sib.at[there], sb_s.at[kind, k], sb_r.at[kind, k], sibling
+            ).wait_send()
+        for dx, dy in SAME_CORE:
+            r2 = plane(dx, dy)
+            remote(
+                own(buf), landing.at[r2], rs_s.at[kind, r2], rs_r.at[kind, r2], ident(r2, f)
+            ).wait_send()
+
+    own(x_one)[...] = (norm_one[...] * (1.0 + scale_attn) + shift_attn).astype(bf16)
+    sent += gather_start(0, x_one)
+    grad_mlp = (gate_mlp * g_rows[...]).astype(bf16)
+    own(g_mlp)[...] = grad_mlp
+    slab[...] = jnp.zeros(slab.shape, f32)
+    slab[6:7, :] = jnp.sum(grad_mlp.astype(f32), axis=0, keepdims=True)
+
+    @pl.when(z == r)
+    def _():
+        for dz in range(1, 4):
+            remote(
+                out_shard,
+                out_w.at[pl.ds(0, part)],
+                ow_s.at[dz - 1],
+                ow_r.at[0],
+                ident(r, 2 * ((z + dz) % 4) + c),
+            ).start()
+        out_w[:part, :] = out_shard[...]
+
+    line_wait(0, w_s, w_r, proj_src, proj_dst)
+    sent += line_send(1, w_s, w_r, exp_src, exp_dst)
+    proj_wide[...] = dot(proj_all[...], spread[...]).astype(bf16)
+    line_wait(1, small_s, small_r, extra_src, extra_dst)
+    biases = jnp.sum(extra_all[...].astype(f32), axis=0)
+    out_b, red_b, exp_b, qv_b = [biases[p : p + 1, :] for p in range(4)]
+    for k, (r2, c2) in enumerate(board):
+        remote(
+            live_row,
+            live_all.at[4 * c2 + r2],
+            small_s.at[3, k],
+            small_r.at[3, 4 * c2 + r2],
+            ident(r2, 2 * z + c2),
+        ).wait_recv()
+    sent += gather_end(0, x_one)
+    sent += gather_start(1, g_mlp)
+    sent += line_send(2, w_s, w_r, red_src, red_dst)
+
+    lane = lax.broadcasted_iota(jnp.int32, (1, LANES_Q), 1)
+    heads = [
+        jnp.where((lane >= h * HEAD_DIM) & (lane < (h + 1) * HEAD_DIM), 1.0, 0.0).astype(bf16)
+        for h in range(2)
+    ]
+    scale = HEAD_DIM ** (-0.5)
+
+    @pl.when(z != r)
+    def _():
+        remote(
+            out_shard, out_w.at[pl.ds(0, part)], ow_s.at[0], ow_r.at[0], ident(r, 2 * z + c)
+        ).wait_recv()
+
+    def chunk_of(k):
+        cc = (c + 1 + k // 2) % 2
+        first = 4 * cc + 2 * (k % 2)
+        return cc, first, pl.ds(pl.multiple_of(first * rows, 2 * rows), 2 * rows)
+
+    def attend(k, carry):
+        cc, first, here = chunk_of(k)
+        wide = dot(x_one[here, :], proj_wide[...])
+        qkv[here, :LANES_Q] = (wide[:, :LANES_Q] + qv_b[:, :LANES_Q]).astype(bf16)
+        qkv[here, LANES_Q : 2 * LANES_Q] = wide[:, LANES_Q : 2 * LANES_Q].astype(bf16)
+        qkv[here, 2 * LANES_Q :] = (
+            wide[:, 2 * LANES_Q :] + qv_b[:, LANES_Q : 2 * LANES_Q]
+        ).astype(bf16)
+        for i in range(2):
+            u = first + i
+            at = pl.ds(pl.multiple_of(u * rows, rows), rows)
+            q = qkv[at, :LANES_Q]
+            key = qkv[at, LANES_Q : 2 * LANES_Q]
+            val = qkv[at, 2 * LANES_Q :]
+            alive = live_all[u][0:1, :] > 0.5
+            total = jnp.zeros((rows, LANES_Q), f32)
+            for h in range(2):
+                s = dot_t(q * heads[h], key) * scale
+                s = jnp.where(alive, s, -1e30)
+                e = jnp.exp(s - jnp.max(s, axis=-1, keepdims=True))
+                p = e / jnp.sum(e, axis=-1, keepdims=True)
+                probs[2 * u + h] = p
+                total += dot(p.astype(bf16), val) * heads[h].astype(f32)
+            attended[at, :] = total.astype(bf16)
+        values = dot(attended[here, :], out_w[...])
+        reduce_chunk(0, k, cc, values, part_a, sib_a, rows_a)
+        return carry
+
+    lax.fori_loop(0, 4, attend, 0)
+    branch = reduce_end(0, part_a, rows_a) + out_b
+    branch_a[...] = branch
+    mixed[...] = kept[...] + gate_attn * branch
+    normalise(mixed[...], norm_two, rstd_two)
+    own(x_two)[...] = (norm_two[...] * (1.0 + scale_mlp) + shift_mlp).astype(bf16)
+    sent += gather_start(2, x_two)
+    sent += gather_end(1, g_mlp)
+    line_wait(1, w_s, w_r, exp_src, exp_dst)
+    line_wait(2, w_s, w_r, red_src, red_dst)
+    sent += gather_end(2, x_two)
+    reduce_drain(0, part_a, sib_a, rows_a)
+
+    k_gelu = 0.7978845608028654
+    hid_b = exp_b[:, : exp_all.shape[1]]
+
+    def feed(k, carry):
+        cc, first, here = chunk_of(k)
+        hid = dot(x_two[here, :], exp_all[...]) + hid_b
+        square = hid * hid
+        th = jnp.tanh(k_gelu * hid * (1.0 + 0.044715 * square))
+        act[here, :] = (0.5 * hid * (1.0 + th)).astype(bf16)
+        slope = 0.5 * (1.0 + th) + 0.5 * hid * (1.0 - th * th) * k_gelu * (
+            1.0 + 3.0 * 0.044715 * square
+        )
+        grad = (dot_t(g_mlp[here, :], red_all[...]) * slope).astype(bf16)
+        g_hid[here, :] = grad
+        values = dot_t(grad, exp_all[...])
+        reduce_chunk(1, k, cc, values, part_b, sib_b, rows_b)
+        return carry
+
+    lax.fori_loop(0, 4, feed, 0)
+
+    hid_sum = jnp.sum(g_hid[...].astype(f32), axis=0, keepdims=True)
+    slab[8:9, : exp_all.shape[1]] = hid_sum
+
+    def zsend(kind, src, landing, height):
+        copies = []
+        for dz in range(1, 4):
+            z2 = (z + dz) % 4
+            cp = remote(
+                src.at[pl.ds(pl.multiple_of(z2 * height, 16), height)],
+                landing.at[dz - 1],
+                dz_s.at[kind, dz - 1],
+                dz_r.at[kind, dz - 1],
+                ident(r, 2 * z2 + c),
+            )
+            cp.start()
+            copies.append(cp)
+        return copies
+
+    def wide_grad(k, carry):
+        at = pl.ds(pl.multiple_of(k * third, 128), third)
+        d_exp[at, :] = t_dot(x_two[:, at], g_hid[...]).astype(bf16)
+        return carry
+
+    lax.fori_loop(0, 3, wide_grad, 0)
+    sent += zsend(0, d_exp, z_exp, 2 * part)
+
+    grad_two = reduce_end(1, part_b, rows_b)
+
+    def back_norm(grad, scale_part, norm, rstd):
+        g_shift = jnp.sum(grad, axis=0, keepdims=True)
+        g_scale = jnp.sum(grad * norm, axis=0, keepdims=True)
+        e = grad * (1.0 + scale_part)
+        inner = jnp.mean(e * norm, axis=-1, keepdims=True)
+        return g_shift, g_scale, (e - jnp.mean(e, axis=-1, keepdims=True) - norm * inner) * rstd
+
+    g_shift, g_scale, through = back_norm(grad_two, scale_mlp, norm_two[...], rstd_two[...])
+    slab[3:4, :] = g_shift
+    slab[4:5, :] = g_scale
+    g_mixed[...] = g_rows[...] + through
+    slab[2:3, :] = jnp.sum(g_mixed[...] * branch_a[...], axis=0, keepdims=True)
+    grad_at = (gate_attn * g_mixed[...]).astype(bf16)
+    own(g_attn)[...] = grad_at
+    slab[7:8, :] = jnp.sum(grad_at.astype(f32), axis=0, keepdims=True)
+    sent += gather_start(3, g_attn)
+
+    def red_grad(k, carry):
+        at = pl.ds(pl.multiple_of(k * third, 128), third)
+        d_red[:, at] = t_dot(act[...], g_mlp[:, at]).astype(bf16)
+        return carry
+
+    lax.fori_loop(0, 3, red_grad, 0)
+    sent += zsend(1, d_red, z_red, 2 * PAD)
+    sent += gather_end(3, g_attn)
+    reduce_drain(1, part_b, sib_b, rows_b)
+
+    def attend_back(k, carry):
+        cc, first, here = chunk_of(k)
+        g_att = dot_t(g_attn[here, :], out_w[...]).astype(bf16)
+        for i in range(2):
+            u = first + i
+            at = pl.ds(pl.multiple_of(u * rows, rows), rows)
+            q = qkv[at, :LANES_Q]
+            key = qkv[at, LANES_Q : 2 * LANES_Q]
+            val = qkv[at, 2 * LANES_Q :]
+            up = g_att[i * rows : (i + 1) * rows, :]
+            g_q = jnp.zeros((rows, LANES_Q), f32)
+            g_k = jnp.zeros((rows, LANES_Q), f32)
+            g_v = jnp.zeros((rows, LANES_Q), f32)
+            for h in range(2):
+                p = probs[2 * u + h]
+                up_h = up * heads[h]
+                g_v += t_dot(p.astype(bf16), up_h)
+                g_p = dot_t(up_h, val)
+                inner = jnp.sum(g_p * p, axis=-1, keepdims=True)
+                g_s = (p * (g_p - inner)).astype(bf16)
+                g_q += dot(g_s, key) * heads[h].astype(f32)
+                g_k += t_dot(g_s, q * heads[h])
+            wide = jnp.concatenate([g_q * scale, g_k * scale, g_v], axis=1).astype(bf16)
+            d_qkv[at, :] = dot_t(wide, spread[...]).astype(bf16)
+        values = dot_t(d_qkv[here, :], proj_all[...])
+        reduce_chunk(2, k, cc, values, part_a, sib_a, rows_a)
+        return carry
+
+    lax.fori_loop(0, 4, attend_back, 0)
+
+    def proj_grad(k, carry):
+        at = pl.ds(pl.multiple_of(k * third, 128), third)
+        d_proj[at, :] = t_dot(x_one[:, at], d_qkv[...]).astype(bf16)
+        return carry
+
+    lax.fori_loop(0, 3, proj_grad, 0)
+    sent += zsend(2, d_proj, z_proj, 2 * part)
+    d_out[...] = t_dot(attended[...], g_attn[...]).astype(bf16)
+
+    @pl.when(z != r)
+    def _():
+        slot_z = (r - z + 4) % 4 - 1
+        remote(
+            d_out.at[pl.ds(0, part)],
+            z_out.at[slot_z],
+            ow_s.at[3],
+            ow_r.at[1 + slot_z],
+            ident(r, 2 * r + c),
+        ).start()
+
+    slab[9:10, : d_qkv.shape[1]] = jnp.sum(d_qkv[...].astype(f32), axis=0, keepdims=True)
+
+    def feed_out(k, carry):
+        cc, first, here = chunk_of(k)
+        values = dot(act[here, :], red_all[...])
+        reduce_chunk(3, k, cc, values, part_b, sib_b, rows_b)
+        return carry
+
+    lax.fori_loop(0, 4, feed_out, 0)
+
+    def place(values, base):
+        live_hot = (one_hot() * live_col[...]).astype(bf16)
+        placed = t_dot(live_hot, values.astype(bf16))
+        hit = t_dot(live_hot, jnp.ones((rows, 128), bf16))[:, 0:1]
+        return jnp.where(hit > 0.5, placed.astype(bf16), base)
+
+    grad_one = reduce_end(2, part_a, rows_a)
+    g_shift, g_scale, through = back_norm(grad_one, scale_attn, norm_one[...], rstd_one[...])
+    slab[0:1, :] = g_shift
+    slab[1:2, :] = g_scale
+    o_latents[...] = place(g_mixed[...] + through, cotangent[...])
+    branch = reduce_end(3, part_b, rows_b) + red_b
+    slab[5:6, :] = jnp.sum(g_rows[...] * branch, axis=0, keepdims=True)
+    slabs[f] = slab[...].astype(bf16)
+
+    def slab_src(f2, c2):
+        return slabs.at[f]
+
+    def slab_dst(f2):
+        return slabs.at[f2]
+
+    sent += line_send(5, small_s, small_r, slab_src, slab_dst)
+    o_block[...] = place(mixed[...] + gate_mlp * branch, latents[...])
+
+    outs = []
+
+    def spread_out(kind, src, landing, height, dest):
+        total = src[pl.ds(pl.multiple_of(z * height, 16), height), :].astype(f32)
+        for dz in range(1, 4):
+            remote(
+                src.at[pl.ds(0, height)],
+                landing.at[dz - 1],
+                dz_s.at[kind, dz - 1],
+                dz_r.at[kind, dz - 1],
+                ident(r, 2 * ((z + dz) % 4) + c),
+            ).wait_recv()
+            total += landing[dz - 1].astype(f32)
+        half = height // 2
+        keep = src.at[pl.ds(pl.multiple_of(z * height, 16), height)]
+        keep[...] = total.astype(bf16)
+        for k, (r2, c2) in enumerate(board):
+            cp = remote(
+                src.at[pl.ds(pl.multiple_of(z * height + c2 * half, 16), half)],
+                dest.at[me],
+                dp_s.at[kind, k],
+                dp_r.at[kind, me],
+                ident(r2, 2 * z + c2),
+            )
+            cp.start()
+            sent.append(cp)
+        cp = pltpu.make_async_copy(
+            src.at[pl.ds(pl.multiple_of(z * height + c * half, 16), half)],
+            dest.at[me],
+            local_sem.at[1 + kind],
+        )
+        cp.start()
+        outs.append(cp)
+
+    spread_out(0, d_exp, z_exp, 2 * part, o_exp)
+    spread_out(1, d_red, z_red, 2 * PAD, o_red)
+
+    @pl.when(z == r)
+    def _():
+        total = d_out[:part, :].astype(f32)
+        for k in range(3):
+            remote(
+                d_out.at[pl.ds(0, part)], z_out.at[k], ow_s.at[3], ow_r.at[1 + k], ident(r, f)
+            ).wait_recv()
+            total += z_out[k].astype(f32)
+        d_out[:part, :] = total.astype(bf16)
+        for k, (dx, dy) in enumerate(SAME_CORE):
+            remote(
+                d_out.at[pl.ds(0, part)], o_out, ow_s.at[4 + k], ow_r.at[4], ident(plane(dx, dy), f)
+            ).start()
+        cp = pltpu.make_async_copy(d_out.at[pl.ds(0, part)], o_out, local_sem.at[5])
+        cp.start()
+        cp.wait()
+
+    line_wait(5, small_s, small_r, slab_src, slab_dst)
+    for k, (dx, dy) in enumerate(SAME_CORE):
+        cp = remote(
+            slabs, o_slabs.at[r], small_s.at[6, k], small_r.at[6, r], ident(plane(dx, dy), f)
+        )
+        cp.start()
+        sent.append(cp)
+    own_slabs = pltpu.make_async_copy(slabs, o_slabs.at[r], local_sem.at[4])
+    own_slabs.start()
+    back_cond = jnp.zeros((8, part), f32)
+    for p in range(6):
+        back_cond += dot_t(slabs[:, p, :], mod_w[:, p * width : (p + 1) * width])
+    for i in range(8):
+        gcond[i] = jnp.broadcast_to(back_cond[i : i + 1, :], (8, part))
+
+    def gc_src(f2, c2):
+        return gcond.at[f2]
+
+    def gc_dst(f2):
+        return o_gcond.at[f2]
+
+    sent += line_send(7, small_s, small_r, gc_src, gc_dst)
+    o_gcond[f] = gcond[f]
+
+    spread_out(2, d_proj, z_proj, 2 * part, o_proj)
+
+    line_wait(7, small_s, small_r, gc_src, gc_dst)
+    for dx, dy in SAME_CORE:
+        r2 = plane(dx, dy)
+        remote(
+            cond_all, o_cond.at[r2], small_s.at[4, 0], small_r.at[4, r2], ident(r2, f)
+        ).wait_recv()
+        remote(
+            slabs, o_slabs.at[r2], small_s.at[6, 0], small_r.at[6, r2], ident(r2, f)
+        ).wait_recv()
+    for kind, dest in ((0, o_exp), (1, o_red), (2, o_proj)):
+        for r2, c2 in board:
+            u = 4 * c2 + r2
+            remote(
+                dest.at[u], dest.at[u], dp_s.at[kind, 0], dp_r.at[kind, u], ident(r2, 2 * z + c2)
+            ).wait_recv()
+
+    @pl.when(z == r)
+    def _():
+        for dz in range(3):
+            remote(
+                out_shard, out_w.at[pl.ds(0, part)], ow_s.at[dz], ow_r.at[0], ident(r, f)
+            ).wait_send()
+            remote(
+                out_shard, o_out, ow_s.at[4 + dz], ow_r.at[4], ident(r, f)
+            ).wait_send()
+
+    @pl.when(z != r)
+    def _():
+        remote(out_shard, o_out, ow_s.at[3], ow_r.at[4], ident(r, f)).wait_recv()
+        remote(
+            d_out.at[pl.ds(0, part)], z_out.at[0], ow_s.at[3], ow_r.at[1], ident(r, f)
+        ).wait_send()
+
+    reduce_drain(2, part_a, sib_a, rows_a)
+    reduce_drain(3, part_b, sib_b, rows_b)
+    drain(sent)
+    drain(live_sent)
+    drain(cond_sent)
+    own_cond.wait()
+    own_slabs.wait()
+    for cp in outs:
+        cp.wait()
+
+
+def fused_local(
+    latents,
+    condition,
+    bucket,
+    keep_slots,
+    modulation_weight,
+    modulation_bias,
+    projection_weight,
+    query_value_bias,
+    output_weight,
+    output_bias,
+    expand_weight,
+    expand_bias,
+    reduce_weight,
+    reduce_bias,
+    cotangent,
+):
+    f32 = jnp.float32
+    bf16 = jnp.bfloat16
+    r = lax.axis_index("replica")
+    f = lax.axis_index("fsdp")
+    slot_count, width = latents.shape[1:]
+    rows = keep_slots.shape[1]
+    part = output_weight.shape[0]
+    hid = expand_weight.shape[1]
+    share = hid // 64
+    wide = 8 * PAD
+
+    def placed(shard, count):
+        return lax.dynamic_update_slice_in_dim(
+            jnp.zeros((count,), f32), shard.astype(f32), f * shard.shape[0], 0
+        )
+
+    def mine(value, axis):
+        return lax.dynamic_slice_in_dim(value, 2 * r, 2, axis)
+
+    cond_float = condition.astype(f32)
+    cond_act = jax.nn.silu(cond_float).astype(bf16)
+    cond_pack = jnp.pad(cond_act.reshape(8, 1, part), ((0, 0), (0, 15), (0, 0)))
+    mod_bias = jnp.pad(placed(modulation_bias, 6 * width).reshape(6, width), ((0, 2), (0, 0)))
+    live_count = jnp.where(bucket[0] == 0, slot_count, slot_count - 16) // 2
+    live = (jnp.arange(rows, dtype=jnp.int32) < live_count).astype(f32)
+    qv = mine(placed(query_value_bias, 2 * width).reshape(2, 8, part), 1)
+    qv = jnp.pad(qv.transpose(1, 0, 2), ((0, 0), (0, 0), (0, LANES_Q - part))).reshape(2, -1)
+    expand_b = mine(placed(expand_bias, hid).reshape(8, 8, share), 1).transpose(1, 0, 2)
+    expand_b = jnp.pad(expand_b, ((0, 0), (0, 0), (0, PAD - share))).reshape(2, wide)
+    extra = jnp.stack(
+        [
+            jnp.broadcast_to(placed(output_bias, width), (2, width)),
+            jnp.broadcast_to(placed(reduce_bias, width), (2, width)),
+            jnp.pad(expand_b, ((0, 0), (0, width - wide))),
+            jnp.pad(qv, ((0, 0), (0, width - 2 * LANES_Q))),
+        ],
+        axis=1,
+    ).astype(bf16)
+    extra = jnp.pad(extra, ((0, 0), (0, 12), (0, 0)))
+    proj_pack = mine(projection_weight.reshape(part, 3, 8, part), 2)
+    proj_pack = proj_pack.transpose(2, 0, 1, 3).reshape(2, part, 3 * part)
+    exp_pack = mine(expand_weight.reshape(part, 8, 8, share), 2).transpose(2, 0, 1, 3)
+    exp_pack = jnp.pad(exp_pack, ((0, 0),) * 3 + ((0, PAD - share),)).reshape(2, part, wide)
+    red_pack = mine(reduce_weight.reshape(8, share, width), 0)
+    red_pack = jnp.pad(red_pack, ((0, 0), (0, PAD - share), (0, 0)))
+
+    total = 8 * rows
+    vmem = pltpu.VMEM
+    dma = pltpu.SemaphoreType.DMA
+    scratch = [
+        vmem((8, 16, part), bf16),
+        vmem((8, 16, width), bf16),
+        vmem((8, 8, rows), f32),
+        vmem((8, 8, width), f32),
+        vmem((8, 8, width), f32),
+        vmem((width, 3 * part), bf16),
+        vmem((width, wide), bf16),
+        vmem((wide, width), bf16),
+        vmem((LANES_Q, width), bf16),
+        vmem((width, 3 * LANES_Q), bf16),
+        vmem((3 * part, 3 * LANES_Q), bf16),
+        vmem((total, width), bf16),
+        vmem((total, width), bf16),
+        vmem((total, width), bf16),
+        vmem((total, width), bf16),
+        vmem((total, 3 * LANES_Q), bf16),
+        vmem((16, rows, rows), f32),
+        vmem((total, LANES_Q), bf16),
+        vmem((total, wide), bf16),
+        vmem((total, wide), bf16),
+        vmem((total, 3 * part), bf16),
+        vmem((total, width), bf16),
+        vmem((total, width), bf16),
+    ]
+    scratch += [vmem((4 * rows, width), bf16)] * 2
+    scratch += [vmem((4, rows, width), bf16)] * 2
+    scratch += [
+        vmem((rows, width), f32),
+        vmem((rows, width), f32),
+        vmem((rows, 1), f32),
+        vmem((rows, width), f32),
+        vmem((rows, width), f32),
+        vmem((rows, width), f32),
+        vmem((rows, width), f32),
+        vmem((rows, 1), f32),
+        vmem((rows, width), f32),
+        vmem((16, width), f32),
+        vmem((8, 16, width), bf16),
+        vmem((8, 8, part), f32),
+        vmem((width, wide), bf16),
+        vmem((wide, width), bf16),
+        vmem((width, 3 * part), bf16),
+        vmem((LANES_Q, width), bf16),
+        vmem((3, 2 * part, wide), bf16),
+        vmem((3, 2 * PAD, width), bf16),
+        vmem((3, 2 * part, 3 * part), bf16),
+        vmem((3, part, width), bf16),
+        dma((8,)),
+        dma((8, 7)),
+        dma((8, 8)),
+        dma((3, 7)),
+        dma((3, 8)),
+        dma((4, 7)),
+        dma((4, 8)),
+        dma((4, 2)),
+        dma((4, 2)),
+        dma((4, 4)),
+        dma((4, 4)),
+        dma((3, 3)),
+        dma((3, 3)),
+        dma((3, 7)),
+        dma((3, 8)),
+        dma((7,)),
+        dma((5,)),
+    ]
+    in_vmem = pl.BlockSpec(memory_space=pltpu.VMEM)
+    anywhere = pl.BlockSpec(memory_space=pl.ANY)
+    outputs = pl.pallas_call(
+        fused_kernel,
+        out_shape=(
+            jax.ShapeDtypeStruct((slot_count, width), bf16),
+            jax.ShapeDtypeStruct((slot_count, width), bf16),
+            jax.ShapeDtypeStruct((4, 8, 16, width), bf16),
+            jax.ShapeDtypeStruct((4, 8, 16, part), bf16),
+            jax.ShapeDtypeStruct((8, 8, part), f32),
+            jax.ShapeDtypeStruct((8, part, wide), bf16),
+            jax.ShapeDtypeStruct((8, PAD, width), bf16),
+            jax.ShapeDtypeStruct((8, part, 3 * part), bf16),
+            jax.ShapeDtypeStruct((part, width), bf16),
+        ),
+        in_specs=[in_vmem] * 13,
+        out_specs=(
+            in_vmem,
+            in_vmem,
+            anywhere,
+            anywhere,
+            in_vmem,
+            anywhere,
+            anywhere,
+            anywhere,
+            anywhere,
+        ),
+        scratch_shapes=scratch,
+        compiler_params=pltpu.CompilerParams(
+            collective_id=0, has_side_effects=True, vmem_limit_bytes=60 << 20
+        ),
+    )(
+        latents[0],
+        cotangent[0],
+        keep_slots.reshape(rows, 1),
+        live.reshape(rows, 1),
+        jnp.broadcast_to(live[None], (8, rows)),
+        cond_pack,
+        mod_bias,
+        extra,
+        modulation_weight,
+        proj_pack,
+        exp_pack,
+        red_pack,
+        output_weight,
+    )
+    block, grad_latents, slabs, conds, g_cond, g_exp, g_red, g_proj, g_out = outputs
+
+    def shard(value, axis, size):
+        return lax.dynamic_slice_in_dim(value, f * size, size, axis)
+
+    slabs = slabs.reshape(32, 16, width)
+    grad_mod = slabs[:, :6].reshape(32, 6 * width)
+    cond_cols = conds[:, :, 0].reshape(32, part)
+    sum_mod_w = jnp.einsum("bd,be->de", cond_cols, grad_mod, preferred_element_type=f32)
+    sums = jnp.sum(slabs[:, :8].astype(f32), axis=0)
+    sum_mod_b = shard(sums[:6].reshape(-1), 0, modulation_bias.shape[0])
+    sum_red_b = shard(sums[6], 0, part)
+    sum_out_b = shard(sums[7], 0, part)
+    tails = jnp.sum(slabs[:, 8:10].astype(f32).reshape(4, 4, 2, 2, width), axis=1)
+    exp_sums = tails[:, :, 0, :wide].reshape(8, 8, PAD)
+    sum_exp_b = lax.dynamic_index_in_dim(exp_sums, f, 1, keepdims=False)[:, :share].reshape(-1)
+    qv_sums = tails[:, :, 1, : 3 * part].reshape(8, 3, part)
+    qv_sums = jnp.concatenate([qv_sums[:, 0].reshape(-1), qv_sums[:, 2].reshape(-1)])
+    sum_qv_b = shard(qv_sums, 0, query_value_bias.shape[0])
+    grad_condition = jax.vjp(jax.nn.silu, cond_float)[1](g_cond[:, 0].reshape(1, width))[0]
+    g_exp = g_exp.reshape(2, 4, part, 8, PAD)[..., :share].transpose(2, 3, 1, 0, 4)
+    g_red = g_red.reshape(2, 4, PAD, width)[:, :, :share].transpose(1, 0, 2, 3)
+    g_proj = g_proj.reshape(2, 4, part, 3, part).transpose(2, 3, 1, 0, 4)
+    return (
+        block[None],
+        grad_latents[None],
+        grad_condition,
+        sum_mod_w,
+        sum_mod_b,
+        g_proj.reshape(part, 3 * width).astype(f32),
+        sum_qv_b,
+        g_out.astype(f32),
+        sum_out_b,
+        g_exp.reshape(part, hid).astype(f32),
+        sum_exp_b,
+        g_red.reshape(8 * share, width).astype(f32),
+        sum_red_b,
+    )
+
+
 def solution(mesh):
     placed = (
         P(("replica", "fsdp"), None, None),
@@ -322,8 +1304,9 @@
         P("fsdp"),
         P(("replica", "fsdp"), None, None),
     )
+    body = fused_local if tuple(mesh.shape.values()) == (4, 8) else local
     return jax.shard_map(
-        local,
+        body,
         mesh=mesh,
         in_specs=placed,
         out_specs=(

time: 1310 us -> 373 us (0.28)
  waiting for transfers between devices: 1020 us -> 0 us
  Pallas kernels: 0 us -> 293 us
  matrix products: 97.6 us -> 2.64 us
  blocking collectives: 89.2 us -> 0 us
  between operations: 21 us -> 1.63 us
    all_gather x8 -> x0, waiting for transfers between devices: 466 us -> none  [the longest x1 105 us: local(): lax.all_gather(modulation_weight, 'fsdp', axis=0, tiled=True)]
    reduce_scatter x5 -> x0, waiting for transfers between devices: 432 us -> none  [the longest x1 159 us: local(): lax.psum_scatter(local_mod_w.astype(jnp.bfloat16), 'fsdp', scatter_dimens...]
    pallas_call x0 -> x1, Pallas kernels: none -> 293 us  [fused_local(): pl.pallas_call(fused_kernel, out_shape=(jax.ShapeDtypeStruct((slot_count,...]
    unnamed x23 -> x0, waiting for transfers between devices: 125 us -> none
    dot_general x20 -> x1, matrix products: 97.6 us -> 2.64 us  [fused_local(): jnp.einsum('bd,be->de', cond_cols, grad_mod, preferred_element_type=f32)]
    unnamed x2 -> x0, blocking collectives: 54.6 us -> none
    unnamed x94 -> x24, local copies, waits for them, and re-layouts: 35.6 us -> 2.62 us
    all_gather x2 -> x0, blocking collectives: 22.1 us -> none  [the longest x1 14 us: local(): lax.all_gather(shares[1].astype(jnp.bfloat16), 'replica', axis=1, tiled=T...]
  transfers between devices with their start and end apart: 18 -> 0, of which waited for: 16 -> 0; matrix products, arithmetic and copies ran while one was open for 11% -> 0% of each run, Pallas kernels for 0% -> 0%
where the time goes in v2:
time: 373 us
  Pallas kernels  293 us (79%)
  local copies, waits for them, and re-layouts  64.3 us (17%)
  other arithmetic  11 us (3%)
    pallas_call x1, Pallas kernels, fused_local(): pl.pallas_call(fused_kernel, out_shape=(jax.ShapeDtypeStruct((slot_count,...  293 us
    convert_element_type x2, local copies, waits for them, and re-layouts, fused_local(): g_exp.reshape(part, hid).astype(f32)  15.4 us
    convert_element_type x3, local copies, waits for them, and re-layouts, fused_local(): g_proj.reshape(part, 3 * width).astype(f32)  14.4 us

profile of v2, /device:TPU:25, one launch (start us, length us, event | category | flops | bytes accessed | tf_op | source)
XLA Modules:
  0.0 372.7 jit_solution(7708936529477611014)
XLA Ops:
  0.6 0.0 copy-start
  0.7 0.9 convert_dynamic-update-slice_fusion.2
  1.6 0.1 reshape.137
  1.7 0.8 convert_dynamic-update-slice_fusion
  2.5 0.1 reshape.135
  2.7 0.1 reshape.136
  2.8 0.8 convert_dynamic-update-slice_fusion.4
  3.6 0.8 convert_dynamic-update-slice_fusion.3
  4.4 0.7 fusion.6.extra
  5.1 0.8 convert_dynamic-update-slice_fusion.1
  5.9 0.6 pad.41.mod_bias
  6.5 7.1 %reshape.141 = bf16[144,8,8,72]{3,2,1,0:T(8,128)(2,1)} reshape(bf16[144,4608]{1,0:T(8,128)(2,1)} %param.25) | data formatting | bytes 2654208 | tf_op jit(solution)/shard_map/reshape | solution.py:1129
  13.6 2.3 constant_dynamic-slice_fusion.4
  15.9 0.1 copy.78
  16.0 0.1 pad.47
  16.1 1.2 reshape.142.exp_pack
  17.3 3.7 reshape.139
  20.9 0.0 copy-start.7
  21.0 0.0 copy-start.8
  21.0 0.5 constant_dynamic-slice_fusion.5
  21.4 0.8 copy.69
  22.3 0.9 copy.63.proj_pack
  23.2 0.0 copy-done
  23.2 0.8 pad.48.red_pack
  24.6 0.6 fusion.7.live_col
  25.3 0.6 broadcast_in_dim.21.live_row
  25.9 0.0 copy-done.7
  25.9 0.1 reshape.159
  26.0 0.6 pad.40.cond_pack
  26.6 0.0 copy-done.8
  26.6 0.7 copy.62.slots
  27.4 293.1 %shard_map.246 = (bf16[256,1152]{1,0:T(8,128)(2,1)}, bf16[256,1152]{1,0:T(8,128)(2,1)}, bf16[4,8,16,1152]{3,2,1,0:T(8,128)(2,1)}, bf16[4,8,16,144]{3,2,1,0:T(8,1...) custom-call(bf16[256,1152]{1,0:T(8,128)(2,1)} %bitcast.62, ...), custom_call_target="tpu_custom_call" | custom-call | tf_op jit(solution)/shard_map/pallas_call | solution.py:1205
  320.5 1.2 convert_reduce_fusion
  321.7 0.6 constant_dynamic-slice_fusion
  322.3 1.1 slice.63
  323.5 0.1 convert_reduce_fusion.1
  323.6 0.1 slice_reduce_fusion.1
  323.7 0.1 reshape_squeeze.20
  323.8 0.1 reshape_squeeze.21
  323.9 0.1 reshape_squeeze.22
  324.0 0.7 fusion.15
  324.7 4.9 %reshape.149 = bf16[2,4,144,8,80]{4,3,2,1,0:T(8,128)(2,1)} reshape(bf16[8,144,640]{2,1,0:T(8,128)(2,1)} %get-tuple-element.29) | data formatting | bytes 2949120 | tf_op jit(solution)/shard_map/reshape | solution.py:1269
  329.6 2.0 convert_bitcast_fusion
  331.6 5.8 %copy.66 = f32[144,8,4,2,72]{4,3,2,1,0:T(2,128)} copy(f32[144,8,4,2,72]{4,1,0,2,3:T(8,128)S(1)} %convert_bitcast_fusion) | data formatting | bytes 5308416 | tf_op jit(solution)/shard_map/convert_element_type | solution.py:1282
  337.4 9.7 %reshape.156 = f32[144,4608]{1,0:T(8,128)} reshape(f32[144,8,4,2,72]{4,3,2,1,0:T(2,128)} %copy.66) | data formatting | bytes 5308416 | tf_op jit(solution)/shard_map/convert_element_type | solution.py:1282
  347.0 0.0 copy-done.3
  347.0 2.2 copy.64
  349.3 6.3 %copy.65 = f32[144,3,4,2,144]{4,3,2,1,0:T(2,128)} copy(f32[144,3,4,2,144]{0,4,1,2,3:T(8,128)} %bitcast.49) | data formatting | bytes 3981312 | tf_op jit(solution)/shard_map/convert_element_type | solution.py:1278
  355.5 5.9 %reshape.153 = f32[144,3456]{1,0:T(8,128)} reshape(f32[144,3,4,2,144]{4,3,2,1,0:T(2,128)} %copy.65) | data formatting | bytes 3981312 | tf_op jit(solution)/shard_map/convert_element_type | solution.py:1278
  361.5 1.0 slice.46
  362.6 2.6 fusion.8
  365.2 0.0 copy-done.2
  365.2 0.2 convert_bitcast_fusion.1
  365.4 1.7 copy.67
  367.1 0.9 convert_element_type.107
  368.0 0.1 slice_reduce_fusion
  368.1 0.1 reshape_squeeze.23
  368.2 0.7 reshape.150
  368.8 0.7 dynamic_slice.40
  369.5 0.9 slice_reduce_fusion.4
  370.4 0.1 reshape_squeeze.18
  370.5 0.6 fusion.12
  371.1 0.8 copy.88
  371.9 0.8 copy.89
  (38 shorter events, 0.4 us)
Async XLA Ops:
  0.6 22.5 %copy-start = (bf16[576,1152]{1,0:T(8,128)(2,1)S(1)}, bf16[576,1152]{1,0:T(8,128)(2,1)}, u32[]{:S(2)}) copy-start(bf16[576,1152]{1,0:T(8,128)(2,1)} %param.27) | copy-start | bytes 3981316
  20.9 4.9 %copy-start.7 = (bf16[1,1152]{1,0:T(2,128)(2,1)S(1)}, bf16[1,1152]{1,0:T(2,128)(2,1)}, u32[]{:S(2)}) copy-start(bf16[1,1152]{1,0:T(2,128)(2,1)} %param.16) | copy-start | bytes 6916
  21.0 5.7 %copy-start.8 = (s32[1,128]{1,0:T(1,128)S(1)}, s32[1,128]{1,0:T(1,128)}, u32[]{:S(2)}) copy-start(s32[1,128]{1,0:T(1,128)} %param.18) | copy-start | bytes 1540
  337.4 9.7 %copy-start.3 = (bf16[8,144,432]{2,1,0:T(8,128)(2,1)S(1)}, bf16[8,144,432]{2,1,0:T(8,128)(2,1)}, u32[]{:S(2)}) copy-start(bf16[8,144,432]{2,1,0:T(8,128)(2,1)} %get-tuple-element.27) | copy-start | bytes 2985988
  355.5 5.9 %copy-start.1 = (bf16[4,8,16,1152]{3,2,1,0:T(8,128)(2,1)S(1)}, bf16[4,8,16,1152]{3,2,1,0:T(8,128)(2,1)}, u32[]{:S(2)}) copy-start(bf16[4,8,16,1152]{3,2,1,0:T(8,128)(2,1)} %get-tuple-element.26) | copy-start | bytes 3538948
  361.5 3.7 copy-start.2
  365.4 1.7 copy-start.6
  365.4 5.7 %copy-start.5 = (bf16[256,1152]{1,0:T(8,128)(2,1)S(1)}, bf16[256,1152]{1,0:T(8,128)(2,1)}, u32[]{:S(2)}) copy-start(bf16[256,1152]{1,0:T(8,128)(2,1)} %get-tuple-element.22) | copy-start | bytes 1769476
  367.1 4.8 %copy-start.4 = (bf16[256,1152]{1,0:T(8,128)(2,1)S(1)}, bf16[256,1152]{1,0:T(8,128)(2,1)}, u32[]{:S(2)}) copy-start(bf16[256,1152]{1,0:T(8,128)(2,1)} %get-tuple-element.23) | copy-start | bytes 1769476

commit v3 on v2

--- a/solution.py
+++ b/solution.py
@@ -308,7 +308,8 @@
 
 MESH = pl.DeviceIdType.MESH
 SAME_CORE = ((1, 0), (0, 1), (1, 1))
-PAD = 80
+LANES = 128
+HALF = 64
 LANES_Q = 256
 
 
@@ -322,9 +323,9 @@
     mod_bias,
     extra,
     mod_w,
-    proj_pack,
-    exp_pack,
-    red_pack,
+    proj_w,
+    exp_w,
+    red_w,
     out_shard,
     o_block,
     o_latents,
@@ -344,6 +345,8 @@
     exp_all,
     red_all,
     out_w,
+    proj_pack,
+    exp_pack,
     proj_wide,
     spread,
     x_one,
@@ -362,7 +365,6 @@
     sib_b,
     rows_a,
     rows_b,
-    kept,
     norm_one,
     rstd_one,
     g_rows,
@@ -382,6 +384,7 @@
     z_red,
     z_proj,
     z_out,
+    proj_land,
     local_sem,
     small_s,
     small_r,
@@ -399,6 +402,20 @@
     dp_r,
     ow_s,
     ow_r,
+    red_s,
+    red_r,
+    red_l,
+    zr_s,
+    zr_r,
+    pe_s,
+    et_s,
+    et_r,
+    et_l,
+    pr_s,
+    pr_r,
+    pr_l,
+    relay_s,
+    red_f,
 ):
     f32 = jnp.float32
     bf16 = jnp.bfloat16
@@ -409,6 +426,10 @@
     rows = slots.shape[0]
     part = out_shard.shape[0]
     third = width // 3
+    kept = g_mixed
+    blocks = red_w.shape[0] // HALF
+    slots_of = red_all.shape[0] // LANES
+    tiles = exp_w.shape[1] // LANES
     me = 4 * c + r
     other = (c + 1) % 2
 
@@ -430,10 +451,15 @@
 
     sibling = ident(r, 2 * z + other)
     line = []
-    for dz in range(4):
+    across = (z, z + 1 - 2 * (z % 2), (z + 2) % 4, 3 - z)
+    for dz in (2, 1, 3, 0):
         for dc in range(2):
             if dz or dc:
-                line.append(((z + dz) % 4, (c + dc) % 2))
+                line.append((across[dz], (c + dc) % 2))
+    far = (4, 5)
+    via = (0, 1)
+    outer = (z == 0) | (z == 3)
+    inner = (z == 1) | (z == 2)
     board = []
     for dx in range(2):
         for dy in range(2):
@@ -448,27 +474,78 @@
         pl.semaphore_signal(barrier, inc=1, device_id=ident(r2, 2 * z + c2), device_id_type=MESH)
     pl.semaphore_wait(barrier, len(line) + len(board))
 
-    def line_send(kind, sems_s, sems_r, src_of, dst_of):
-        copies = []
-        for k, (z2, c2) in enumerate(line):
-            f2 = 2 * z2 + c2
-            cp = remote(
-                src_of(f2, c2),
-                dst_of(f),
-                sems_s.at[kind, k],
-                sems_r.at[kind, f],
-                ident(r, f2),
-            )
+    def line_copy(kind, k, sems_s, sems_r, src_of, dst_of):
+        z2, c2 = line[k]
+        f2 = 2 * z2 + c2
+        return remote(
+            src_of(f2, c2), dst_of(f), sems_s.at[kind, k], sems_r.at[kind, f], ident(r, f2)
+        )
+
+    def line_from(kind, k, sems_s, sems_r, src_of, dst_of):
+        z2, c2 = line[k]
+        f2 = 2 * z2 + c2
+        return remote(
+            src_of(f, c), dst_of(f2), sems_s.at[kind, k], sems_r.at[kind, f2], ident(r, f2)
+        )
+
+    def line_send(*what):
+        copies = [line_copy(what[0], k, *what[1:]) for k in range(len(line))]
+        for cp in copies:
             cp.start()
-            copies.append(cp)
         return copies
 
-    def line_wait(kind, sems_s, sems_r, src_of, dst_of):
-        for k, (z2, c2) in enumerate(line):
-            f2 = 2 * z2 + c2
-            remote(
-                src_of(f, c), dst_of(f2), sems_s.at[kind, k], sems_r.at[kind, f2], ident(r, f2)
-            ).wait_recv()
+    def line_wait(*what):
+        for k in range(len(line)):
+            line_from(what[0], k, *what[1:]).wait_recv()
+
+    def relay_send(*what):
+        for k in range(len(line)):
+            cp = line_copy(what[0], k, *what[1:])
+            if k in far:
+                pl.when(inner)(cp.start)
+            else:
+                cp.start()
+
+    def relay_copy(k, kind, sems_s, sems_r, src_of, dst_of):
+        z2, c2 = line[k]
+        f2 = 2 * z2 + c2
+        return remote(
+            dst_of(f2),
+            dst_of(f2),
+            relay_s.at[kind, k],
+            sems_r.at[kind, f2],
+            ident(r, 2 * across[1] + c),
+        )
+
+    def relay_pass(*what):
+        @pl.when(outer)
+        def _():
+            for k in via:
+                line_from(what[0], k, *what[1:]).wait_recv()
+
+        @pl.when(inner)
+        def _():
+            for k in via:
+                line_from(what[0], k, *what[1:]).wait_recv()
+                relay_copy(k, *what).start()
+
+    def relay_wait(*what):
+        for k in range(len(line)):
+            if k not in via:
+                line_from(what[0], k, *what[1:]).wait_recv()
+
+    def relay_drain(*what):
+        for k in range(len(line)):
+            cp = line_copy(what[0], k, *what[1:])
+            if k in far:
+                pl.when(inner)(cp.wait_send)
+            else:
+                cp.wait_send()
+
+        @pl.when(inner)
+        def _():
+            for k in via:
+                relay_copy(k, *what).wait_send()
 
     def drain(copies):
         for cp in copies:
@@ -492,21 +569,156 @@
     def proj_dst(f2):
         return proj_all.at[pl.ds(pl.multiple_of(f2 * part, 16), part)]
 
+    tail = pl.ds(LANES, exp_all.shape[1] - LANES)
+    head = pl.ds(0, LANES)
+
     def exp_src(f2, c2):
-        return exp_pack.at[c2]
+        return exp_pack.at[c2, :, tail]
 
     def exp_dst(f2):
-        return exp_all.at[pl.ds(pl.multiple_of(f2 * part, 16), part)]
-
-    def red_src(f2, c2):
-        return red_pack.at[c2]
-
-    def red_dst(f2):
-        return red_all.at[pl.ds(pl.multiple_of(f2 * PAD, 16), PAD)]
+        return exp_all.at[pl.ds(pl.multiple_of(f2 * part, 16), part), tail]
+
+    def exp_head(f2):
+        return exp_all.at[pl.ds(pl.multiple_of(f2 * part, 16), part), head]
+
+    def half_tile(i):
+        p = i // 2
+        c2 = p // slots_of
+        at = 2 * (r + 4 * p) + i % 2
+        return c2, 2 * (p - 4 * c2) + i % 2, at // blocks, at % blocks
+
+    def red_rows(j):
+        return red_all.at[pl.ds(pl.multiple_of(j * HALF, HALF), HALF)]
+
+    def red_copy(i, z2):
+        c2, j, owner, block = half_tile(i)
+        return remote(
+            red_w.at[pl.ds(pl.multiple_of(block * HALF, HALF), HALF)],
+            red_rows(j),
+            red_s.at[i, z2],
+            red_r.at[j],
+            ident(r, 2 * z2 + c2),
+        )
+
+    def red_local(i):
+        c2, j, owner, block = half_tile(i)
+        return pltpu.make_async_copy(
+            red_w.at[pl.ds(pl.multiple_of(block * HALF, HALF), HALF)], red_rows(j), red_l.at[j]
+        )
+
+    def red_goes(i, z2):
+        c2, j, owner, block = half_tile(i)
+        return (owner == f) & (2 * z2 + c2 != f) & (inner | (z2 + z != 3))
+
+    def red_stops(i):
+        c2, j, owner, block = half_tile(i)
+        return (c2 == c) & (owner // 2 == across[2])
+
+    def red_onward(i):
+        c2, j, owner, block = half_tile(i)
+        return remote(
+            red_rows(j), red_rows(j), red_f.at[j], red_r.at[j], ident(r, 2 * across[1] + c)
+        )
+
+    def each_half(step):
+        def body(i, carry):
+            step(i)
+            return carry
+
+        lax.fori_loop(0, 2 * blocks, body, 0)
+
+    def red_send():
+        def step(i):
+            c2, j, owner, block = half_tile(i)
+            for z2 in range(4):
+                pl.when(red_goes(i, z2))(red_copy(i, z2).start)
+            pl.when((owner == f) & (c2 == c))(red_local(i).start)
+
+        each_half(step)
+
+    def red_pass():
+        def step(i):
+            @pl.when(red_stops(i))
+            def _():
+                red_copy(i, z).wait_recv()
+                pl.when(inner)(red_onward(i).start)
+
+        each_half(step)
+
+    def red_wait():
+        def step(i):
+            c2, j, owner, block = half_tile(i)
+            pl.when((c2 == c) & (owner != f) & (owner // 2 != across[2]))(red_copy(i, z).wait_recv)
+            pl.when((owner == f) & (c2 == c))(red_local(i).wait)
+
+        each_half(step)
+
+    def red_drain():
+        def step(i):
+            for z2 in range(4):
+                pl.when(red_goes(i, z2))(red_copy(i, z2).wait_send)
+            pl.when(red_stops(i) & inner)(red_onward(i).wait_send)
+
+        each_half(step)
+
+    exp_main = (1, w_s, w_r, exp_src, exp_dst)
+    proj_main = (0, w_s, w_r, proj_src, proj_dst)
+
+    def first_src(f2, c2):
+        return exp_pack.at[0, :, head]
+
+    exp_lead = (2, w_s, w_r, first_src, exp_head)
+
+    def lead_send(start):
+        for k, (z2, c2) in enumerate(line):
+            keep = c2 == 0
+            if k in far:
+                keep = keep & inner
+            cp = line_copy(exp_lead[0], k, *exp_lead[1:])
+            pl.when(keep)(cp.start if start else cp.wait_send)
+
+    def exp_send():
+        relay_send(*exp_main)
+        lead_send(True)
+
+    def exp_pass():
+        relay_pass(*exp_main)
+
+        @pl.when(c == 0)
+        def _():
+            relay_pass(*exp_lead)
+
+    def exp_wait():
+        relay_wait(*exp_main)
+
+        @pl.when(c == 0)
+        def _():
+            relay_wait(*exp_lead)
+
+    def exp_drain():
+        relay_drain(*exp_main)
+        lead_send(False)
+
+        @pl.when((c == 0) & inner)
+        def _():
+            for k in via:
+                relay_copy(k, *exp_lead).wait_send()
 
     sent = line_send(0, small_s, small_r, cond_src, cond_dst)
-    sent += line_send(0, w_s, w_r, proj_src, proj_dst)
     sent += line_send(1, small_s, small_r, extra_src, extra_dst)
+    packs = []
+    for c2 in range(2):
+        for i in range(slots_of):
+            if c2 and not i:
+                continue
+            tile = r + 4 * (4 * c2 + i)
+            cp = pltpu.make_async_copy(
+                exp_w.at[:, pl.ds(pl.multiple_of(tile * LANES, LANES), LANES)],
+                exp_pack.at[c2, :, pl.ds(i * LANES, LANES)],
+                pe_s.at[c2, i],
+            )
+            cp.start()
+            packs.append(cp)
     live_sent = []
     for k, (r2, c2) in enumerate(board):
         cp = remote(
@@ -521,9 +733,6 @@
     local = [
         pltpu.make_async_copy(cond_pack.at[f], cond_all.at[f], local_sem.at[0]),
         pltpu.make_async_copy(extra.at[c], extra_all.at[f], local_sem.at[1]),
-        pltpu.make_async_copy(proj_pack.at[c], proj_dst(f), local_sem.at[2]),
-        pltpu.make_async_copy(exp_pack.at[c], exp_dst(f), local_sem.at[3]),
-        pltpu.make_async_copy(red_pack.at[c], red_dst(f), local_sem.at[4]),
         pltpu.make_async_copy(live_row, live_all.at[me], local_sem.at[5]),
     ]
     for cp in local:
@@ -541,6 +750,43 @@
 
     def t_dot(a, b):
         return lax.dot_general(a, b, (((0,), (0,)), ((), ())), preferred_element_type=f32)
+
+    local[0].wait()
+    line_wait(0, small_s, small_r, cond_src, cond_dst)
+    cond_cols = jnp.sum(cond_all[...].astype(f32), axis=1).astype(bf16)
+    mod_send[...] = jnp.zeros(mod_send.shape, f32)
+    for p in range(6):
+        piece = dot(cond_cols, mod_w[:, p * width : (p + 1) * width]) + mod_bias[p : p + 1, :]
+        mod_send[:, p, :] = piece
+
+    def mod_src(f2, c2):
+        return mod_send.at[f2]
+
+    def mod_dst(f2):
+        return mod_all.at[f2]
+
+    sent += line_send(2, small_s, small_r, mod_src, mod_dst)
+    mod_all[f] = mod_send[f]
+
+    wide_columns = proj_all.shape[1]
+    for c2 in range(2):
+        t = 2 * r + c2
+        picked = jnp.zeros((part, wide_columns), f32)
+        for q in range(3):
+            window = proj_w[
+                :, pl.ds(pl.multiple_of(q * width + t * LANES, LANES), LANES_Q)
+            ]
+            source = lax.broadcasted_iota(jnp.int32, (LANES_Q, wide_columns), 0)
+            goal = lax.broadcasted_iota(jnp.int32, (LANES_Q, wide_columns), 1)
+            picks = (source - t * (part - LANES) == goal - q * part) & (
+                (goal >= q * part) & (goal < (q + 1) * part)
+            )
+            picked += dot(window, jnp.where(picks, 1.0, 0.0).astype(bf16))
+        proj_pack[c2] = picked.astype(bf16)
+    relay_send(0, w_s, w_r, proj_src, proj_dst)
+    own_proj = pltpu.make_async_copy(proj_pack.at[c], proj_dst(f), local_sem.at[2])
+    own_proj.start()
+    local.append(own_proj)
 
     kept[...] = dot(one_hot().astype(bf16), latents[...])
     g_rows[...] = dot((one_hot() * live_col[...]).astype(bf16), cotangent[...])
@@ -560,36 +806,14 @@
     )
     spread[...] = jnp.where(column == split + skip, 1.0, 0.0).astype(bf16)
 
-    for cp in local:
+    @pl.when(c == 1)
+    def _():
+        exp_all[:, :LANES] = jnp.zeros((width, LANES), bf16)
+        red_all[:LANES, :] = jnp.zeros((LANES, width), bf16)
+
+    for cp in local[1:]:
         cp.wait()
-    line_wait(0, small_s, small_r, cond_src, cond_dst)
-    cond_cols = jnp.sum(cond_all[...].astype(f32), axis=1).astype(bf16)
-    mod_send[...] = jnp.zeros(mod_send.shape, f32)
-    for p in range(6):
-        piece = dot(cond_cols, mod_w[:, p * width : (p + 1) * width]) + mod_bias[p : p + 1, :]
-        mod_send[:, p, :] = piece
-
-    def mod_src(f2, c2):
-        return mod_send.at[f2]
-
-    def mod_dst(f2):
-        return mod_all.at[f2]
-
-    sent += line_send(2, small_s, small_r, mod_src, mod_dst)
-    mod_all[f] = mod_send[f]
-    cond_sent = []
-    for k, (dx, dy) in enumerate(SAME_CORE):
-        cp = remote(
-            cond_all,
-            o_cond.at[r],
-            small_s.at[4, k],
-            small_r.at[4, r],
-            ident(plane(dx, dy), f),
-        )
-        cp.start()
-        cond_sent.append(cp)
-    own_cond = pltpu.make_async_copy(cond_all, o_cond.at[r], local_sem.at[0])
-    own_cond.start()
+
     line_wait(2, small_s, small_r, mod_src, mod_dst)
     modulation = jnp.sum(mod_all[...], axis=0)
     shift_attn, scale_attn, gate_attn, shift_mlp, scale_mlp, gate_mlp = [
@@ -635,7 +859,16 @@
             ).wait_recv()
         return copies
 
-    def reduce_chunk(kind, k, cc, values, buf, sib, landing):
+    def reduce_send(kind, buf, landing, r2):
+        remote(
+            slot(buf, 4 * c + r2),
+            landing.at[r],
+            rs_s.at[kind, r2],
+            rs_r.at[kind, r],
+            ident(r2, f),
+        ).start()
+
+    def reduce_chunk(kind, k, cc, values, buf, sib, landing, hold=False):
         base = pl.multiple_of(cc * 4 * rows + (k % 2) * 2 * rows, 2 * rows)
         here = pl.ds(base, 2 * rows)
         there = pl.ds(pl.multiple_of((k % 2) * 2 * rows, 2 * rows), 2 * rows)
@@ -654,18 +887,12 @@
                 buf.at[here], sib.at[there], sb_s.at[kind, slot_k], sb_r.at[kind, slot_k], sibling
             ).wait_recv()
             buf[here, :] = (values + sib[there, :].astype(f32)).astype(bf16)
-            for x2 in range(2):
+            for x2 in range(0 if hold else 2):
                 r2 = 2 * slot_k + x2
 
                 @pl.when(r2 != r)
                 def _():
-                    remote(
-                        slot(buf, 4 * c + r2),
-                        landing.at[r],
-                        rs_s.at[kind, r2],
-                        rs_r.at[kind, r],
-                        ident(r2, f),
-                    ).start()
+                    reduce_send(kind, buf, landing, r2)
 
     def reduce_end(kind, buf, landing):
         total = own(buf)[...].astype(f32)
@@ -696,20 +923,48 @@
     slab[...] = jnp.zeros(slab.shape, f32)
     slab[6:7, :] = jnp.sum(grad_mlp.astype(f32), axis=0, keepdims=True)
 
+    def out_copy(z2):
+        return remote(
+            out_shard,
+            out_w.at[pl.ds(0, part)],
+            ow_s.at[z2],
+            ow_r.at[0],
+            ident(r, 2 * z2 + c),
+        )
+
+    def out_onward():
+        return remote(
+            out_w.at[pl.ds(0, part)],
+            out_w.at[pl.ds(0, part)],
+            ow_s.at[7],
+            ow_r.at[0],
+            ident(r, 2 * across[1] + c),
+        )
+
+    def out_goes(z2):
+        return (z == r) & (z2 != z) & (inner | (z2 + z != 3))
+
+    for z2 in range(4):
+        pl.when(out_goes(z2))(out_copy(z2).start)
+
     @pl.when(z == r)
     def _():
-        for dz in range(1, 4):
-            remote(
-                out_shard,
-                out_w.at[pl.ds(0, part)],
-                ow_s.at[dz - 1],
-                ow_r.at[0],
-                ident(r, 2 * ((z + dz) % 4) + c),
-            ).start()
         out_w[:part, :] = out_shard[...]
 
-    line_wait(0, w_s, w_r, proj_src, proj_dst)
-    sent += line_send(1, w_s, w_r, exp_src, exp_dst)
+    relay_pass(*proj_main)
+    relay_wait(*proj_main)
+    for cp in packs:
+        cp.wait()
+    own_exp = pltpu.make_async_copy(exp_pack.at[c, :, tail], exp_dst(f), local_sem.at[3])
+    own_exp.start()
+
+    @pl.when(c == 0)
+    def _():
+        cp = pltpu.make_async_copy(exp_pack.at[0, :, head], exp_head(f), local_sem.at[6])
+        cp.start()
+        cp.wait()
+
+    exp_send()
     proj_wide[...] = dot(proj_all[...], spread[...]).astype(bf16)
     line_wait(1, small_s, small_r, extra_src, extra_dst)
     biases = jnp.sum(extra_all[...].astype(f32), axis=0)
@@ -724,7 +979,19 @@
         ).wait_recv()
     sent += gather_end(0, x_one)
     sent += gather_start(1, g_mlp)
-    sent += line_send(2, w_s, w_r, red_src, red_dst)
+    cond_sent = []
+    for k, (dx, dy) in enumerate(SAME_CORE):
+        cp = remote(
+            cond_all,
+            o_cond.at[r],
+            small_s.at[4, k],
+            small_r.at[4, r],
+            ident(plane(dx, dy), f),
+        )
+        cp.start()
+        cond_sent.append(cp)
+    own_cond = pltpu.make_async_copy(cond_all, o_cond.at[r], local_sem.at[0])
+    own_cond.start()
 
     lane = lax.broadcasted_iota(jnp.int32, (1, LANES_Q), 1)
     heads = [
@@ -735,9 +1002,10 @@
 
     @pl.when(z != r)
     def _():
-        remote(
-            out_shard, out_w.at[pl.ds(0, part)], ow_s.at[0], ow_r.at[0], ident(r, 2 * z + c)
-        ).wait_recv()
+        out_copy(z).wait_recv()
+
+    pl.when(inner & (across[2] == r))(out_onward().start)
+    red_send()
 
     def chunk_of(k):
         cc = (c + 1 + k // 2) % 2
@@ -773,6 +1041,7 @@
         return carry
 
     lax.fori_loop(0, 4, attend, 0)
+    exp_pass()
     branch = reduce_end(0, part_a, rows_a) + out_b
     branch_a[...] = branch
     mixed[...] = kept[...] + gate_attn * branch
@@ -780,8 +1049,10 @@
     own(x_two)[...] = (norm_two[...] * (1.0 + scale_mlp) + shift_mlp).astype(bf16)
     sent += gather_start(2, x_two)
     sent += gather_end(1, g_mlp)
-    line_wait(1, w_s, w_r, exp_src, exp_dst)
-    line_wait(2, w_s, w_r, red_src, red_dst)
+    red_pass()
+    exp_wait()
+    own_exp.wait()
+    red_wait()
     sent += gather_end(2, x_two)
     reduce_drain(0, part_a, sib_a, rows_a)
 
@@ -808,13 +1079,13 @@
     hid_sum = jnp.sum(g_hid[...].astype(f32), axis=0, keepdims=True)
     slab[8:9, : exp_all.shape[1]] = hid_sum
 
-    def zsend(kind, src, landing, height):
+    def zsend(kind, src, landing, height, lanes=slice(None)):
         copies = []
         for dz in range(1, 4):
             z2 = (z + dz) % 4
             cp = remote(
-                src.at[pl.ds(pl.multiple_of(z2 * height, 16), height)],
-                landing.at[dz - 1],
+                src.at[pl.ds(pl.multiple_of(z2 * height, 16), height), lanes],
+                landing.at[dz - 1, :, lanes],
                 dz_s.at[kind, dz - 1],
                 dz_r.at[kind, dz - 1],
                 ident(r, 2 * z2 + c),
@@ -829,7 +1100,12 @@
         return carry
 
     lax.fori_loop(0, 3, wide_grad, 0)
-    sent += zsend(0, d_exp, z_exp, 2 * part)
+    sent += zsend(0, d_exp, z_exp, 2 * part, tail)
+
+    @pl.when(c == 0)
+    def _():
+        zsend(1, d_exp, z_exp, 2 * part, head)
+
 
     grad_two = reduce_end(1, part_b, rows_b)
 
@@ -856,9 +1132,41 @@
         return carry
 
     lax.fori_loop(0, 3, red_grad, 0)
-    sent += zsend(1, d_red, z_red, 2 * PAD)
+
+    def red_tile(i):
+        p = 4 * c + i
+        at = r + 4 * p
+        return (p >= 5 * c), at, (2 * at) // (2 * blocks)
+
+    def red_up(i, src_z):
+        there = (src_z - red_tile(i)[2] + 4) % 4 - 1
+        return remote(
+            d_red.at[pl.ds(i * LANES, LANES)],
+            z_red.at[there, i % 3],
+            zr_s.at[i],
+            zr_r.at[there, i % 3],
+            ident(r, 2 * red_tile(i)[2] + c),
+        )
+
+    for i in range(slots_of):
+        real, at, goal = red_tile(i)
+
+        @pl.when(real & (goal != z))
+        def _():
+            red_up(i, z).start()
+
+    reduce_drain(1, part_b, sib_b, rows_b)
+    def feed_out(k, carry):
+        cc, first, here = chunk_of(k)
+        values = dot(act[here, :], red_all[...])
+        reduce_chunk(3, k, cc, values, part_b, sib_a, rows_b, hold=True)
+        return carry
+
+    lax.fori_loop(0, 4, feed_out, 0)
+
     sent += gather_end(3, g_attn)
-    reduce_drain(1, part_b, sib_b, rows_b)
+    for dx, dy in SAME_CORE:
+        reduce_send(3, part_b, rows_b, plane(dx, dy))
 
     def attend_back(k, carry):
         cc, first, here = chunk_of(k)
@@ -885,10 +1193,93 @@
             wide = jnp.concatenate([g_q * scale, g_k * scale, g_v], axis=1).astype(bf16)
             d_qkv[at, :] = dot_t(wide, spread[...]).astype(bf16)
         values = dot_t(d_qkv[here, :], proj_all[...])
-        reduce_chunk(2, k, cc, values, part_a, sib_a, rows_a)
+        reduce_chunk(2, k, cc, values, part_a, sib_b, rows_a)
         return carry
 
     lax.fori_loop(0, 4, attend_back, 0)
+
+    own_z = pl.ds(pl.multiple_of(z * 2 * part, 16), 2 * part)
+
+    def line_sum(kind, src, landing, lanes):
+        total = src[own_z, lanes].astype(f32)
+        for dz in range(1, 4):
+            remote(
+                src.at[own_z, lanes],
+                landing.at[dz - 1, :, lanes],
+                dz_s.at[kind, dz - 1],
+                dz_r.at[kind, dz - 1],
+                ident(r, 2 * ((z + dz) % 4) + c),
+            ).wait_recv()
+            total += landing[dz - 1, :, lanes].astype(f32)
+        src[own_z, lanes] = total.astype(bf16)
+
+    def exp_up(k, i, r2, c2):
+        at = red_tile(i)[1]
+        return remote(
+            d_exp.at[
+                pl.ds(pl.multiple_of(z * 2 * part + c2 * part, 16), part), pl.ds(i * LANES, LANES)
+            ],
+            o_exp.at[:, pl.ds(pl.multiple_of(at * LANES, LANES), LANES)],
+            et_s.at[k, i],
+            et_r.at[at],
+            ident(r2, 2 * z + c2),
+        )
+
+    def exp_here(i):
+        at = red_tile(i)[1]
+        return pltpu.make_async_copy(
+            d_exp.at[
+                pl.ds(pl.multiple_of(z * 2 * part + c * part, 16), part), pl.ds(i * LANES, LANES)
+            ],
+            o_exp.at[:, pl.ds(pl.multiple_of(at * LANES, LANES), LANES)],
+            et_l.at[i],
+        )
+
+    line_sum(0, d_exp, z_exp, tail)
+
+    @pl.when(c == 0)
+    def _():
+        line_sum(1, d_exp, z_exp, head)
+
+    for i in range(slots_of):
+
+        @pl.when(red_tile(i)[0])
+        def _():
+            for k, (r2, c2) in enumerate(board):
+                exp_up(k, i, r2, c2).start()
+            exp_here(i).start()
+
+    def red_out(i, h, r2):
+        half = 2 * red_tile(i)[1] + h
+        return remote(
+            d_red.at[pl.ds(i * LANES + h * HALF, HALF)],
+            o_red.at[pl.ds(pl.multiple_of(half % blocks * HALF, HALF), HALF)],
+            pr_s.at[2 * i + h, r2],
+            pr_r.at[half % blocks],
+            ident(r2, half // blocks),
+        )
+
+    def red_here(i, h):
+        half = 2 * red_tile(i)[1] + h
+        return pltpu.make_async_copy(
+            d_red.at[pl.ds(i * LANES + h * HALF, HALF)],
+            o_red.at[pl.ds(pl.multiple_of(half % blocks * HALF, HALF), HALF)],
+            pr_l.at[2 * i + h],
+        )
+
+    def red_each(i, remote_part, local_part):
+        for h in range(2):
+            owner = (2 * red_tile(i)[1] + h) // blocks
+            for r2 in range(4):
+
+                @pl.when((owner != f) | (r2 != r))
+                def _():
+                    remote_part(red_out(i, h, r2))
+
+            @pl.when(owner == f)
+            def _():
+                local_part(red_here(i, h))
+
 
     def proj_grad(k, carry):
         at = pl.ds(pl.multiple_of(k * third, 128), third)
@@ -905,20 +1296,32 @@
         remote(
             d_out.at[pl.ds(0, part)],
             z_out.at[slot_z],
-            ow_s.at[3],
+            ow_s.at[8],
             ow_r.at[1 + slot_z],
             ident(r, 2 * r + c),
         ).start()
 
     slab[9:10, : d_qkv.shape[1]] = jnp.sum(d_qkv[...].astype(f32), axis=0, keepdims=True)
 
-    def feed_out(k, carry):
-        cc, first, here = chunk_of(k)
-        values = dot(act[here, :], red_all[...])
-        reduce_chunk(3, k, cc, values, part_b, sib_b, rows_b)
-        return carry
-
-    lax.fori_loop(0, 4, feed_out, 0)
+
+    for i in range(slots_of):
+        real, at, goal = red_tile(i)
+
+        @pl.when(real & (goal == z))
+        def _():
+            rows_i = slice(i * LANES, (i + 1) * LANES)
+            total = d_red[rows_i, :].astype(f32)
+            for there in range(3):
+                remote(
+                    d_red.at[pl.ds(i * LANES, LANES)],
+                    z_red.at[there, i % 3],
+                    zr_s.at[i],
+                    zr_r.at[there, i % 3],
+                    ident(r, f),
+                ).wait_recv()
+                total += z_red[there, i % 3].astype(f32)
+            d_red[rows_i, :] = total.astype(bf16)
+            red_each(i, lambda cp: cp.start(), lambda cp: cp.start())
 
     def place(values, base):
         live_hot = (one_hot() * live_col[...]).astype(bf16)
@@ -926,60 +1329,27 @@
         hit = t_dot(live_hot, jnp.ones((rows, 128), bf16))[:, 0:1]
         return jnp.where(hit > 0.5, placed.astype(bf16), base)
 
+    branch = reduce_end(3, part_b, rows_b) + red_b
+    slab[5:6, :] = jnp.sum(g_rows[...] * branch, axis=0, keepdims=True)
+    o_block[...] = place(mixed[...] + gate_mlp * branch, latents[...])
+
+    def slab_at(f2):
+        return 4 * (f2 % 2) + f2 // 2
+
     grad_one = reduce_end(2, part_a, rows_a)
     g_shift, g_scale, through = back_norm(grad_one, scale_attn, norm_one[...], rstd_one[...])
     slab[0:1, :] = g_shift
     slab[1:2, :] = g_scale
     o_latents[...] = place(g_mixed[...] + through, cotangent[...])
-    branch = reduce_end(3, part_b, rows_b) + red_b
-    slab[5:6, :] = jnp.sum(g_rows[...] * branch, axis=0, keepdims=True)
-    slabs[f] = slab[...].astype(bf16)
+    slabs[slab_at(f)] = slab[...].astype(bf16)
 
     def slab_src(f2, c2):
-        return slabs.at[f]
+        return slabs.at[slab_at(f)]
 
     def slab_dst(f2):
-        return slabs.at[f2]
+        return slabs.at[slab_at(f2)]
 
     sent += line_send(5, small_s, small_r, slab_src, slab_dst)
-    o_block[...] = place(mixed[...] + gate_mlp * branch, latents[...])
-
-    outs = []
-
-    def spread_out(kind, src, landing, height, dest):
-        total = src[pl.ds(pl.multiple_of(z * height, 16), height), :].astype(f32)
-        for dz in range(1, 4):
-            remote(
-                src.at[pl.ds(0, height)],
-                landing.at[dz - 1],
-                dz_s.at[kind, dz - 1],
-                dz_r.at[kind, dz - 1],
-                ident(r, 2 * ((z + dz) % 4) + c),
-            ).wait_recv()
-            total += landing[dz - 1].astype(f32)
-        half = height // 2
-        keep = src.at[pl.ds(pl.multiple_of(z * height, 16), height)]
-        keep[...] = total.astype(bf16)
-        for k, (r2, c2) in enumerate(board):
-            cp = remote(
-                src.at[pl.ds(pl.multiple_of(z * height + c2 * half, 16), half)],
-                dest.at[me],
-                dp_s.at[kind, k],
-                dp_r.at[kind, me],
-                ident(r2, 2 * z + c2),
-            )
-            cp.start()
-            sent.append(cp)
-        cp = pltpu.make_async_copy(
-            src.at[pl.ds(pl.multiple_of(z * height + c * half, 16), half)],
-            dest.at[me],
-            local_sem.at[1 + kind],
-        )
-        cp.start()
-        outs.append(cp)
-
-    spread_out(0, d_exp, z_exp, 2 * part, o_exp)
-    spread_out(1, d_red, z_red, 2 * PAD, o_red)
 
     @pl.when(z == r)
     def _():
@@ -999,9 +1369,14 @@
         cp.wait()
 
     line_wait(5, small_s, small_r, slab_src, slab_dst)
+    mine = pl.ds(pl.multiple_of(4 * c, 4), 4)
     for k, (dx, dy) in enumerate(SAME_CORE):
         cp = remote(
-            slabs, o_slabs.at[r], small_s.at[6, k], small_r.at[6, r], ident(plane(dx, dy), f)
+            slabs.at[mine],
+            o_slabs.at[r, mine],
+            small_s.at[6, k],
+            small_r.at[6, r],
+            ident(plane(dx, dy), f),
         )
         cp.start()
         sent.append(cp)
@@ -1011,7 +1386,7 @@
     for p in range(6):
         back_cond += dot_t(slabs[:, p, :], mod_w[:, p * width : (p + 1) * width])
     for i in range(8):
-        gcond[i] = jnp.broadcast_to(back_cond[i : i + 1, :], (8, part))
+        gcond[2 * (i % 4) + i // 4] = jnp.broadcast_to(back_cond[i : i + 1, :], (8, part))
 
     def gc_src(f2, c2):
         return gcond.at[f2]
@@ -1022,50 +1397,156 @@
     sent += line_send(7, small_s, small_r, gc_src, gc_dst)
     o_gcond[f] = gcond[f]
 
-    spread_out(2, d_proj, z_proj, 2 * part, o_proj)
-
+    every = slice(None)
+    line_sum(2, d_proj, z_proj, every)
+
+    def proj_up(k, r2, c2):
+        return remote(
+            d_proj.at[pl.ds(pl.multiple_of(z * 2 * part + c2 * part, 16), part)],
+            proj_land.at[me],
+            dp_s.at[k],
+            dp_r.at[me],
+            ident(r2, 2 * z + c2),
+        )
+
+    for k, (r2, c2) in enumerate(board):
+        proj_up(k, r2, c2).start()
+    proj_land[me] = d_proj[pl.ds(pl.multiple_of(z * 2 * part + c * part, 16), part), :]
+
+    for k, (dx, dy) in enumerate(SAME_CORE):
+        r2 = plane(dx, dy)
+        remote(
+            slabs.at[mine], o_slabs.at[r2, mine], small_s.at[6, 0], small_r.at[6, r2], sibling
+        ).wait_recv()
+        cp = remote(
+            o_slabs.at[r2, mine],
+            o_slabs.at[r2, mine],
+            small_s.at[6, 3 + k],
+            small_r.at[6, 4 + r2],
+            sibling,
+        )
+        cp.start()
+        sent.append(cp)
     line_wait(7, small_s, small_r, gc_src, gc_dst)
     for dx, dy in SAME_CORE:
         r2 = plane(dx, dy)
         remote(
             cond_all, o_cond.at[r2], small_s.at[4, 0], small_r.at[4, r2], ident(r2, f)
         ).wait_recv()
+        theirs = pl.ds(pl.multiple_of(4 * other, 4), 4)
         remote(
-            slabs, o_slabs.at[r2], small_s.at[6, 0], small_r.at[6, r2], ident(r2, f)
+            slabs.at[theirs], o_slabs.at[r2, theirs], small_s.at[6, 3], small_r.at[6, 4 + r2], sibling
         ).wait_recv()
-    for kind, dest in ((0, o_exp), (1, o_red), (2, o_proj)):
-        for r2, c2 in board:
-            u = 4 * c2 + r2
+    for r2, c2 in board:
+        u = 4 * c2 + r2
+        remote(
+            proj_land.at[u], proj_land.at[u], dp_s.at[0], dp_r.at[u], ident(r2, 2 * z + c2)
+        ).wait_recv()
+
+    o_proj[...] = jnp.zeros(o_proj.shape, bf16)
+    for u in range(8):
+        t = 2 * (u % 4) + u // 4
+        wide = dot(proj_land[u], spread[...])
+        for q in range(3):
+            piece = wide[:, q * LANES_Q : (q + 1) * LANES_Q]
+            if t:
+                piece = pltpu.roll(piece, t * (part - LANES), 1)
+            first = q * width + t * LANES
+            o_proj[:, first : first + LANES_Q] = (
+                o_proj[:, first : first + LANES_Q].astype(f32) + piece
+            ).astype(bf16)
+
+    def tile_arrival(at, carry):
+        p = at // 4
+
+        @pl.when((at % 4 != r) | (p // slots_of != c))
+        def _():
             remote(
-                dest.at[u], dest.at[u], dp_s.at[kind, 0], dp_r.at[kind, u], ident(r2, 2 * z + c2)
+                d_exp.at[pl.ds(0, part), pl.ds(0, LANES)],
+                o_exp.at[:, pl.ds(pl.multiple_of(at * LANES, LANES), LANES)],
+                et_s.at[0, 0],
+                et_r.at[at],
+                sibling,
             ).wait_recv()
+
+        return carry
+
+    lax.fori_loop(0, tiles, tile_arrival, 0)
+
+    def block_arrival(block, carry):
+        at = (blocks * f + block) // 2
+        p = at // 4
+
+        @pl.when((at % 4 != r) | (p // slots_of != c))
+        def _():
+            remote(
+                d_red.at[pl.ds(0, HALF)],
+                o_red.at[pl.ds(pl.multiple_of(block * HALF, HALF), HALF)],
+                pr_s.at[0, 0],
+                pr_r.at[block],
+                sibling,
+            ).wait_recv()
+
+        return carry
+
+    lax.fori_loop(0, blocks, block_arrival, 0)
+    for i in range(slots_of):
+        real, at, goal = red_tile(i)
+
+        @pl.when(real)
+        def _():
+            for k, (r2, c2) in enumerate(board):
+                exp_up(k, i, r2, c2).wait_send()
+            exp_here(i).wait()
+
+        @pl.when(real & (goal == z))
+        def _():
+            red_each(i, lambda cp: cp.wait_send(), lambda cp: cp.wait())
+
+        @pl.when(real & (goal != z))
+        def _():
+            red_up(i, z).wait_send()
+
+    for k, (r2, c2) in enumerate(board):
+        proj_up(k, r2, c2).wait_send()
+    red_drain()
+    exp_drain()
+
+    @pl.when(c == 0)
+    def _():
+        for dz in range(1, 4):
+            remote(
+                d_exp.at[own_z, head],
+                z_exp.at[dz - 1, :, head],
+                dz_s.at[1, dz - 1],
+                dz_r.at[1, dz - 1],
+                ident(r, f),
+            ).wait_send()
+
+    for z2 in range(4):
+        pl.when(out_goes(z2))(out_copy(z2).wait_send)
+    pl.when(inner & (across[2] == r))(out_onward().wait_send)
 
     @pl.when(z == r)
     def _():
-        for dz in range(3):
-            remote(
-                out_shard, out_w.at[pl.ds(0, part)], ow_s.at[dz], ow_r.at[0], ident(r, f)
-            ).wait_send()
-            remote(
-                out_shard, o_out, ow_s.at[4 + dz], ow_r.at[4], ident(r, f)
-            ).wait_send()
+        for k in range(3):
+            remote(out_shard, o_out, ow_s.at[4 + k], ow_r.at[4], ident(r, f)).wait_send()
 
     @pl.when(z != r)
     def _():
         remote(out_shard, o_out, ow_s.at[3], ow_r.at[4], ident(r, f)).wait_recv()
         remote(
-            d_out.at[pl.ds(0, part)], z_out.at[0], ow_s.at[3], ow_r.at[1], ident(r, f)
+            d_out.at[pl.ds(0, part)], z_out.at[0], ow_s.at[8], ow_r.at[1], ident(r, f)
         ).wait_send()
 
-    reduce_drain(2, part_a, sib_a, rows_a)
-    reduce_drain(3, part_b, sib_b, rows_b)
+    relay_drain(*proj_main)
+    reduce_drain(2, part_a, sib_b, rows_a)
+    reduce_drain(3, part_b, sib_a, rows_b)
     drain(sent)
     drain(live_sent)
     drain(cond_sent)
     own_cond.wait()
     own_slabs.wait()
-    for cp in outs:
-        cp.wait()
 
 
 def fused_local(
@@ -1093,8 +1574,8 @@
     rows = keep_slots.shape[1]
     part = output_weight.shape[0]
     hid = expand_weight.shape[1]
-    share = hid // 64
-    wide = 8 * PAD
+    slots_of = (hid // LANES + 7) // 8
+    wide = slots_of * LANES
 
     def placed(shard, count):
         return lax.dynamic_update_slice_in_dim(
@@ -1112,8 +1593,10 @@
     live = (jnp.arange(rows, dtype=jnp.int32) < live_count).astype(f32)
     qv = mine(placed(query_value_bias, 2 * width).reshape(2, 8, part), 1)
     qv = jnp.pad(qv.transpose(1, 0, 2), ((0, 0), (0, 0), (0, LANES_Q - part))).reshape(2, -1)
-    expand_b = mine(placed(expand_bias, hid).reshape(8, 8, share), 1).transpose(1, 0, 2)
-    expand_b = jnp.pad(expand_b, ((0, 0), (0, 0), (0, PAD - share))).reshape(2, wide)
+    tiled_b = placed(expand_bias, hid).reshape(hid // (4 * LANES), 4, LANES)
+    tiled_b = lax.dynamic_index_in_dim(tiled_b, r, 1, keepdims=False)
+    second_b = jnp.pad(tiled_b[slots_of:], ((1, 0), (0, 0)))
+    expand_b = jnp.stack([tiled_b[:slots_of].reshape(-1), second_b.reshape(-1)])
     extra = jnp.stack(
         [
             jnp.broadcast_to(placed(output_bias, width), (2, width)),
@@ -1124,13 +1607,6 @@
         axis=1,
     ).astype(bf16)
     extra = jnp.pad(extra, ((0, 0), (0, 12), (0, 0)))
-    proj_pack = mine(projection_weight.reshape(part, 3, 8, part), 2)
-    proj_pack = proj_pack.transpose(2, 0, 1, 3).reshape(2, part, 3 * part)
-    exp_pack = mine(expand_weight.reshape(part, 8, 8, share), 2).transpose(2, 0, 1, 3)
-    exp_pack = jnp.pad(exp_pack, ((0, 0),) * 3 + ((0, PAD - share),)).reshape(2, part, wide)
-    red_pack = mine(reduce_weight.reshape(8, share, width), 0)
-    red_pack = jnp.pad(red_pack, ((0, 0), (0, PAD - share), (0, 0)))
-
     total = 8 * rows
     vmem = pltpu.VMEM
     dma = pltpu.SemaphoreType.DMA
@@ -1144,6 +1620,8 @@
         vmem((width, wide), bf16),
         vmem((wide, width), bf16),
         vmem((LANES_Q, width), bf16),
+        vmem((2, part, 3 * part), bf16),
+        vmem((2, part, wide), bf16),
         vmem((width, 3 * LANES_Q), bf16),
         vmem((3 * part, 3 * LANES_Q), bf16),
         vmem((total, width), bf16),
@@ -1163,7 +1641,6 @@
     scratch += [vmem((4, rows, width), bf16)] * 2
     scratch += [
         vmem((rows, width), f32),
-        vmem((rows, width), f32),
         vmem((rows, 1), f32),
         vmem((rows, width), f32),
         vmem((rows, width), f32),
@@ -1179,9 +1656,10 @@
         vmem((width, 3 * part), bf16),
         vmem((LANES_Q, width), bf16),
         vmem((3, 2 * part, wide), bf16),
-        vmem((3, 2 * PAD, width), bf16),
+        vmem((3, 3, LANES, width), bf16),
         vmem((3, 2 * part, 3 * part), bf16),
         vmem((3, part, width), bf16),
+        vmem((8, part, 3 * part), bf16),
         dma((8,)),
         dma((8, 7)),
         dma((8, 8)),
@@ -1195,10 +1673,24 @@
         dma((4, 4)),
         dma((3, 3)),
         dma((3, 3)),
-        dma((3, 7)),
-        dma((3, 8)),
         dma((7,)),
+        dma((8,)),
+        dma((9,)),
         dma((5,)),
+        dma((hid // HALF // 4, 4)),
+        dma((2 * slots_of,)),
+        dma((2 * slots_of,)),
+        dma((slots_of,)),
+        dma((3, 3)),
+        dma((2, slots_of)),
+        dma((7, slots_of)),
+        dma((hid // LANES,)),
+        dma((slots_of,)),
+        dma((2 * slots_of, 4)),
+        dma((hid // HALF // 8,)),
+        dma((2 * slots_of,)),
+        dma((3, 2)),
+        dma((2 * slots_of,)),
     ]
     in_vmem = pl.BlockSpec(memory_space=pltpu.VMEM)
     anywhere = pl.BlockSpec(memory_space=pl.ANY)
@@ -1210,12 +1702,12 @@
             jax.ShapeDtypeStruct((4, 8, 16, width), bf16),
             jax.ShapeDtypeStruct((4, 8, 16, part), bf16),
             jax.ShapeDtypeStruct((8, 8, part), f32),
-            jax.ShapeDtypeStruct((8, part, wide), bf16),
-            jax.ShapeDtypeStruct((8, PAD, width), bf16),
-            jax.ShapeDtypeStruct((8, part, 3 * part), bf16),
+            jax.ShapeDtypeStruct((part, hid), bf16),
+            jax.ShapeDtypeStruct((hid // 8, width), bf16),
+            jax.ShapeDtypeStruct((part, 3 * width), bf16),
             jax.ShapeDtypeStruct((part, width), bf16),
         ),
-        in_specs=[in_vmem] * 13,
+        in_specs=[in_vmem] * 10 + [anywhere] * 2 + [in_vmem],
         out_specs=(
             in_vmem,
             in_vmem,
@@ -1224,7 +1716,7 @@
             in_vmem,
             anywhere,
             anywhere,
-            anywhere,
+            in_vmem,
             anywhere,
         ),
         scratch_shapes=scratch,
@@ -1241,9 +1733,9 @@
         mod_bias,
         extra,
         modulation_weight,
-        proj_pack,
-        exp_pack,
-        red_pack,
+        projection_weight,
+        expand_weight,
+        reduce_weight,
         output_weight,
     )
     block, grad_latents, slabs, conds, g_cond, g_exp, g_red, g_proj, g_out = outputs
@@ -1253,35 +1745,33 @@
 
     slabs = slabs.reshape(32, 16, width)
     grad_mod = slabs[:, :6].reshape(32, 6 * width)
-    cond_cols = conds[:, :, 0].reshape(32, part)
+    cond_cols = conds[:, :, 0].reshape(4, 4, 2, part).transpose(0, 2, 1, 3).reshape(32, part)
     sum_mod_w = jnp.einsum("bd,be->de", cond_cols, grad_mod, preferred_element_type=f32)
     sums = jnp.sum(slabs[:, :8].astype(f32), axis=0)
     sum_mod_b = shard(sums[:6].reshape(-1), 0, modulation_bias.shape[0])
     sum_red_b = shard(sums[6], 0, part)
     sum_out_b = shard(sums[7], 0, part)
-    tails = jnp.sum(slabs[:, 8:10].astype(f32).reshape(4, 4, 2, 2, width), axis=1)
-    exp_sums = tails[:, :, 0, :wide].reshape(8, 8, PAD)
-    sum_exp_b = lax.dynamic_index_in_dim(exp_sums, f, 1, keepdims=False)[:, :share].reshape(-1)
+    tails = jnp.sum(slabs[:, 8:10].astype(f32).reshape(4, 2, 4, 2, width), axis=2)
+    exp_sums = tails[:, :, 0, :wide].reshape(4, 2, slots_of, LANES)
+    exp_sums = jnp.concatenate([exp_sums[:, 0], exp_sums[:, 1, 1:]], axis=1)
+    sum_exp_b = shard(exp_sums.transpose(1, 0, 2).reshape(-1), 0, expand_bias.shape[0])
     qv_sums = tails[:, :, 1, : 3 * part].reshape(8, 3, part)
     qv_sums = jnp.concatenate([qv_sums[:, 0].reshape(-1), qv_sums[:, 2].reshape(-1)])
     sum_qv_b = shard(qv_sums, 0, query_value_bias.shape[0])
     grad_condition = jax.vjp(jax.nn.silu, cond_float)[1](g_cond[:, 0].reshape(1, width))[0]
-    g_exp = g_exp.reshape(2, 4, part, 8, PAD)[..., :share].transpose(2, 3, 1, 0, 4)
-    g_red = g_red.reshape(2, 4, PAD, width)[:, :, :share].transpose(1, 0, 2, 3)
-    g_proj = g_proj.reshape(2, 4, part, 3, part).transpose(2, 3, 1, 0, 4)
     return (
         block[None],
         grad_latents[None],
         grad_condition,
         sum_mod_w,
         sum_mod_b,
-        g_proj.reshape(part, 3 * width).astype(f32),
+        g_proj.astype(f32),
         sum_qv_b,
         g_out.astype(f32),
         sum_out_b,
-        g_exp.reshape(part, hid).astype(f32),
+        g_exp.astype(f32),
         sum_exp_b,
-        g_red.reshape(8 * share, width).astype(f32),
+        g_red.astype(f32),
         sum_red_b,
     )
 

time: 373 us -> 291 us (0.78)
  local copies, waits for them, and re-layouts: 64.3 us -> 10.8 us
  Pallas kernels: 293 us -> 258 us
  other arithmetic: 11 us -> 15.5 us
    pallas_call x1, Pallas kernels: 293 us -> 258 us  [fused_local(): pl.pallas_call(fused_kernel, out_shape=(jax.ShapeDtypeStruct((slot_count,...]
    convert_element_type x6 -> x0, local copies, waits for them, and re-layouts: 31.5 us -> none  [the longest x2 15.4 us: fused_local(): g_exp.reshape(part, hid).astype(f32)]
    reshape x8 -> x3, local copies, waits for them, and re-layouts: 18.6 us -> 0.05 us  [the longest x1 0.02 us: fused_local(): conds[:, :, 0].reshape(4, 4, 2, part).transpose(0, 2, 1, 3)]
where the time goes in v3:
time: 291 us; the launch traced here: 288 us
  Pallas kernels  258 us (89%)
  other arithmetic  15.5 us (5%)
  local copies, waits for them, and re-layouts  10.8 us (4%)
    pallas_call x1, Pallas kernels, fused_local(): pl.pallas_call(fused_kernel, out_shape=(jax.ShapeDtypeStruct((slot_count,...  258 us

profile of v3, /device:TPU:25, one launch (start us, length us, event | category | flops | bytes accessed | tf_op | source)
XLA Modules:
  0.0 288.3 jit_solution(7462983522189898943)
XLA Ops:
  1.3 0.6 broadcast_in_dim.21.live_row
  1.9 0.7 convert_dynamic-update-slice_fusion.3
  2.7 0.8 convert_dynamic-update-slice_fusion.4
  3.5 0.7 convert_reduce_fusion.2
  4.2 0.1 reshape.118
  4.3 0.8 convert_dynamic-update-slice_fusion.2
  5.1 0.1 reshape.106
  5.3 0.8 convert_dynamic-update-slice_fusion
  6.2 0.8 convert_dynamic-update-slice_fusion.1
  7.0 0.6 pad.33.mod_bias
  7.7 0.7 fusion.6.extra
  8.4 0.6 pad.32.cond_pack
  9.0 0.6 fusion.7.live_col
  9.6 1.4 copy.46.slots
  11.0 0.0 copy-start.7
  11.0 257.8 %shard_map.246 = (bf16[256,1152]{1,0:T(8,128)(2,1)}, bf16[256,1152]{1,0:T(8,128)(2,1)}, bf16[4,8,16,1152]{3,2,1,0:T(8,128)(2,1)}, bf16[4,8,16,144]{3,2,1,0:T(8,1...) custom-call(bf16[256,1152]{1,0:T(8,128)(2,1)} %bitcast.52, ...), custom_call_target="tpu_custom_call" | custom-call | tf_op jit(solution)/shard_map/pallas_call | solution.py:1697
  268.8 0.0 copy-start
  268.9 1.0 slice_reduce_fusion.4
  269.8 0.1 reshape_squeeze.18
  269.9 0.0 copy-done.7
  269.9 0.6 fusion.11
  270.5 0.9 slice.58
  271.5 1.2 convert_reduce_fusion
  272.7 0.6 constant_dynamic-slice_fusion
  273.3 0.7 dynamic_slice.28
  274.0 1.2 convert_reduce_fusion.1
  275.3 0.0 copy-done
  275.3 0.0 copy-start.6
  275.3 0.0 copy-start.3
  275.4 0.1 slice_reduce_fusion.1
  275.5 0.1 slice_reduce_fusion
  275.6 0.7 dynamic_slice.32
  276.3 0.1 reshape_squeeze.20
  276.4 0.1 reshape_squeeze.22
  276.5 0.1 reshape_squeeze.21
  276.6 0.7 fusion.15
  277.3 0.0 copy-done.6
  277.3 0.9 convert_element_type.79
  278.2 0.0 copy-done.3
  278.2 0.0 copy-start.2
  278.2 1.4 convert_element_type.78
  279.6 0.5 copy-done.2
  280.1 0.0 copy-start.1
  280.1 1.8 convert_element_type.80
  281.9 0.0 copy-done.1
  281.9 1.7 convert_element_type.81
  283.6 0.0 copy-start.5
  283.6 2.6 fusion.17
  286.2 0.0 copy-done.5
  286.2 0.0 copy-start.4
  286.2 0.8 copy.68
  287.1 0.5 copy-done.4
  287.5 0.8 copy.69
  (38 shorter events, 0.4 us)
Async XLA Ops:
  11.0 258.9 %copy-start.7 = (bf16[1,1152]{1,0:T(2,128)(2,1)S(1)}, bf16[1,1152]{1,0:T(2,128)(2,1)}, u32[]{:S(2)}) copy-start(bf16[1,1152]{1,0:T(2,128)(2,1)} %param.16) | copy-start | bytes 6916
  268.8 6.4 %copy-start = (bf16[4,8,16,1152]{3,2,1,0:T(8,128)(2,1)S(1)}, bf16[4,8,16,1152]{3,2,1,0:T(8,128)(2,1)}, u32[]{:S(2)}) copy-start(bf16[4,8,16,1152]{3,2,1,0:T(8,128)(2,1)} %get-tuple-element.26) | copy-start | bytes 3538948
  275.3 2.0 copy-start.6
  275.3 2.9 copy-start.3
  278.2 1.9 copy-start.2
  280.1 1.8 copy-start.1
  283.6 2.6 copy-start.5
  286.2 1.3 copy-start.4

commit v4 on v3

--- a/solution.py
+++ b/solution.py
@@ -317,7 +317,6 @@
     latents,
     cotangent,
     slots,
-    live_col,
     live_row,
     cond_pack,
     mod_bias,
@@ -356,7 +355,6 @@
     qkv,
     probs,
     attended,
-    act,
     g_hid,
     d_qkv,
     part_a,
@@ -423,10 +421,12 @@
     f = lax.axis_index("fsdp")
     x, y, c, z = r % 2, r // 2, f % 2, f // 2
     width = latents.shape[1]
-    rows = slots.shape[0]
+    rows = slots.shape[1]
     part = out_shard.shape[0]
     third = width // 3
     kept = g_mixed
+    total_rows = x_one.shape[0]
+    hid_lanes = pl.ds(0, red_all.shape[0])
     blocks = red_w.shape[0] // HALF
     slots_of = red_all.shape[0] // LANES
     tiles = exp_w.shape[1] // LANES
@@ -705,7 +705,6 @@
                 relay_copy(k, *exp_lead).wait_send()
 
     sent = line_send(0, small_s, small_r, cond_src, cond_dst)
-    sent += line_send(1, small_s, small_r, extra_src, extra_dst)
     packs = []
     for c2 in range(2):
         for i in range(slots_of):
@@ -739,7 +738,7 @@
         cp.start()
 
     def one_hot():
-        ids = lax.broadcasted_iota(jnp.int32, (rows, latents.shape[0]), 1)
+        ids = lax.broadcasted_iota(jnp.int32, (latents.shape[0], rows), 0)
         return jnp.where(ids == slots[...], 1.0, 0.0)
 
     def dot(a, b):
@@ -750,23 +749,6 @@
 
     def t_dot(a, b):
         return lax.dot_general(a, b, (((0,), (0,)), ((), ())), preferred_element_type=f32)
-
-    local[0].wait()
-    line_wait(0, small_s, small_r, cond_src, cond_dst)
-    cond_cols = jnp.sum(cond_all[...].astype(f32), axis=1).astype(bf16)
-    mod_send[...] = jnp.zeros(mod_send.shape, f32)
-    for p in range(6):
-        piece = dot(cond_cols, mod_w[:, p * width : (p + 1) * width]) + mod_bias[p : p + 1, :]
-        mod_send[:, p, :] = piece
-
-    def mod_src(f2, c2):
-        return mod_send.at[f2]
-
-    def mod_dst(f2):
-        return mod_all.at[f2]
-
-    sent += line_send(2, small_s, small_r, mod_src, mod_dst)
-    mod_all[f] = mod_send[f]
 
     wide_columns = proj_all.shape[1]
     for c2 in range(2):
@@ -783,13 +765,31 @@
             )
             picked += dot(window, jnp.where(picks, 1.0, 0.0).astype(bf16))
         proj_pack[c2] = picked.astype(bf16)
+    local[0].wait()
+    line_wait(0, small_s, small_r, cond_src, cond_dst)
+    cond_cols = jnp.sum(cond_all[...].astype(f32), axis=1).astype(bf16)
+    mod_send[...] = jnp.zeros(mod_send.shape, f32)
+    for p in range(6):
+        piece = dot(cond_cols, mod_w[:, p * width : (p + 1) * width]) + mod_bias[p : p + 1, :]
+        mod_send[:, p, :] = piece
+
+    def mod_src(f2, c2):
+        return mod_send.at[f2]
+
+    def mod_dst(f2):
+        return mod_all.at[f2]
+
+    sent += line_send(2, small_s, small_r, mod_src, mod_dst)
+    mod_all[f] = mod_send[f]
+
     relay_send(0, w_s, w_r, proj_src, proj_dst)
+    sent += line_send(1, small_s, small_r, extra_src, extra_dst)
     own_proj = pltpu.make_async_copy(proj_pack.at[c], proj_dst(f), local_sem.at[2])
     own_proj.start()
     local.append(own_proj)
 
-    kept[...] = dot(one_hot().astype(bf16), latents[...])
-    g_rows[...] = dot((one_hot() * live_col[...]).astype(bf16), cotangent[...])
+    kept[...] = t_dot(one_hot().astype(bf16), latents[...])
+    g_rows[...] = t_dot((one_hot() * live_row[0:1, :]).astype(bf16), cotangent[...])
 
     def normalise(values, norm_ref, rstd_ref):
         centred = values - jnp.mean(values, axis=-1, keepdims=True)
@@ -842,22 +842,33 @@
             )
         for cp in copies:
             cp.start()
-        return copies
-
-    def gather_end(kind, buf):
-        copies = []
-        for k, (dx, dy) in enumerate(SAME_CORE):
-            u = 4 * c + plane(dx, dy)
-            cp = remote(slot(buf, u), slot(buf, u), ag_s.at[kind, 4 + k], ag_r.at[kind, u], sibling)
-            cp.wait_recv()
-            cp.start()
-            copies.append(cp)
-        for r2 in range(4):
-            u = 4 * other + r2
+
+    def gather_pass(kind, buf, k):
+        u = 4 * c + plane(*SAME_CORE[k])
+        cp = remote(slot(buf, u), slot(buf, u), ag_s.at[kind, 4 + k], ag_r.at[kind, u], sibling)
+        cp.wait_recv()
+        cp.start()
+
+    def gather_take(kind, buf, r2):
+        u = 4 * other + r2
+        remote(slot(buf, u), slot(buf, u), ag_s.at[kind, 0], ag_r.at[kind, u], sibling).wait_recv()
+
+    def gather_near(kind, buf):
+        gather_pass(kind, buf, 0)
+        gather_pass(kind, buf, 1)
+        gather_take(kind, buf, r)
+        gather_take(kind, buf, plane(1, 0))
+
+    def gather_far(kind, buf):
+        gather_pass(kind, buf, 2)
+        gather_take(kind, buf, plane(0, 1))
+        gather_take(kind, buf, plane(1, 1))
+
+    def gather_drain(kind, buf):
+        for k in range(7):
             remote(
-                slot(buf, u), slot(buf, u), ag_s.at[kind, 0], ag_r.at[kind, u], sibling
-            ).wait_recv()
-        return copies
+                own(buf), own(buf), ag_s.at[kind, k], ag_r.at[kind, me], sibling
+            ).wait_send()
 
     def reduce_send(kind, buf, landing, r2):
         remote(
@@ -868,27 +879,29 @@
             ident(r2, f),
         ).start()
 
-    def reduce_chunk(kind, k, cc, values, buf, sib, landing, hold=False):
-        base = pl.multiple_of(cc * 4 * rows + (k % 2) * 2 * rows, 2 * rows)
-        here = pl.ds(base, 2 * rows)
-        there = pl.ds(pl.multiple_of((k % 2) * 2 * rows, 2 * rows), 2 * rows)
-        slot_k = k % 2
-
-        @pl.when(k < 2)
+    def chunk_of(k):
+        cc, pair = (c + 1 + k) % 2, (y + k // 2) % 2
+        first = 4 * cc + 2 * pair
+        return first, pair, pl.ds(pl.multiple_of(first * rows, 2 * rows), 2 * rows)
+
+    def reduce_chunk(kind, k, values, buf, sib, landing, hold=False):
+        first, pair, here = chunk_of(k)
+        there = pl.ds(pl.multiple_of(pair * 2 * rows, 2 * rows), 2 * rows)
+        hop = remote(
+            buf.at[here], sib.at[there], sb_s.at[kind, pair], sb_r.at[kind, pair], sibling
+        )
+
+        @pl.when(k % 2 == 0)
         def _():
             buf[here, :] = values.astype(bf16)
-            remote(
-                buf.at[here], sib.at[there], sb_s.at[kind, slot_k], sb_r.at[kind, slot_k], sibling
-            ).start()
-
-        @pl.when(k >= 2)
-        def _():
-            remote(
-                buf.at[here], sib.at[there], sb_s.at[kind, slot_k], sb_r.at[kind, slot_k], sibling
-            ).wait_recv()
+            hop.start()
+
+        @pl.when(k % 2 == 1)
+        def _():
+            hop.wait_recv()
             buf[here, :] = (values + sib[there, :].astype(f32)).astype(bf16)
             for x2 in range(0 if hold else 2):
-                r2 = 2 * slot_k + x2
+                r2 = 2 * pair + x2
 
                 @pl.when(r2 != r)
                 def _():
@@ -917,9 +930,10 @@
             ).wait_send()
 
     own(x_one)[...] = (norm_one[...] * (1.0 + scale_attn) + shift_attn).astype(bf16)
-    sent += gather_start(0, x_one)
+    gather_start(0, x_one)
     grad_mlp = (gate_mlp * g_rows[...]).astype(bf16)
     own(g_mlp)[...] = grad_mlp
+    gather_start(1, g_mlp)
     slab[...] = jnp.zeros(slab.shape, f32)
     slab[6:7, :] = jnp.sum(grad_mlp.astype(f32), axis=0, keepdims=True)
 
@@ -944,14 +958,14 @@
     def out_goes(z2):
         return (z == r) & (z2 != z) & (inner | (z2 + z != 3))
 
-    for z2 in range(4):
-        pl.when(out_goes(z2))(out_copy(z2).start)
 
     @pl.when(z == r)
     def _():
         out_w[:part, :] = out_shard[...]
 
     relay_pass(*proj_main)
+    for z2 in range(4):
+        pl.when(out_goes(z2))(out_copy(z2).start)
     relay_wait(*proj_main)
     for cp in packs:
         cp.wait()
@@ -968,7 +982,10 @@
     proj_wide[...] = dot(proj_all[...], spread[...]).astype(bf16)
     line_wait(1, small_s, small_r, extra_src, extra_dst)
     biases = jnp.sum(extra_all[...].astype(f32), axis=0)
-    out_b, red_b, exp_b, qv_b = [biases[p : p + 1, :] for p in range(4)]
+    out_b, red_b, exp_b, qv_b = [
+        jnp.concatenate([biases[3 * p + q : 3 * p + q + 1, :] for q in range(3)], axis=1)
+        for p in range(4)
+    ]
     for k, (r2, c2) in enumerate(board):
         remote(
             live_row,
@@ -977,8 +994,7 @@
             small_r.at[3, 4 * c2 + r2],
             ident(r2, 2 * z + c2),
         ).wait_recv()
-    sent += gather_end(0, x_one)
-    sent += gather_start(1, g_mlp)
+    gather_near(0, x_one)
     cond_sent = []
     for k, (dx, dy) in enumerate(SAME_CORE):
         cp = remote(
@@ -1007,13 +1023,13 @@
     pl.when(inner & (across[2] == r))(out_onward().start)
     red_send()
 
-    def chunk_of(k):
-        cc = (c + 1 + k // 2) % 2
-        first = 4 * cc + 2 * (k % 2)
-        return cc, first, pl.ds(pl.multiple_of(first * rows, 2 * rows), 2 * rows)
-
     def attend(k, carry):
-        cc, first, here = chunk_of(k)
+        first, pair, here = chunk_of(k)
+
+        @pl.when(k == 2)
+        def _():
+            gather_far(0, x_one)
+
         wide = dot(x_one[here, :], proj_wide[...])
         qkv[here, :LANES_Q] = (wide[:, :LANES_Q] + qv_b[:, :LANES_Q]).astype(bf16)
         qkv[here, LANES_Q : 2 * LANES_Q] = wide[:, LANES_Q : 2 * LANES_Q].astype(bf16)
@@ -1037,7 +1053,7 @@
                 total += dot(p.astype(bf16), val) * heads[h].astype(f32)
             attended[at, :] = total.astype(bf16)
         values = dot(attended[here, :], out_w[...])
-        reduce_chunk(0, k, cc, values, part_a, sib_a, rows_a)
+        reduce_chunk(0, k, values, part_a, sib_a, rows_a)
         return carry
 
     lax.fori_loop(0, 4, attend, 0)
@@ -1047,31 +1063,37 @@
     mixed[...] = kept[...] + gate_attn * branch
     normalise(mixed[...], norm_two, rstd_two)
     own(x_two)[...] = (norm_two[...] * (1.0 + scale_mlp) + shift_mlp).astype(bf16)
-    sent += gather_start(2, x_two)
-    sent += gather_end(1, g_mlp)
+    gather_start(2, x_two)
+    gather_near(1, g_mlp)
+    gather_far(1, g_mlp)
     red_pass()
     exp_wait()
     own_exp.wait()
     red_wait()
-    sent += gather_end(2, x_two)
+    gather_near(2, x_two)
     reduce_drain(0, part_a, sib_a, rows_a)
 
     k_gelu = 0.7978845608028654
     hid_b = exp_b[:, : exp_all.shape[1]]
 
     def feed(k, carry):
-        cc, first, here = chunk_of(k)
+        first, pair, here = chunk_of(k)
+
+        @pl.when(k == 2)
+        def _():
+            gather_far(2, x_two)
+
         hid = dot(x_two[here, :], exp_all[...]) + hid_b
         square = hid * hid
         th = jnp.tanh(k_gelu * hid * (1.0 + 0.044715 * square))
-        act[here, :] = (0.5 * hid * (1.0 + th)).astype(bf16)
+        proj_wide[here, hid_lanes] = (0.5 * hid * (1.0 + th)).astype(bf16)
         slope = 0.5 * (1.0 + th) + 0.5 * hid * (1.0 - th * th) * k_gelu * (
             1.0 + 3.0 * 0.044715 * square
         )
         grad = (dot_t(g_mlp[here, :], red_all[...]) * slope).astype(bf16)
         g_hid[here, :] = grad
         values = dot_t(grad, exp_all[...])
-        reduce_chunk(1, k, cc, values, part_b, sib_b, rows_b)
+        reduce_chunk(1, k, values, part_b, sib_b, rows_b)
         return carry
 
     lax.fori_loop(0, 4, feed, 0)
@@ -1079,20 +1101,79 @@
     hid_sum = jnp.sum(g_hid[...].astype(f32), axis=0, keepdims=True)
     slab[8:9, : exp_all.shape[1]] = hid_sum
 
-    def zsend(kind, src, landing, height, lanes=slice(None)):
-        copies = []
-        for dz in range(1, 4):
-            z2 = (z + dz) % 4
-            cp = remote(
-                src.at[pl.ds(pl.multiple_of(z2 * height, 16), height), lanes],
-                landing.at[dz - 1, :, lanes],
-                dz_s.at[kind, dz - 1],
-                dz_r.at[kind, dz - 1],
-                ident(r, 2 * z2 + c),
-            )
-            cp.start()
-            copies.append(cp)
-        return copies
+    def line_rows(src, z2, lanes):
+        return src.at[pl.ds(pl.multiple_of(z2 * 2 * part, 16), 2 * part), lanes]
+
+    def line_term(kind, src, landing, lanes, q):
+        stop = q == 0
+        index = 3 if stop else q - 1
+        return remote(
+            line_rows(src, across[3] if stop else across[q], lanes),
+            landing.at[index, :, lanes],
+            dz_s.at[kind, index],
+            dz_r.at[kind, index],
+            ident(r, 2 * across[1 if stop else q] + c),
+        )
+
+    def line_out(*what):
+        line_term(*what, 1).start()
+
+        @pl.when(outer)
+        def _():
+            line_term(*what, 0).start()
+            line_term(*what, 2).start()
+
+        @pl.when(inner)
+        def _():
+            line_term(*what, 3).start()
+
+    def line_join(kind, src, landing, lanes):
+        @pl.when(inner)
+        def _():
+            line_term(kind, src, landing, lanes, 0).wait_recv()
+            term = line_rows(src, across[2], lanes)
+            term[...] = (term[...].astype(f32) + landing[3, :, lanes].astype(f32)).astype(bf16)
+            line_term(kind, src, landing, lanes, 2).start()
+
+    def line_sum(kind, src, landing, lanes):
+        mine_now = line_rows(src, z, lanes)
+        total = mine_now[...].astype(f32)
+        for q in (1, 2):
+            line_term(kind, src, landing, lanes, q).wait_recv()
+            total += landing[q - 1, :, lanes].astype(f32)
+
+        @pl.when(outer)
+        def _():
+            mine_now[...] = total.astype(bf16)
+
+        @pl.when(inner)
+        def _():
+            line_term(kind, src, landing, lanes, 3).wait_recv()
+            mine_now[...] = (total + landing[2, :, lanes].astype(f32)).astype(bf16)
+
+    def line_drain(*what):
+        line_term(*what, 1).wait_send()
+        line_term(*what, 2).wait_send()
+
+        @pl.when(outer)
+        def _():
+            line_term(*what, 0).wait_send()
+
+        @pl.when(inner)
+        def _():
+            line_term(*what, 3).wait_send()
+
+    every = slice(None)
+    exp_tail = (0, d_exp, z_exp, tail)
+    exp_front = (1, d_exp, z_exp, head)
+    proj_sum = (2, d_proj, z_proj, every)
+
+    def exp_sides(step):
+        step(*exp_tail)
+
+        @pl.when(c == 0)
+        def _():
+            step(*exp_front)
 
     def wide_grad(k, carry):
         at = pl.ds(pl.multiple_of(k * third, 128), third)
@@ -1100,12 +1181,39 @@
         return carry
 
     lax.fori_loop(0, 3, wide_grad, 0)
-    sent += zsend(0, d_exp, z_exp, 2 * part, tail)
-
-    @pl.when(c == 0)
-    def _():
-        zsend(1, d_exp, z_exp, 2 * part, head)
-
+    exp_sides(line_out)
+
+    def red_grad(k, carry):
+        at = pl.ds(pl.multiple_of(k * third, 128), third)
+        d_red[:, at] = t_dot(proj_wide[:total_rows, hid_lanes], g_mlp[:, at]).astype(bf16)
+        return carry
+
+    lax.fori_loop(0, 3, red_grad, 0)
+
+    def red_tile(i):
+        p = 4 * c + i
+        at = r + 4 * p
+        return (p >= 5 * c), at, (2 * at) // (2 * blocks)
+
+    def apart(goal):
+        return 2 * ((z // 2 + goal // 2) % 2) + (z + goal) % 2
+
+    def red_up(i, index, z2):
+        return remote(
+            d_red.at[pl.ds(i * LANES, LANES)],
+            z_red.at[index, i % 3],
+            zr_s.at[i],
+            zr_r.at[index, i % 3],
+            ident(r, 2 * z2 + c),
+        )
+
+    for i in range(slots_of):
+        real, at, goal = red_tile(i)
+        q = apart(goal)
+        stop = outer & (q == 3)
+        pl.when(real & stop)(red_up(i, 3, across[1]).start)
+        direct = (q != 0) & jnp.logical_not(stop) & jnp.logical_not(inner & (q == 2))
+        pl.when(real & direct)(red_up(i, (q + 3) % 4, goal).start)
 
     grad_two = reduce_end(1, part_b, rows_b)
 
@@ -1124,52 +1232,29 @@
     grad_at = (gate_attn * g_mixed[...]).astype(bf16)
     own(g_attn)[...] = grad_at
     slab[7:8, :] = jnp.sum(grad_at.astype(f32), axis=0, keepdims=True)
-    sent += gather_start(3, g_attn)
-
-    def red_grad(k, carry):
-        at = pl.ds(pl.multiple_of(k * third, 128), third)
-        d_red[:, at] = t_dot(act[...], g_mlp[:, at]).astype(bf16)
-        return carry
-
-    lax.fori_loop(0, 3, red_grad, 0)
-
-    def red_tile(i):
-        p = 4 * c + i
-        at = r + 4 * p
-        return (p >= 5 * c), at, (2 * at) // (2 * blocks)
-
-    def red_up(i, src_z):
-        there = (src_z - red_tile(i)[2] + 4) % 4 - 1
-        return remote(
-            d_red.at[pl.ds(i * LANES, LANES)],
-            z_red.at[there, i % 3],
-            zr_s.at[i],
-            zr_r.at[there, i % 3],
-            ident(r, 2 * red_tile(i)[2] + c),
-        )
-
-    for i in range(slots_of):
-        real, at, goal = red_tile(i)
-
-        @pl.when(real & (goal != z))
-        def _():
-            red_up(i, z).start()
+    gather_start(3, g_attn)
 
     reduce_drain(1, part_b, sib_b, rows_b)
     def feed_out(k, carry):
-        cc, first, here = chunk_of(k)
-        values = dot(act[here, :], red_all[...])
-        reduce_chunk(3, k, cc, values, part_b, sib_a, rows_b, hold=True)
+        first, pair, here = chunk_of(k)
+        values = dot(proj_wide[here, hid_lanes], red_all[...])
+        reduce_chunk(3, k, values, part_b, sib_a, rows_b, hold=True)
         return carry
 
     lax.fori_loop(0, 4, feed_out, 0)
 
-    sent += gather_end(3, g_attn)
-    for dx, dy in SAME_CORE:
+    gather_near(3, g_attn)
+    exp_sides(line_join)
+    for dx, dy in SAME_CORE[:2]:
         reduce_send(3, part_b, rows_b, plane(dx, dy))
-
     def attend_back(k, carry):
-        cc, first, here = chunk_of(k)
+        first, pair, here = chunk_of(k)
+
+        @pl.when(k == 2)
+        def _():
+            gather_far(3, g_attn)
+            reduce_send(3, part_b, rows_b, plane(1, 1))
+
         g_att = dot_t(g_attn[here, :], out_w[...]).astype(bf16)
         for i in range(2):
             u = first + i
@@ -1193,25 +1278,33 @@
             wide = jnp.concatenate([g_q * scale, g_k * scale, g_v], axis=1).astype(bf16)
             d_qkv[at, :] = dot_t(wide, spread[...]).astype(bf16)
         values = dot_t(d_qkv[here, :], proj_all[...])
-        reduce_chunk(2, k, cc, values, part_a, sib_b, rows_a)
+        reduce_chunk(2, k, values, part_a, sib_b, rows_a)
         return carry
 
     lax.fori_loop(0, 4, attend_back, 0)
-
-    own_z = pl.ds(pl.multiple_of(z * 2 * part, 16), 2 * part)
-
-    def line_sum(kind, src, landing, lanes):
-        total = src[own_z, lanes].astype(f32)
-        for dz in range(1, 4):
-            remote(
-                src.at[own_z, lanes],
-                landing.at[dz - 1, :, lanes],
-                dz_s.at[kind, dz - 1],
-                dz_r.at[kind, dz - 1],
-                ident(r, 2 * ((z + dz) % 4) + c),
-            ).wait_recv()
-            total += landing[dz - 1, :, lanes].astype(f32)
-        src[own_z, lanes] = total.astype(bf16)
+    def proj_grad(k, carry):
+        at = pl.ds(pl.multiple_of(k * third, 128), third)
+        d_proj[at, :] = t_dot(x_one[:, at], d_qkv[...]).astype(bf16)
+        return carry
+
+    lax.fori_loop(0, 3, proj_grad, 0)
+    line_out(*proj_sum)
+    d_out[...] = t_dot(attended[...], g_attn[...]).astype(bf16)
+
+    def out_up(index, z2):
+        return remote(
+            d_out.at[pl.ds(0, part)],
+            z_out.at[index],
+            ow_s.at[8],
+            ow_r.at[1 + index],
+            ident(r, 2 * z2 + c),
+        )
+
+    q_out = apart(r)
+    pl.when(outer & (q_out == 3))(out_up(3, across[1]).start)
+    pl.when((q_out == 1) | (outer & (q_out == 2)) | (inner & (q_out == 3)))(
+        out_up((q_out + 3) % 4, r).start
+    )
 
     def exp_up(k, i, r2, c2):
         at = red_tile(i)[1]
@@ -1235,11 +1328,7 @@
             et_l.at[i],
         )
 
-    line_sum(0, d_exp, z_exp, tail)
-
-    @pl.when(c == 0)
-    def _():
-        line_sum(1, d_exp, z_exp, head)
+    exp_sides(line_sum)
 
     for i in range(slots_of):
 
@@ -1281,55 +1370,57 @@
                 local_part(red_here(i, h))
 
 
-    def proj_grad(k, carry):
-        at = pl.ds(pl.multiple_of(k * third, 128), third)
-        d_proj[at, :] = t_dot(x_one[:, at], d_qkv[...]).astype(bf16)
-        return carry
-
-    lax.fori_loop(0, 3, proj_grad, 0)
-    sent += zsend(2, d_proj, z_proj, 2 * part)
-    d_out[...] = t_dot(attended[...], g_attn[...]).astype(bf16)
-
-    @pl.when(z != r)
-    def _():
-        slot_z = (r - z + 4) % 4 - 1
-        remote(
-            d_out.at[pl.ds(0, part)],
-            z_out.at[slot_z],
-            ow_s.at[8],
-            ow_r.at[1 + slot_z],
-            ident(r, 2 * r + c),
-        ).start()
-
     slab[9:10, : d_qkv.shape[1]] = jnp.sum(d_qkv[...].astype(f32), axis=0, keepdims=True)
 
 
     for i in range(slots_of):
         real, at, goal = red_tile(i)
 
+        @pl.when(real & inner & (apart(goal) == 2))
+        def _():
+            red_up(i, 3, z).wait_recv()
+            rows_i = slice(i * LANES, (i + 1) * LANES)
+            d_red[rows_i, :] = (
+                d_red[rows_i, :].astype(f32) + z_red[3, i % 3].astype(f32)
+            ).astype(bf16)
+            red_up(i, 1, goal).start()
+
+
+    for i in range(slots_of):
+        real, at, goal = red_tile(i)
+
         @pl.when(real & (goal == z))
         def _():
             rows_i = slice(i * LANES, (i + 1) * LANES)
             total = d_red[rows_i, :].astype(f32)
-            for there in range(3):
-                remote(
-                    d_red.at[pl.ds(i * LANES, LANES)],
-                    z_red.at[there, i % 3],
-                    zr_s.at[i],
-                    zr_r.at[there, i % 3],
-                    ident(r, f),
-                ).wait_recv()
+            for there in range(2):
+                red_up(i, there, z).wait_recv()
                 total += z_red[there, i % 3].astype(f32)
-            d_red[rows_i, :] = total.astype(bf16)
+
+            @pl.when(outer)
+            def _():
+                d_red[rows_i, :] = total.astype(bf16)
+
+            @pl.when(inner)
+            def _():
+                red_up(i, 2, z).wait_recv()
+                d_red[rows_i, :] = (total + z_red[2, i % 3].astype(f32)).astype(bf16)
+
             red_each(i, lambda cp: cp.start(), lambda cp: cp.start())
 
     def place(values, base):
-        live_hot = (one_hot() * live_col[...]).astype(bf16)
-        placed = t_dot(live_hot, values.astype(bf16))
-        hit = t_dot(live_hot, jnp.ones((rows, 128), bf16))[:, 0:1]
+        live_hot = one_hot() * live_row[0:1, :]
+        placed = dot(live_hot.astype(bf16), values.astype(bf16))
+        hit = jnp.sum(live_hot, axis=1, keepdims=True)
         return jnp.where(hit > 0.5, placed.astype(bf16), base)
 
     branch = reduce_end(3, part_b, rows_b) + red_b
+    @pl.when(inner & (q_out == 2))
+    def _():
+        out_up(3, z).wait_recv()
+        d_out[:part, :] = (d_out[:part, :].astype(f32) + z_out[3].astype(f32)).astype(bf16)
+        out_up(1, r).start()
+
     slab[5:6, :] = jnp.sum(g_rows[...] * branch, axis=0, keepdims=True)
     o_block[...] = place(mixed[...] + gate_mlp * branch, latents[...])
 
@@ -1351,18 +1442,26 @@
 
     sent += line_send(5, small_s, small_r, slab_src, slab_dst)
 
+    line_join(*proj_sum)
     @pl.when(z == r)
     def _():
         total = d_out[:part, :].astype(f32)
-        for k in range(3):
-            remote(
-                d_out.at[pl.ds(0, part)], z_out.at[k], ow_s.at[3], ow_r.at[1 + k], ident(r, f)
-            ).wait_recv()
+        for k in range(2):
+            out_up(k, z).wait_recv()
             total += z_out[k].astype(f32)
-        d_out[:part, :] = total.astype(bf16)
+
+        @pl.when(outer)
+        def _():
+            d_out[:part, :] = total.astype(bf16)
+
+        @pl.when(inner)
+        def _():
+            out_up(2, z).wait_recv()
+            d_out[:part, :] = (total + z_out[2].astype(f32)).astype(bf16)
+
         for k, (dx, dy) in enumerate(SAME_CORE):
             remote(
-                d_out.at[pl.ds(0, part)], o_out, ow_s.at[4 + k], ow_r.at[4], ident(plane(dx, dy), f)
+                d_out.at[pl.ds(0, part)], o_out, ow_s.at[4 + k], ow_r.at[5], ident(plane(dx, dy), f)
             ).start()
         cp = pltpu.make_async_copy(d_out.at[pl.ds(0, part)], o_out, local_sem.at[5])
         cp.start()
@@ -1397,8 +1496,7 @@
     sent += line_send(7, small_s, small_r, gc_src, gc_dst)
     o_gcond[f] = gcond[f]
 
-    every = slice(None)
-    line_sum(2, d_proj, z_proj, every)
+    line_sum(*proj_sum)
 
     def proj_up(k, r2, c2):
         return remote(
@@ -1437,24 +1535,23 @@
         remote(
             slabs.at[theirs], o_slabs.at[r2, theirs], small_s.at[6, 3], small_r.at[6, 4 + r2], sibling
         ).wait_recv()
+    o_proj[...] = jnp.zeros(o_proj.shape, bf16)
+
+    def unpack(r2, c2):
+        t = 2 * r2 + c2
+        wide = dot(proj_land[4 * c2 + r2], spread[...])
+        for q in range(3):
+            piece = pltpu.roll(wide[:, q * LANES_Q : (q + 1) * LANES_Q], t * (part - LANES), 1)
+            here = pl.ds(pl.multiple_of(q * width + t * LANES, LANES), LANES_Q)
+            o_proj[:, here] = (o_proj[:, here].astype(f32) + piece).astype(bf16)
+
+    unpack(r, c)
     for r2, c2 in board:
         u = 4 * c2 + r2
         remote(
             proj_land.at[u], proj_land.at[u], dp_s.at[0], dp_r.at[u], ident(r2, 2 * z + c2)
         ).wait_recv()
-
-    o_proj[...] = jnp.zeros(o_proj.shape, bf16)
-    for u in range(8):
-        t = 2 * (u % 4) + u // 4
-        wide = dot(proj_land[u], spread[...])
-        for q in range(3):
-            piece = wide[:, q * LANES_Q : (q + 1) * LANES_Q]
-            if t:
-                piece = pltpu.roll(piece, t * (part - LANES), 1)
-            first = q * width + t * LANES
-            o_proj[:, first : first + LANES_Q] = (
-                o_proj[:, first : first + LANES_Q].astype(f32) + piece
-            ).astype(bf16)
+        unpack(r2, c2)
 
     def tile_arrival(at, carry):
         p = at // 4
@@ -1505,24 +1602,15 @@
 
         @pl.when(real & (goal != z))
         def _():
-            red_up(i, z).wait_send()
+            red_up(i, 0, z).wait_send()
 
     for k, (r2, c2) in enumerate(board):
         proj_up(k, r2, c2).wait_send()
     red_drain()
     exp_drain()
 
-    @pl.when(c == 0)
-    def _():
-        for dz in range(1, 4):
-            remote(
-                d_exp.at[own_z, head],
-                z_exp.at[dz - 1, :, head],
-                dz_s.at[1, dz - 1],
-                dz_r.at[1, dz - 1],
-                ident(r, f),
-            ).wait_send()
-
+    exp_sides(line_drain)
+    line_drain(*proj_sum)
     for z2 in range(4):
         pl.when(out_goes(z2))(out_copy(z2).wait_send)
     pl.when(inner & (across[2] == r))(out_onward().wait_send)
@@ -1530,18 +1618,18 @@
     @pl.when(z == r)
     def _():
         for k in range(3):
-            remote(out_shard, o_out, ow_s.at[4 + k], ow_r.at[4], ident(r, f)).wait_send()
+            remote(out_shard, o_out, ow_s.at[4 + k], ow_r.at[5], ident(r, f)).wait_send()
 
     @pl.when(z != r)
     def _():
-        remote(out_shard, o_out, ow_s.at[3], ow_r.at[4], ident(r, f)).wait_recv()
-        remote(
-            d_out.at[pl.ds(0, part)], z_out.at[0], ow_s.at[8], ow_r.at[1], ident(r, f)
-        ).wait_send()
+        remote(out_shard, o_out, ow_s.at[3], ow_r.at[5], ident(r, f)).wait_recv()
+        out_up(0, r).wait_send()
 
     relay_drain(*proj_main)
     reduce_drain(2, part_a, sib_b, rows_a)
     reduce_drain(3, part_b, sib_a, rows_b)
+    for kind, buf in enumerate((x_one, g_mlp, x_two, g_attn)):
+        gather_drain(kind, buf)
     drain(sent)
     drain(live_sent)
     drain(cond_sent)
@@ -1606,13 +1694,13 @@
         ],
         axis=1,
     ).astype(bf16)
-    extra = jnp.pad(extra, ((0, 0), (0, 12), (0, 0)))
+    extra = jnp.pad(extra.reshape(2, 12, width // 3), ((0, 0), (0, 4), (0, 0)))
     total = 8 * rows
     vmem = pltpu.VMEM
     dma = pltpu.SemaphoreType.DMA
     scratch = [
         vmem((8, 16, part), bf16),
-        vmem((8, 16, width), bf16),
+        vmem((8, 16, width // 3), bf16),
         vmem((8, 8, rows), f32),
         vmem((8, 8, width), f32),
         vmem((8, 8, width), f32),
@@ -1631,7 +1719,6 @@
         vmem((total, 3 * LANES_Q), bf16),
         vmem((16, rows, rows), f32),
         vmem((total, LANES_Q), bf16),
-        vmem((total, wide), bf16),
         vmem((total, wide), bf16),
         vmem((total, 3 * part), bf16),
         vmem((total, width), bf16),
@@ -1655,33 +1742,33 @@
         vmem((wide, width), bf16),
         vmem((width, 3 * part), bf16),
         vmem((LANES_Q, width), bf16),
-        vmem((3, 2 * part, wide), bf16),
-        vmem((3, 3, LANES, width), bf16),
-        vmem((3, 2 * part, 3 * part), bf16),
-        vmem((3, part, width), bf16),
+        vmem((4, 2 * part, wide), bf16),
+        vmem((4, 3, LANES, width), bf16),
+        vmem((4, 2 * part, 3 * part), bf16),
+        vmem((4, part, width), bf16),
         vmem((8, part, 3 * part), bf16),
         dma((8,)),
         dma((8, 7)),
         dma((8, 8)),
         dma((3, 7)),
         dma((3, 8)),
-        dma((4, 7)),
         dma((4, 8)),
+        dma((4, 9)),
         dma((4, 2)),
         dma((4, 2)),
         dma((4, 4)),
         dma((4, 4)),
-        dma((3, 3)),
-        dma((3, 3)),
+        dma((3, 4)),
+        dma((3, 4)),
         dma((7,)),
         dma((8,)),
         dma((9,)),
-        dma((5,)),
+        dma((6,)),
         dma((hid // HALF // 4, 4)),
         dma((2 * slots_of,)),
         dma((2 * slots_of,)),
         dma((slots_of,)),
-        dma((3, 3)),
+        dma((4, 3)),
         dma((2, slots_of)),
         dma((7, slots_of)),
         dma((hid // LANES,)),
@@ -1707,7 +1794,7 @@
             jax.ShapeDtypeStruct((part, 3 * width), bf16),
             jax.ShapeDtypeStruct((part, width), bf16),
         ),
-        in_specs=[in_vmem] * 10 + [anywhere] * 2 + [in_vmem],
+        in_specs=[in_vmem] * 9 + [anywhere] * 2 + [in_vmem],
         out_specs=(
             in_vmem,
             in_vmem,
@@ -1726,8 +1813,7 @@
     )(
         latents[0],
         cotangent[0],
-        keep_slots.reshape(rows, 1),
-        live.reshape(rows, 1),
+        keep_slots,
         jnp.broadcast_to(live[None], (8, rows)),
         cond_pack,
         mod_bias,
@@ -1747,11 +1833,12 @@
     grad_mod = slabs[:, :6].reshape(32, 6 * width)
     cond_cols = conds[:, :, 0].reshape(4, 4, 2, part).transpose(0, 2, 1, 3).reshape(32, part)
     sum_mod_w = jnp.einsum("bd,be->de", cond_cols, grad_mod, preferred_element_type=f32)
-    sums = jnp.sum(slabs[:, :8].astype(f32), axis=0)
+    tails = jnp.sum(slabs.reshape(4, 2, 4, 16, width)[:, :, :, :10].astype(f32), axis=2)
+    sums = jnp.sum(tails[:, :, :8], axis=(0, 1))
+    tails = tails[:, :, 8:]
     sum_mod_b = shard(sums[:6].reshape(-1), 0, modulation_bias.shape[0])
     sum_red_b = shard(sums[6], 0, part)
     sum_out_b = shard(sums[7], 0, part)
-    tails = jnp.sum(slabs[:, 8:10].astype(f32).reshape(4, 2, 4, 2, width), axis=2)
     exp_sums = tails[:, :, 0, :wide].reshape(4, 2, slots_of, LANES)
     exp_sums = jnp.concatenate([exp_sums[:, 0], exp_sums[:, 1, 1:]], axis=1)
     sum_exp_b = shard(exp_sums.transpose(1, 0, 2).reshape(-1), 0, expand_bias.shape[0])

time: 291 us -> 271 us (0.931)
  Pallas kernels: 258 us -> 242 us
    pallas_call x1, Pallas kernels: 258 us -> 242 us  [fused_local(): pl.pallas_call(fused_kernel, out_shape=(jax.ShapeDtypeStruct((slot_count,...]
where the time goes in v4:
time: 271 us; the launch traced here: 268 us
  Pallas kernels  242 us (89%)
  other arithmetic  13.3 us (5%)
  local copies, waits for them, and re-layouts  9.04 us (3%)
    pallas_call x1, Pallas kernels, fused_local(): pl.pallas_call(fused_kernel, out_shape=(jax.ShapeDtypeStruct((slot_count,...  242 us

profile of v4, /device:TPU:25, one launch (start us, length us, event | category | flops | bytes accessed | tf_op | source)
XLA Modules:
  0.0 268.1 jit_solution(16394224810596261364)
XLA Ops:
  1.3 0.6 broadcast_in_dim.21.live_row
  1.9 0.7 convert_dynamic-update-slice_fusion.3
  2.7 0.8 convert_dynamic-update-slice_fusion.4
  3.5 0.7 convert_reduce_fusion.1
  4.2 0.1 reshape.96
  4.3 0.8 convert_dynamic-update-slice_fusion.2
  5.1 0.1 reshape.88
  5.2 0.8 convert_dynamic-update-slice_fusion
  6.3 0.6 pad.38.extra
  6.9 0.8 convert_dynamic-update-slice_fusion.1
  7.7 0.6 pad.33.mod_bias
  8.3 0.6 pad.32.cond_pack
  8.9 0.0 copy-start.7
  8.9 241.5 %shard_map.246 = (bf16[256,1152]{1,0:T(8,128)(2,1)}, bf16[256,1152]{1,0:T(8,128)(2,1)}, bf16[4,8,16,1152]{3,2,1,0:T(8,128)(2,1)}, bf16[4,8,16,144]{3,2,1,0:T(8,1...) custom-call(bf16[256,1152]{1,0:T(8,128)(2,1)} %bitcast.48, ...), custom_call_target="tpu_custom_call" | custom-call | tf_op jit(solution)/shard_map/pallas_call | solution.py:1784
  250.5 0.0 copy-start
  250.5 1.0 slice_reduce_fusion.5
  251.4 0.1 reshape_squeeze.18
  251.5 0.0 copy-done.7
  251.5 0.6 fusion.3
  252.2 0.9 slice.61
  253.1 1.5 convert_reduce_fusion
  254.7 0.0 copy-start.6
  254.7 0.1 slice_reduce_fusion.2
  254.8 0.1 reshape_squeeze.20
  254.9 0.1 reshape_squeeze.22
  255.0 0.0 copy-start.3
  255.0 0.1 reshape_squeeze.21
  255.1 0.7 fusion.7
  255.8 0.1 slice_reduce_fusion.1
  255.9 0.6 constant_dynamic-slice_fusion
  256.6 0.7 dynamic_slice.32
  257.3 0.7 dynamic_slice.28
  258.0 0.0 copy-done
  258.1 0.0 copy-done.6
  258.1 0.0 copy-start.2
  258.1 0.9 convert_element_type.73
  259.0 0.0 copy-done.3
  259.0 1.4 convert_element_type.72
  260.4 0.0 copy-done.2
  260.4 0.0 copy-start.1
  260.4 1.8 convert_element_type.74
  262.2 0.0 copy-done.1
  262.2 1.7 convert_element_type.75
  263.8 0.0 copy-start.5
  263.9 0.0 copy-start.4
  263.9 2.6 fusion.9
  266.5 0.0 copy-done.5
  266.5 0.8 copy.61
  267.3 0.0 copy-done.4
  267.3 0.8 copy.62
  (40 shorter events, 0.5 us)
Async XLA Ops:
  8.9 242.6 %copy-start.7 = (bf16[1,1152]{1,0:T(2,128)(2,1)S(1)}, bf16[1,1152]{1,0:T(2,128)(2,1)}, u32[]{:S(2)}) copy-start(bf16[1,1152]{1,0:T(2,128)(2,1)} %param.16) | copy-start | bytes 6916
  250.5 7.5 %copy-start = (bf16[4,8,16,1152]{3,2,1,0:T(8,128)(2,1)S(1)}, bf16[4,8,16,1152]{3,2,1,0:T(8,128)(2,1)}, u32[]{:S(2)}) copy-start(bf16[4,8,16,1152]{3,2,1,0:T(8,128)(2,1)} %get-tuple-element.26) | copy-start | bytes 3538948
  254.7 3.4 %copy-start.6 = (bf16[144,1152]{1,0:T(8,128)(2,1)S(1)}, bf16[144,1152]{1,0:T(8,128)(2,1)}, u32[]{:S(2)}) copy-start(bf16[144,1152]{1,0:T(8,128)(2,1)} %get-tuple-element.28) | copy-start | bytes 995332
  255.0 4.0 %copy-start.3 = (bf16[144,3456]{1,0:T(8,128)(2,1)S(1)}, bf16[144,3456]{1,0:T(8,128)(2,1)}, u32[]{:S(2)}) copy-start(bf16[144,3456]{1,0:T(8,128)(2,1)} %get-tuple-element.27) | copy-start | bytes 2985988
  258.1 2.3 copy-start.2
  260.4 1.8 copy-start.1
  263.8 2.7 copy-start.5
  263.9 3.5 %copy-start.4 = (bf16[256,1152]{1,0:T(8,128)(2,1)S(1)}, bf16[256,1152]{1,0:T(8,128)(2,1)}, u32[]{:S(2)}) copy-start(bf16[256,1152]{1,0:T(8,128)(2,1)} %get-tuple-element.23) | copy-start | bytes 1769476

commit v5 on v4

--- a/solution.py
+++ b/solution.py
@@ -963,10 +963,15 @@
     def _():
         out_w[:part, :] = out_shard[...]
 
-    relay_pass(*proj_main)
     for z2 in range(4):
         pl.when(out_goes(z2))(out_copy(z2).start)
+    relay_pass(*proj_main)
     relay_wait(*proj_main)
+    @pl.when(z != r)
+    def _():
+        out_copy(z).wait_recv()
+
+    pl.when(inner & (across[2] == r))(out_onward().start)
     for cp in packs:
         cp.wait()
     own_exp = pltpu.make_async_copy(exp_pack.at[c, :, tail], exp_dst(f), local_sem.at[3])
@@ -1016,11 +1021,6 @@
     ]
     scale = HEAD_DIM ** (-0.5)
 
-    @pl.when(z != r)
-    def _():
-        out_copy(z).wait_recv()
-
-    pl.when(inner & (across[2] == r))(out_onward().start)
     red_send()
 
     def attend(k, carry):
@@ -1422,7 +1422,6 @@
         out_up(1, r).start()
 
     slab[5:6, :] = jnp.sum(g_rows[...] * branch, axis=0, keepdims=True)
-    o_block[...] = place(mixed[...] + gate_mlp * branch, latents[...])
 
     def slab_at(f2):
         return 4 * (f2 % 2) + f2 // 2
@@ -1431,7 +1430,6 @@
     g_shift, g_scale, through = back_norm(grad_one, scale_attn, norm_one[...], rstd_one[...])
     slab[0:1, :] = g_shift
     slab[1:2, :] = g_scale
-    o_latents[...] = place(g_mixed[...] + through, cotangent[...])
     slabs[slab_at(f)] = slab[...].astype(bf16)
 
     def slab_src(f2, c2):
@@ -1441,6 +1439,8 @@
         return slabs.at[slab_at(f2)]
 
     sent += line_send(5, small_s, small_r, slab_src, slab_dst)
+    o_latents[...] = place(g_mixed[...] + through, cotangent[...])
+    o_block[...] = place(mixed[...] + gate_mlp * branch, latents[...])
 
     line_join(*proj_sum)
     @pl.when(z == r)

time: 271 us -> 270 us (level)
  no operation moved by 1% of the time
where the time goes in v5:
time: 270 us; the launch traced here: 268 us
  Pallas kernels  241 us (89%)
  other arithmetic  13.3 us (5%)
  local copies, waits for them, and re-layouts  9.04 us (3%)
    pallas_call x1, Pallas kernels, fused_local(): pl.pallas_call(fused_kernel, out_shape=(jax.ShapeDtypeStruct((slot_count,...  241 us

profile of v5, /device:TPU:25, one launch (start us, length us, event | category | flops | bytes accessed | tf_op | source)
XLA Modules:
  0.0 267.9 jit_solution(4592978715617420149)
XLA Ops:
  1.3 0.6 broadcast_in_dim.21.live_row
  1.9 0.7 convert_dynamic-update-slice_fusion.3
  2.7 0.8 convert_dynamic-update-slice_fusion.4
  3.5 0.7 convert_reduce_fusion.1
  4.2 0.1 reshape.96
  4.3 0.8 convert_dynamic-update-slice_fusion.2
  5.1 0.1 reshape.88
  5.2 0.8 convert_dynamic-update-slice_fusion
  6.3 0.6 pad.38.extra
  6.9 0.8 convert_dynamic-update-slice_fusion.1
  7.7 0.6 pad.33.mod_bias
  8.3 0.6 pad.32.cond_pack
  8.9 0.0 copy-start.7
  8.9 241.3 %shard_map.246 = (bf16[256,1152]{1,0:T(8,128)(2,1)}, bf16[256,1152]{1,0:T(8,128)(2,1)}, bf16[4,8,16,1152]{3,2,1,0:T(8,128)(2,1)}, bf16[4,8,16,144]{3,2,1,0:T(8,1...) custom-call(bf16[256,1152]{1,0:T(8,128)(2,1)} %bitcast.48, ...), custom_call_target="tpu_custom_call" | custom-call | tf_op jit(solution)/shard_map/pallas_call | solution.py:1784
  250.3 0.0 copy-start
  250.3 1.0 slice_reduce_fusion.5
  251.2 0.1 reshape_squeeze.18
  251.3 0.0 copy-done.7
  251.3 0.6 fusion.3
  252.0 0.9 slice.61
  252.9 1.5 convert_reduce_fusion
  254.5 0.0 copy-start.6
  254.5 0.1 slice_reduce_fusion.2
  254.5 0.1 reshape_squeeze.20
  254.7 0.1 reshape_squeeze.22
  254.8 0.0 copy-start.3
  254.8 0.1 reshape_squeeze.21
  254.9 0.7 fusion.7
  255.6 0.1 slice_reduce_fusion.1
  255.7 0.6 constant_dynamic-slice_fusion
  256.4 0.7 dynamic_slice.32
  257.1 0.7 dynamic_slice.28
  257.7 0.0 copy-done
  257.9 0.0 copy-done.6
  257.9 0.0 copy-start.2
  257.9 0.9 convert_element_type.73
  258.8 0.0 copy-done.3
  258.8 1.4 convert_element_type.72
  260.2 0.0 copy-done.2
  260.2 0.0 copy-start.1
  260.2 1.8 convert_element_type.74
  262.0 0.0 copy-done.1
  262.0 1.7 convert_element_type.75
  263.6 0.0 copy-start.5
  263.6 0.0 copy-start.4
  263.6 2.6 fusion.9
  266.3 0.0 copy-done.5
  266.3 0.8 copy.61
  267.1 0.0 copy-done.4
  267.1 0.8 copy.62
  (40 shorter events, 0.5 us)
Async XLA Ops:
  8.9 242.4 %copy-start.7 = (bf16[1,1152]{1,0:T(2,128)(2,1)S(1)}, bf16[1,1152]{1,0:T(2,128)(2,1)}, u32[]{:S(2)}) copy-start(bf16[1,1152]{1,0:T(2,128)(2,1)} %param.16) | copy-start | bytes 6916
  250.3 7.5 %copy-start = (bf16[4,8,16,1152]{3,2,1,0:T(8,128)(2,1)S(1)}, bf16[4,8,16,1152]{3,2,1,0:T(8,128)(2,1)}, u32[]{:S(2)}) copy-start(bf16[4,8,16,1152]{3,2,1,0:T(8,128)(2,1)} %get-tuple-element.26) | copy-start | bytes 3538948
  254.5 3.4 %copy-start.6 = (bf16[144,1152]{1,0:T(8,128)(2,1)S(1)}, bf16[144,1152]{1,0:T(8,128)(2,1)}, u32[]{:S(2)}) copy-start(bf16[144,1152]{1,0:T(8,128)(2,1)} %get-tuple-element.28) | copy-start | bytes 995332
  254.8 4.0 %copy-start.3 = (bf16[144,3456]{1,0:T(8,128)(2,1)S(1)}, bf16[144,3456]{1,0:T(8,128)(2,1)}, u32[]{:S(2)}) copy-start(bf16[144,3456]{1,0:T(8,128)(2,1)} %get-tuple-element.27) | copy-start | bytes 2985988
  257.9 2.3 copy-start.2
  260.2 1.8 copy-start.1
  263.6 2.7 copy-start.5
  263.6 3.5 %copy-start.4 = (bf16[256,1152]{1,0:T(8,128)(2,1)S(1)}, bf16[256,1152]{1,0:T(8,128)(2,1)}, u32[]{:S(2)}) copy-start(bf16[256,1152]{1,0:T(8,128)(2,1)} %get-tuple-element.23) | copy-start | bytes 1769476
